TPU v7x, 32 devices: a whole 2x2x4 slice. The times are simulated.
32 devices in a mesh: dom: 4 (over y, x), head: 8 (over z, core).
Axes of the slice: x: 2, y: 2, z: 4, core: 2. Of those that a mesh axis runs over, the one named last changes fastest.
Arguments:
- node_queries: bfloat16 [8192, 1024], P(('dom', 'head')), may hold values from -20 to 20
- node_keys: bfloat16 [8192, 1024], P(('dom', 'head')), may hold values from -20 to 20
- node_values: bfloat16 [8192, 1024], P(('dom', 'head')), may hold values from -6 to 6
- out_grad: bfloat16 [8192, 1024], P(('dom', 'head')), may hold values from -6 to 6
- degrees: int32 [8192], P('dom'), may hold values from 8 to 4096
- neighbor_blocks: int32 [64, 12], P('dom'), may hold values from 0 to 31, as said below
- send_slots: int32 [4, 4, 4], replicated, may hold values from -1 to 15, as said below
Outputs:
- grad_queries: bfloat16 [8192, 1024], P(('dom', 'head'))
- grad_keys: bfloat16 [8192, 1024], P(('dom', 'head'))
- grad_values: bfloat16 [8192, 1024], P(('dom', 'head'))
Inputs may be any that keep to these rules, and one draw needn't show every extreme that they name: `neighbor_blocks`: an entry t below 16 names block t of the row's own partition; entry 16 + q * 4 + s names slot s of send_slots[q, p] for the row's partition p, and that slot is live. The 12 entries of a row are distinct, and every live slot listed for a partition is named by some row block of it. send_slots[q, p] holds distinct local block numbers of partition q, live slots first and -1 in empty ones; send_slots[p, p] is empty; for every destination p at least one source fills all 4 slots, every other source fills 1 to 4.
All inputs are finite; a program needn't handle non-finite values.
Results may differ from a plain program's by a relative error of at most 0.0068.
Values may be sent and summed in bfloat16 or wider, within the bound.
No kernel may reach another device: no remote copies, remote signals or barrier semaphores. Data moves between devices by JAX's collectives and lax.ppermute only.
A program may use at most 128 MiB of HBM per device.

v0:
```python
import math

import jax
import jax.numpy as jnp
from jax import lax
from jax.sharding import PartitionSpec as P

D = 1024
H = 16
NBR = 12
BS = 128


def borrow_table(keys_h, values_h, my_lists, block):
    rows, width = keys_h.shape
    nblk = rows // block
    kv_local = jnp.concatenate([keys_h, values_h], 1).reshape(nblk, block, 2 * width)
    outgoing = jnp.take(kv_local, jnp.maximum(my_lists, 0).reshape(-1), axis=0)
    borrowed = lax.all_to_all(outgoing, "dom", split_axis=0, concat_axis=0, tiled=True)
    return jnp.concatenate([kv_local, borrowed], 0)


def body(node_queries, node_keys, node_values, out_grad, degrees, neighbor_blocks, send_slots):
    head_dim = D // H
    block = BS
    heads_here = H // lax.axis_size("head")
    parts = lax.axis_size("dom")
    my_lists = lax.dynamic_index_in_dim(send_slots, lax.axis_index("dom"), 0, keepdims=False)
    queries, keys_h, values_h, grads_h = (
        lax.all_to_all(node_queries, "head", split_axis=1, concat_axis=0, tiled=True),
        lax.all_to_all(node_keys, "head", split_axis=1, concat_axis=0, tiled=True),
        lax.all_to_all(node_values, "head", split_axis=1, concat_axis=0, tiled=True),
        lax.all_to_all(out_grad, "head", split_axis=1, concat_axis=0, tiled=True),
    )
    table = borrow_table(keys_h, values_h, my_lists, block)
    rows, width = queries.shape
    nblk = rows // block
    scale_rows = jnp.log(degrees.astype(jnp.float32)) / math.log(64.0) / math.sqrt(head_dim)
    group_rows = 4 * block
    span = NBR * block

    def group(acc, index):
        start = index * group_rows
        queries_g = lax.dynamic_slice_in_dim(queries, start, group_rows, 0).reshape(4, block, width)
        grads_g = lax.dynamic_slice_in_dim(grads_h, start, group_rows, 0).reshape(4, block, width)
        scale = lax.dynamic_slice_in_dim(scale_rows, start, group_rows, 0).reshape(4, block, 1)
        picks = lax.dynamic_slice_in_dim(neighbor_blocks, index * 4, 4, 0).reshape(-1)
        gathered = jnp.take(table, picks, axis=0).reshape(4, span, 2 * width)
        grad_q_heads = []
        grad_k_heads = []
        grad_v_heads = []
        for head in range(heads_here):
            low = head * head_dim
            keys_n = gathered[:, :, low : low + head_dim]
            values_n = gathered[:, :, width + low : width + low + head_dim]
            query_one = queries_g[:, :, low : low + head_dim]
            grad_one = grads_g[:, :, low : low + head_dim]
            scores = (
                jnp.einsum("gid,gjd->gij", query_one, keys_n, preferred_element_type=jnp.float32)
                * scale
            )
            top = jnp.max(scores, axis=-1, keepdims=True)
            expo = jnp.exp(scores - top)
            probs = expo / jnp.sum(expo, axis=-1, keepdims=True)
            dprobs = jnp.einsum(
                "gid,gjd->gij", grad_one, values_n, preferred_element_type=jnp.float32
            )
            delta = jnp.sum(probs * dprobs, axis=-1, keepdims=True)
            dscores = (probs * (dprobs - delta) * scale).astype(jnp.bfloat16)
            probs_b = probs.astype(jnp.bfloat16)
            grad_q_heads.append(
                jnp.einsum("gij,gjd->gid", dscores, keys_n, preferred_element_type=jnp.float32)
            )
            grad_k_heads.append(
                jnp.einsum("gij,gid->gjd", dscores, query_one, preferred_element_type=jnp.float32)
            )
            grad_v_heads.append(
                jnp.einsum("gij,gid->gjd", probs_b, grad_one, preferred_element_type=jnp.float32)
            )
        grad_q = jnp.concatenate(grad_q_heads, -1)
        contrib = jnp.concatenate(grad_k_heads + grad_v_heads, -1).reshape(
            4 * NBR, block, 2 * width
        )
        acc = acc.at[picks].add(contrib)
        return (acc, grad_q.reshape(group_rows, width).astype(jnp.bfloat16))

    acc0 = jnp.zeros((table.shape[0], block, 2 * width), jnp.float32)
    acc, grad_rows = lax.scan(group, acc0, jnp.arange(nblk // 4, dtype=jnp.int32))
    grad_queries_h = grad_rows.reshape(rows, width)
    remote = acc[nblk:].astype(jnp.bfloat16)
    returned = lax.all_to_all(remote, "dom", split_axis=0, concat_axis=0, tiled=True)
    targets = jnp.maximum(my_lists, 0).reshape(-1)
    onehot = (jnp.arange(nblk, dtype=jnp.int32)[:, None] == targets[None, :]).astype(jnp.bfloat16)
    added = jnp.dot(
        onehot, returned.reshape(parts * my_lists.shape[1], -1), preferred_element_type=jnp.float32
    )
    total = (acc[:nblk] + added.reshape(nblk, block, 2 * width)).astype(jnp.bfloat16)
    grad_keys_h = total[:, :, :width].reshape(rows, width)
    grad_values_h = total[:, :, width:].reshape(rows, width)
    grad_queries, grad_keys, grad_values = (
        lax.all_to_all(grad_queries_h, "head", split_axis=0, concat_axis=1, tiled=True),
        lax.all_to_all(grad_keys_h, "head", split_axis=0, concat_axis=1, tiled=True),
        lax.all_to_all(grad_values_h, "head", split_axis=0, concat_axis=1, tiled=True),
    )
    return (grad_queries, grad_keys, grad_values)


def solution(mesh):
    placed = (
        P(("dom", "head"), None),
        P(("dom", "head"), None),
        P(("dom", "head"), None),
        P(("dom", "head"), None),
        P("dom"),
        P("dom", None),
        P(),
    )
    return jax.shard_map(
        body,
        mesh=mesh,
        in_specs=placed,
        out_specs=(P(("dom", "head"), None), P(("dom", "head"), None), P(("dom", "head"), None)),
        check_vma=False,
    )
```

profile of v0, /device:TPU:0, one launch (start us, length us, event | category | flops | bytes accessed | tf_op | source)
XLA Modules:
  0.0 532.5 jit_solution(8709490764186849700)
XLA Ops:
  2.6 6.3 %all-to-all-start.1 = ((bf16[256,8,128]{2,0,1:T(8,128)(2,1)}), bf16[256,8,128]{2,0,1:T(8,128)(2,1)S(1)}, u32[]{:S(2)}, u32[]{:S(2)}) async-start(bf16[256,8,128]{2,0,1:T(8,128)(2,1)} %copy_bitcast_fusion.3), calls=%async_computation.1 | async-start | bytes 1048576 | tf_op jit(solution)/shard_map/all_to_all | solution.py:31
  10.8 13.4 %all-to-all-done.1 = bf16[256,8,128]{2,0,1:T(8,128)(2,1)S(1)} async-done(((bf16[256,8,128]{2,0,1:T(8,128)(2,1)}), bf16[256,8,128]{2,0,1:T(8,128)(2,1)S(1)}, u32[]{:S(2)}, u32[]{:S(2)}) %all-to-all-start.1) | async-done | bytes 524320 | tf_op jit(solution)/shard_map/all_to_all | solution.py:31
  28.7 14.4 %all-to-all-done.2 = bf16[256,8,128]{2,0,1:T(8,128)(2,1)S(1)} async-done(((bf16[256,8,128]{2,0,1:T(8,128)(2,1)}), bf16[256,8,128]{2,0,1:T(8,128)(2,1)S(1)}, u32[]{:S(2)}, u32[]{:S(2)}) %all-to-all-start.2) | async-done | bytes 524320 | tf_op jit(solution)/shard_map/all_to_all | solution.py:32
  43.0 4.1 all-to-all-start
  50.4 12.2 %all-to-all-done = bf16[256,8,128]{2,0,1:T(8,128)(2,1)} async-done(((bf16[256,8,128]{2,0,1:T(8,128)(2,1)}), bf16[256,8,128]{2,0,1:T(8,128)(2,1)}, u32[]{:S(2)}, u32[]{:S(2)}) %all-to-all-start) | async-done | bytes 524320 | tf_op jit(solution)/shard_map/all_to_all | solution.py:30
  62.5 3.7 all-to-all-start.3
  67.2 12.6 %all-to-all-done.3 = bf16[16,128,256]{2,1,0:T(8,128)(2,1)S(1)} async-done(((bf16[16,128,256]{2,1,0:T(8,128)(2,1)}), bf16[16,128,256]{2,1,0:T(8,128)(2,1)S(1)}, u32[]{:S(2)}, u32[]{:S(2)}) %all-to-all-start.3) | async-done | bytes 1048608 | tf_op jit(solution)/shard_map/all_to_all | solution.py:19
  79.8 4.1 all-to-all-start.4
  85.4 13.9 %all-to-all-done.4 = bf16[256,8,128]{2,0,1:T(8,128)(2,1)} async-done(((bf16[256,8,128]{2,0,1:T(8,128)(2,1)}), bf16[256,8,128]{2,0,1:T(8,128)(2,1)}, u32[]{:S(2)}, u32[]{:S(2)}) %all-to-all-start.4) | async-done | bytes 524320 | tf_op jit(solution)/shard_map/all_to_all | solution.py:33
  101.7 354.6 %while.12 = (s32[]{:T(128)}, f32[32,128,256]{2,1,0:T(8,128)}, bf16[4,512,128]{2,1,0:T(8,128)(2,1)}, s32[4]{0:T(128)S(1)}, s32[16,12]{1,0:T(8,128)}, /*index=5*/b...) while((s32[]{:T(128)}, f32[32,128,256]{2,1,0:T(8,128)}, ...), condition=%wide.region_8.9_spmd, body=%wide.region_0.8_spmd.sunk | while | flops 1044722112 | bytes 177150128 | solution.py:88
  108.0 4.6 copy.120
  123.5 7.1 %fusion.165 = bf16[4,128,64]{1,2,0:T(8,128)(2,1)S(1)} fusion(f32[4,128,1536]{2,1,0:T(8,128)} %fusion.162, f32[4,128]{1,0:T(4,128)S(1)} %dynamic-slice_bitcast_fusion.2, bf16[4,1536,256]{1,2,0:T(8,128)(2,1)} %copy-done.2, f32[4,128,1536]{2,1,0:T(8,128)} %get-tuple-element.159, f32[4,128]{1,0:T(4,128)S(1)} %get-tuple-element.160), kind=kOutput, calls=%fused_computation.41.clone.1 | convolution fusion | flops 106203136 | bytes 13441024 | tf_op jit(solution)/shard_map/while/body/eval_jaxpr/gij,gjd->gid/dot_general | solution.py:72
  130.6 8.5 %fusion.163 = f32[4,1536,64]{1,2,0:T(8,128)} fusion(f32[4,128,1536]{2,1,0:T(8,128)} %fusion.162, f32[4,128]{1,0:T(4,128)S(1)} %dynamic-slice_bitcast_fusion.2, bf16[4,128,128]{2,1,0:T(8,128)(2,1)S(1)} %bitcast.109, f32[4,128,1536]{2,1,0:T(8,128)} %get-tuple-element.159, f32[4,128]{1,0:T(4,128)S(1)} %get-tuple-element.160), kind=kOutput, calls=%fused_computation.30.clone.1 | convolution fusion | flops 106170368 | bytes 14292992 | tf_op jit(solution)/shard_map/while/body/eval_jaxpr/gij,gid->gjd/dot_general | solution.py:75
  142.5 3.8 fusion.156
  146.3 7.2 %fusion.164 = bf16[4,128,64]{1,2,0:T(8,128)(2,1)S(1)} fusion(f32[4,128,1536]{2,1,0:T(8,128)} %fusion.160, f32[4,128]{1,0:T(4,128)S(1)} %dynamic-slice_bitcast_fusion.2, bf16[4,1536,256]{1,2,0:T(8,128)(2,1)} %copy-done.2, f32[4,128,1536]{2,1,0:T(8,128)} %get-tuple-element.157, f32[4,128]{1,0:T(4,128)S(1)} %get-tuple-element.158), kind=kOutput, calls=%fused_computation.42.clone.1 | convolution fusion | flops 106203136 | bytes 13441024 | tf_op jit(solution)/shard_map/while/body/eval_jaxpr/gij,gjd->gid/dot_general | solution.py:72
  153.5 8.6 %fusion.161 = f32[4,1536,64]{1,2,0:T(8,128)} fusion(f32[4,128,1536]{2,1,0:T(8,128)} %fusion.160, f32[4,128]{1,0:T(4,128)S(1)} %dynamic-slice_bitcast_fusion.2, bf16[4,128,128]{2,1,0:T(8,128)(2,1)S(1)} %bitcast.111, f32[4,128,1536]{2,1,0:T(8,128)} %get-tuple-element.157, f32[4,128]{1,0:T(4,128)S(1)} %get-tuple-element.158), kind=kOutput, calls=%fused_computation.28.clone.1 | convolution fusion | flops 106170368 | bytes 14292992 | tf_op jit(solution)/shard_map/while/body/eval_jaxpr/gij,gid->gjd/dot_general | solution.py:75
  168.2 6.6 %copy.122 = f32[4,1536,256]{2,1,0:T(8,128)} copy(f32[4,1536,256]{1,2,0:T(8,128)} %pad_maximum_fusion.6) | data formatting | bytes 12582912 | tf_op jit(solution)/shard_map/while/body/eval_jaxpr/concatenate | solution.py:81
  174.8 14.7 %scatter_fusion = f32[32,128,256]{2,1,0:T(8,128)} fusion(f32[32,128,256]{2,1,0:T(8,128)} %get-tuple-element.177, s32[48]{0:T(128)S(1)} %fusion.155, f32[48,128,256]{2,1,0:T(8,128)} %bitcast.96), kind=kCustom, calls=%fused_computation.2.clone.1 | custom fusion | flops 1572864 | bytes 18874560 | tf_op jit(solution)/shard_map/while/body/eval_jaxpr/scatter-add | solution.py:84
  196.7 4.6 copy.120
  212.1 7.1 %fusion.165 = bf16[4,128,64]{1,2,0:T(8,128)(2,1)S(1)} fusion(f32[4,128,1536]{2,1,0:T(8,128)} %fusion.162, f32[4,128]{1,0:T(4,128)S(1)} %dynamic-slice_bitcast_fusion.2, bf16[4,1536,256]{1,2,0:T(8,128)(2,1)} %copy-done.2, f32[4,128,1536]{2,1,0:T(8,128)} %get-tuple-element.159, f32[4,128]{1,0:T(4,128)S(1)} %get-tuple-element.160), kind=kOutput, calls=%fused_computation.41.clone.1 | convolution fusion | flops 106203136 | bytes 13441024 | tf_op jit(solution)/shard_map/while/body/eval_jaxpr/gij,gjd->gid/dot_general | solution.py:72
  219.2 8.5 %fusion.163 = f32[4,1536,64]{1,2,0:T(8,128)} fusion(f32[4,128,1536]{2,1,0:T(8,128)} %fusion.162, f32[4,128]{1,0:T(4,128)S(1)} %dynamic-slice_bitcast_fusion.2, bf16[4,128,128]{2,1,0:T(8,128)(2,1)S(1)} %bitcast.109, f32[4,128,1536]{2,1,0:T(8,128)} %get-tuple-element.159, f32[4,128]{1,0:T(4,128)S(1)} %get-tuple-element.160), kind=kOutput, calls=%fused_computation.30.clone.1 | convolution fusion | flops 106170368 | bytes 14292992 | tf_op jit(solution)/shard_map/while/body/eval_jaxpr/gij,gid->gjd/dot_general | solution.py:75
  231.2 3.8 fusion.156
  234.9 7.2 %fusion.164 = bf16[4,128,64]{1,2,0:T(8,128)(2,1)S(1)} fusion(f32[4,128,1536]{2,1,0:T(8,128)} %fusion.160, f32[4,128]{1,0:T(4,128)S(1)} %dynamic-slice_bitcast_fusion.2, bf16[4,1536,256]{1,2,0:T(8,128)(2,1)} %copy-done.2, f32[4,128,1536]{2,1,0:T(8,128)} %get-tuple-element.157, f32[4,128]{1,0:T(4,128)S(1)} %get-tuple-element.158), kind=kOutput, calls=%fused_computation.42.clone.1 | convolution fusion | flops 106203136 | bytes 13441024 | tf_op jit(solution)/shard_map/while/body/eval_jaxpr/gij,gjd->gid/dot_general | solution.py:72
  242.1 8.6 %fusion.161 = f32[4,1536,64]{1,2,0:T(8,128)} fusion(f32[4,128,1536]{2,1,0:T(8,128)} %fusion.160, f32[4,128]{1,0:T(4,128)S(1)} %dynamic-slice_bitcast_fusion.2, bf16[4,128,128]{2,1,0:T(8,128)(2,1)S(1)} %bitcast.111, f32[4,128,1536]{2,1,0:T(8,128)} %get-tuple-element.157, f32[4,128]{1,0:T(4,128)S(1)} %get-tuple-element.158), kind=kOutput, calls=%fused_computation.28.clone.1 | convolution fusion | flops 106170368 | bytes 14292992 | tf_op jit(solution)/shard_map/while/body/eval_jaxpr/gij,gid->gjd/dot_general | solution.py:75
  256.9 6.6 %copy.122 = f32[4,1536,256]{2,1,0:T(8,128)} copy(f32[4,1536,256]{1,2,0:T(8,128)} %pad_maximum_fusion.6) | data formatting | bytes 12582912 | tf_op jit(solution)/shard_map/while/body/eval_jaxpr/concatenate | solution.py:81
  263.4 14.8 %scatter_fusion = f32[32,128,256]{2,1,0:T(8,128)} fusion(f32[32,128,256]{2,1,0:T(8,128)} %get-tuple-element.177, s32[48]{0:T(128)S(1)} %fusion.155, f32[48,128,256]{2,1,0:T(8,128)} %bitcast.96), kind=kCustom, calls=%fused_computation.2.clone.1 | custom fusion | flops 1572864 | bytes 18874560 | tf_op jit(solution)/shard_map/while/body/eval_jaxpr/scatter-add | solution.py:84
  285.4 4.6 copy.120
  297.1 3.7 fusion.158
  300.8 7.1 %fusion.165 = bf16[4,128,64]{1,2,0:T(8,128)(2,1)S(1)} fusion(f32[4,128,1536]{2,1,0:T(8,128)} %fusion.162, f32[4,128]{1,0:T(4,128)S(1)} %dynamic-slice_bitcast_fusion.2, bf16[4,1536,256]{1,2,0:T(8,128)(2,1)} %copy-done.2, f32[4,128,1536]{2,1,0:T(8,128)} %get-tuple-element.159, f32[4,128]{1,0:T(4,128)S(1)} %get-tuple-element.160), kind=kOutput, calls=%fused_computation.41.clone.1 | convolution fusion | flops 106203136 | bytes 13441024 | tf_op jit(solution)/shard_map/while/body/eval_jaxpr/gij,gjd->gid/dot_general | solution.py:72
  307.9 8.5 %fusion.163 = f32[4,1536,64]{1,2,0:T(8,128)} fusion(f32[4,128,1536]{2,1,0:T(8,128)} %fusion.162, f32[4,128]{1,0:T(4,128)S(1)} %dynamic-slice_bitcast_fusion.2, bf16[4,128,128]{2,1,0:T(8,128)(2,1)S(1)} %bitcast.109, f32[4,128,1536]{2,1,0:T(8,128)} %get-tuple-element.159, f32[4,128]{1,0:T(4,128)S(1)} %get-tuple-element.160), kind=kOutput, calls=%fused_computation.30.clone.1 | convolution fusion | flops 106170368 | bytes 14292992 | tf_op jit(solution)/shard_map/while/body/eval_jaxpr/gij,gid->gjd/dot_general | solution.py:75
  319.9 3.8 fusion.156
  323.7 7.2 %fusion.164 = bf16[4,128,64]{1,2,0:T(8,128)(2,1)S(1)} fusion(f32[4,128,1536]{2,1,0:T(8,128)} %fusion.160, f32[4,128]{1,0:T(4,128)S(1)} %dynamic-slice_bitcast_fusion.2, bf16[4,1536,256]{1,2,0:T(8,128)(2,1)} %copy-done.2, f32[4,128,1536]{2,1,0:T(8,128)} %get-tuple-element.157, f32[4,128]{1,0:T(4,128)S(1)} %get-tuple-element.158), kind=kOutput, calls=%fused_computation.42.clone.1 | convolution fusion | flops 106203136 | bytes 13441024 | tf_op jit(solution)/shard_map/while/body/eval_jaxpr/gij,gjd->gid/dot_general | solution.py:72
  330.8 8.6 %fusion.161 = f32[4,1536,64]{1,2,0:T(8,128)} fusion(f32[4,128,1536]{2,1,0:T(8,128)} %fusion.160, f32[4,128]{1,0:T(4,128)S(1)} %dynamic-slice_bitcast_fusion.2, bf16[4,128,128]{2,1,0:T(8,128)(2,1)S(1)} %bitcast.111, f32[4,128,1536]{2,1,0:T(8,128)} %get-tuple-element.157, f32[4,128]{1,0:T(4,128)S(1)} %get-tuple-element.158), kind=kOutput, calls=%fused_computation.28.clone.1 | convolution fusion | flops 106170368 | bytes 14292992 | tf_op jit(solution)/shard_map/while/body/eval_jaxpr/gij,gid->gjd/dot_general | solution.py:75
  345.6 6.6 %copy.122 = f32[4,1536,256]{2,1,0:T(8,128)} copy(f32[4,1536,256]{1,2,0:T(8,128)} %pad_maximum_fusion.6) | data formatting | bytes 12582912 | tf_op jit(solution)/shard_map/while/body/eval_jaxpr/concatenate | solution.py:81
  352.2 14.6 %scatter_fusion = f32[32,128,256]{2,1,0:T(8,128)} fusion(f32[32,128,256]{2,1,0:T(8,128)} %get-tuple-element.177, s32[48]{0:T(128)S(1)} %fusion.155, f32[48,128,256]{2,1,0:T(8,128)} %bitcast.96), kind=kCustom, calls=%fused_computation.2.clone.1 | custom fusion | flops 1572864 | bytes 18874560 | tf_op jit(solution)/shard_map/while/body/eval_jaxpr/scatter-add | solution.py:84
  374.0 4.6 copy.120
  389.4 7.1 %fusion.165 = bf16[4,128,64]{1,2,0:T(8,128)(2,1)S(1)} fusion(f32[4,128,1536]{2,1,0:T(8,128)} %fusion.162, f32[4,128]{1,0:T(4,128)S(1)} %dynamic-slice_bitcast_fusion.2, bf16[4,1536,256]{1,2,0:T(8,128)(2,1)} %copy-done.2, f32[4,128,1536]{2,1,0:T(8,128)} %get-tuple-element.159, f32[4,128]{1,0:T(4,128)S(1)} %get-tuple-element.160), kind=kOutput, calls=%fused_computation.41.clone.1 | convolution fusion | flops 106203136 | bytes 13441024 | tf_op jit(solution)/shard_map/while/body/eval_jaxpr/gij,gjd->gid/dot_general | solution.py:72
  396.5 8.5 %fusion.163 = f32[4,1536,64]{1,2,0:T(8,128)} fusion(f32[4,128,1536]{2,1,0:T(8,128)} %fusion.162, f32[4,128]{1,0:T(4,128)S(1)} %dynamic-slice_bitcast_fusion.2, bf16[4,128,128]{2,1,0:T(8,128)(2,1)S(1)} %bitcast.109, f32[4,128,1536]{2,1,0:T(8,128)} %get-tuple-element.159, f32[4,128]{1,0:T(4,128)S(1)} %get-tuple-element.160), kind=kOutput, calls=%fused_computation.30.clone.1 | convolution fusion | flops 106170368 | bytes 14292992 | tf_op jit(solution)/shard_map/while/body/eval_jaxpr/gij,gid->gjd/dot_general | solution.py:75
  408.5 3.8 fusion.156
  412.2 7.2 %fusion.164 = bf16[4,128,64]{1,2,0:T(8,128)(2,1)S(1)} fusion(f32[4,128,1536]{2,1,0:T(8,128)} %fusion.160, f32[4,128]{1,0:T(4,128)S(1)} %dynamic-slice_bitcast_fusion.2, bf16[4,1536,256]{1,2,0:T(8,128)(2,1)} %copy-done.2, f32[4,128,1536]{2,1,0:T(8,128)} %get-tuple-element.157, f32[4,128]{1,0:T(4,128)S(1)} %get-tuple-element.158), kind=kOutput, calls=%fused_computation.42.clone.1 | convolution fusion | flops 106203136 | bytes 13441024 | tf_op jit(solution)/shard_map/while/body/eval_jaxpr/gij,gjd->gid/dot_general | solution.py:72
  419.4 8.6 %fusion.161 = f32[4,1536,64]{1,2,0:T(8,128)} fusion(f32[4,128,1536]{2,1,0:T(8,128)} %fusion.160, f32[4,128]{1,0:T(4,128)S(1)} %dynamic-slice_bitcast_fusion.2, bf16[4,128,128]{2,1,0:T(8,128)(2,1)S(1)} %bitcast.111, f32[4,128,1536]{2,1,0:T(8,128)} %get-tuple-element.157, f32[4,128]{1,0:T(4,128)S(1)} %get-tuple-element.158), kind=kOutput, calls=%fused_computation.28.clone.1 | convolution fusion | flops 106170368 | bytes 14292992 | tf_op jit(solution)/shard_map/while/body/eval_jaxpr/gij,gid->gjd/dot_general | solution.py:75
  434.1 6.6 %copy.122 = f32[4,1536,256]{2,1,0:T(8,128)} copy(f32[4,1536,256]{1,2,0:T(8,128)} %pad_maximum_fusion.6) | data formatting | bytes 12582912 | tf_op jit(solution)/shard_map/while/body/eval_jaxpr/concatenate | solution.py:81
  440.7 14.7 %scatter_fusion = f32[32,128,256]{2,1,0:T(8,128)} fusion(f32[32,128,256]{2,1,0:T(8,128)} %get-tuple-element.177, s32[48]{0:T(128)S(1)} %fusion.155, f32[48,128,256]{2,1,0:T(8,128)} %bitcast.96), kind=kCustom, calls=%fused_computation.2.clone.1 | custom fusion | flops 1572864 | bytes 18874560 | tf_op jit(solution)/shard_map/while/body/eval_jaxpr/scatter-add | solution.py:84
  458.0 16.9 %all_to_all.137 = bf16[16,128,256]{2,1,0:T(8,128)(2,1)S(1)} all-to-all(bf16[16,128,256]{2,1,0:T(8,128)(2,1)S(1)} %slice.107), channel_id=1, replica_groups=mesh['dom'=4,'head'=8] {'dom'}, dimensions={0} | all-to-all | bytes 2097152 | tf_op jit(solution)/shard_map/all_to_all | solution.py:91
  478.4 4.6 copy.83
  484.9 8.8 %all-to-all-done.5 = bf16[8,256,128]{2,1,0:T(8,128)(2,1)S(1)} async-done(((bf16[8,256,128]{2,1,0:T(8,128)(2,1)}), bf16[8,256,128]{2,1,0:T(8,128)(2,1)S(1)}, u32[]{:S(2)}, u32[]{:S(2)}) %all-to-all-start.5) | async-done | bytes 524320 | tf_op jit(solution)/shard_map/all_to_all | solution.py:101
  498.1 14.3 %all-to-all-done.8 = bf16[8,256,128]{2,1,0:T(8,128)(2,1)S(1)} async-done(((bf16[8,256,128]{2,1,0:T(8,128)(2,1)}), bf16[8,256,128]{2,1,0:T(8,128)(2,1)S(1)}, u32[]{:S(2)}, u32[]{:S(2)}) %all-to-all-start.8) | async-done | bytes 524320 | tf_op jit(solution)/shard_map/all_to_all | solution.py:103
  518.4 12.8 %all-to-all-done.7 = bf16[8,256,128]{2,1,0:T(8,128)(2,1)S(1)} async-done(((bf16[8,256,128]{2,1,0:T(8,128)(2,1)}), bf16[8,256,128]{2,1,0:T(8,128)(2,1)S(1)}, u32[]{:S(2)}, u32[]{:S(2)}) %all-to-all-start.7) | async-done | bytes 524320 | tf_op jit(solution)/shard_map/all_to_all | solution.py:102
  (158 shorter events, 136.0 us)
Async XLA Ops:
  0.6 1.1 copy-start
  0.6 27.1 %copy-start.7 = (bf16[256,1024]{1,0:T(8,128)(2,1)S(1)}, bf16[256,1024]{1,0:T(8,128)(2,1)}, u32[]{:S(2)}) copy-start(bf16[256,1024]{1,0:T(8,128)(2,1)} %param.9) | copy-start | bytes 1572868
  2.6 21.7 %all-to-all-start.1 = ((bf16[256,8,128]{2,0,1:T(8,128)(2,1)}), bf16[256,8,128]{2,0,1:T(8,128)(2,1)S(1)}, u32[]{:S(2)}, u32[]{:S(2)}) async-start(bf16[256,8,128]{2,0,1:T(8,128)(2,1)} %copy_bitcast_fusion.3), calls=%async_computation.1 | async-start | bytes 1048576 | tf_op jit(solution)/shard_map/all_to_all | solution.py:31
  24.3 18.8 %all-to-all-start.2 = ((bf16[256,8,128]{2,0,1:T(8,128)(2,1)}), bf16[256,8,128]{2,0,1:T(8,128)(2,1)S(1)}, u32[]{:S(2)}, u32[]{:S(2)}) async-start(bf16[256,8,128]{2,0,1:T(8,128)(2,1)} %copy_bitcast_fusion.2), calls=%async_computation.2 | async-start | bytes 1048576 | tf_op jit(solution)/shard_map/all_to_all | solution.py:32
  43.0 19.5 %all-to-all-start = ((bf16[256,8,128]{2,0,1:T(8,128)(2,1)}), bf16[256,8,128]{2,0,1:T(8,128)(2,1)}, u32[]{:S(2)}, u32[]{:S(2)}) async-start(bf16[256,8,128]{2,0,1:T(8,128)(2,1)} %copy_bitcast_fusion.4), calls=%async_computation | async-start | bytes 1048576 | tf_op jit(solution)/shard_map/all_to_all | solution.py:30
  48.0 0.5 copy-start.10
  49.2 17.1 %copy-start.8 = (bf16[256,1024]{1,0:T(8,128)(2,1)S(1)}, bf16[256,1024]{1,0:T(8,128)(2,1)}, u32[]{:S(2)}) copy-start(bf16[256,1024]{1,0:T(8,128)(2,1)} %param.12) | copy-start | bytes 1572868
  49.2 34.7 %copy-start.9 = (s32[2048]{0:T(1024)S(1)}, s32[2048]{0:T(1024)}, u32[]{:S(2)}) copy-start(s32[2048]{0:T(1024)} %param.13) | copy-start | bytes 24580
  62.5 17.2 %all-to-all-start.3 = ((bf16[16,128,256]{2,1,0:T(8,128)(2,1)}), bf16[16,128,256]{2,1,0:T(8,128)(2,1)S(1)}, u32[]{:S(2)}, u32[]{:S(2)}) async-start(bf16[16,128,256]{2,1,0:T(8,128)(2,1)} %broadcast_select_fusion.1), calls=%async_computation.3 | async-start | bytes 2097152 | tf_op jit(solution)/shard_map/all_to_all | solution.py:19
  79.7 4.2 copy-start.6
  79.8 19.5 %all-to-all-start.4 = ((bf16[256,8,128]{2,0,1:T(8,128)(2,1)}), bf16[256,8,128]{2,0,1:T(8,128)(2,1)}, u32[]{:S(2)}, u32[]{:S(2)}) async-start(bf16[256,8,128]{2,0,1:T(8,128)(2,1)} %copy_bitcast_fusion.1), calls=%async_computation.4 | async-start | bytes 1048576 | tf_op jit(solution)/shard_map/all_to_all | solution.py:33
  114.9 2.6 copy-start.2
  162.1 2.6 copy-start.3
  162.1 2.8 copy-start.4
  162.1 3.3 copy-start.5
  203.5 2.6 copy-start.2
  250.7 2.6 copy-start.3
  250.7 2.8 copy-start.4
  250.7 3.3 copy-start.5
  292.2 2.6 copy-start.2
  339.4 2.6 copy-start.3
  339.4 2.8 copy-start.4
  339.4 3.3 copy-start.5
  380.8 2.6 copy-start.2
  428.0 2.6 copy-start.3
  428.0 2.8 copy-start.4
  428.0 3.3 copy-start.5
  474.9 18.8 %all-to-all-start.5 = ((bf16[8,256,128]{2,1,0:T(8,128)(2,1)}), bf16[8,256,128]{2,1,0:T(8,128)(2,1)S(1)}, u32[]{:S(2)}, u32[]{:S(2)}) async-start(bf16[8,256,128]{2,1,0:T(8,128)(2,1)} %bitcast.17), calls=%async_computation.5 | async-start | bytes 1048576 | tf_op jit(solution)/shard_map/all_to_all | solution.py:101
  478.4 4.6 copy-start.11
  493.7 18.8 %all-to-all-start.8 = ((bf16[8,256,128]{2,1,0:T(8,128)(2,1)}), bf16[8,256,128]{2,1,0:T(8,128)(2,1)S(1)}, u32[]{:S(2)}, u32[]{:S(2)}) async-start(bf16[8,256,128]{2,1,0:T(8,128)(2,1)} %bitcast.25), calls=%async_computation.8 | async-start | bytes 1048576 | tf_op jit(solution)/shard_map/all_to_all | solution.py:103
  512.5 18.8 %all-to-all-start.7 = ((bf16[8,256,128]{2,1,0:T(8,128)(2,1)}), bf16[8,256,128]{2,1,0:T(8,128)(2,1)S(1)}, u32[]{:S(2)}, u32[]{:S(2)}) async-start(bf16[8,256,128]{2,1,0:T(8,128)(2,1)} %bitcast.22), calls=%async_computation.7 | async-start | bytes 1048576 | tf_op jit(solution)/shard_map/all_to_all | solution.py:102
  516.0 16.5 %copy-start.1 = (bf16[256,1024]{1,0:T(8,128)(2,1)S(1)}, bf16[256,1024]{1,0:T(8,128)(2,1)}, u32[]{:S(2)}) copy-start(bf16[256,1024]{1,0:T(8,128)(2,1)} %param.10) | copy-start | bytes 1572868
where the time goes:
time: 535 us; the launch traced here: 532 us
  matrix products  200 us (37%)
  waiting for transfers between devices  102 us (19%)
  local copies, waits for them, and re-layouts  89.5 us (17%)
  other arithmetic  85.2 us (16%)
  starting transfers between devices  32.3 us (6%)
  blocking collectives  16.9 us (3%)
  loops' own time  5.52 us (1%)
    dot_general x8, matrix products, group(): jnp.einsum('gij,gid->gjd', dscores, query_one, preferred_element_type=jnp...  68.3 us
    scatter-add x4, other arithmetic, group(): acc = acc.at[picks].add(contrib)  58.8 us
    dot_general x8, matrix products, group(): jnp.einsum('gij,gjd->gid', dscores, keys_n, preferred_element_type=jnp.fl...  57 us
    sub x8, matrix products, group(): expo = jnp.exp(scores - top)  29.9 us
    gather x8, local copies, waits for them, and re-layouts, group(): gathered = jnp.take(table, picks, axis=0).reshape(4, span, 2 * width)  28.6 us
    concatenate x4, local copies, waits for them, and re-layouts, group(): jnp.concatenate(grad_k_heads + grad_v_heads, -1)  26.3 us
    dot_general x8, matrix products, group(): jnp.einsum('gij,gid->gjd', probs_b, grad_one, preferred_element_type=jnp....  24.4 us
    dot_general x8, matrix products, group(): jnp.einsum('gid,gjd->gij', grad_one, values_n, preferred_element_type=jnp...  19.4 us
  transfers between devices with their start and end apart: 8, of which 8 were waited for; matrix products, arithmetic and copies ran while one was open for 3% of the time, Pallas kernels for 0%

commit v1 on v0

v1 whole, which is shorter than its diff:
```python
import functools
import math

import jax
import jax.numpy as jnp
from jax import lax
from jax.experimental import pallas as pl
from jax.experimental.pallas import tpu as pltpu
from jax.sharding import PartitionSpec as P

D = 1024
H = 16
NBR = 12
BS = 128
HD = D // H
LOG2E = 1.4426950408889634
VMEM_LIMIT = 56 << 20

bf16 = jnp.bfloat16
f32 = jnp.float32


def params():
    return pltpu.CompilerParams(vmem_limit_bytes=VMEM_LIMIT)


def cost(flops, bytes_accessed):
    return pl.CostEstimate(flops=flops, bytes_accessed=bytes_accessed, transcendentals=0)


VMEM = pl.BlockSpec(memory_space=pltpu.VMEM)
SMEM = pl.BlockSpec(memory_space=pltpu.SMEM)
ANY = pl.BlockSpec(memory_space=pl.ANY)


def pack_kernel(first, n, q_ref, k_ref, v_ref, g_ref, out_ref):
    rows = q_ref.shape[0]
    for j in range(n):
        cols = pl.ds((first + j) * HD, HD)
        out_ref[j, pl.ds(0, rows), pl.ds(0, HD)] = k_ref[:, cols]
        out_ref[j, pl.ds(0, rows), pl.ds(HD, HD)] = v_ref[:, cols]
        out_ref[j, pl.ds(rows, rows), pl.ds(0, HD)] = q_ref[:, cols]
        out_ref[j, pl.ds(rows, rows), pl.ds(HD, HD)] = g_ref[:, cols]


def pack(queries, keys, values, grads, phase, n):
    rows = queries.shape[0]
    return pl.pallas_call(
        functools.partial(pack_kernel, phase * n, n),
        out_shape=jax.ShapeDtypeStruct((n, 2 * rows, 2 * HD), bf16),
        in_specs=[VMEM] * 4,
        out_specs=VMEM,
        compiler_params=params(),
        cost_estimate=cost(0, 12 * rows * D),
        name="pack",
    )(queries, keys, values, grads)


def lend_kernel(parts, cap, bpd, lists_ref, kv_ref, *outs):
    for k in range(1, parts):
        for s in range(cap):
            b = lists_ref[k * cap + s]
            outs[k - 1][s] = kv_ref[lax.div(b, bpd), lax.rem(b, bpd)]


def lend(lists, recv, parts, cap, bpd):
    return pl.pallas_call(
        functools.partial(lend_kernel, parts, cap, bpd),
        out_shape=[jax.ShapeDtypeStruct((cap, BS, 2 * HD), bf16)] * (parts - 1),
        in_specs=[SMEM, VMEM],
        out_specs=[VMEM] * (parts - 1),
        compiler_params=params(),
        cost_estimate=cost(0, 2 * parts * cap * BS * 4 * HD),
        name="lend",
    )(lists, recv)


def attend_kernel(parts, cap, n, bpd, idx_ref, recv_ref, tau_ref, *refs):
    borrowed = refs[: parts - 1]
    dq_ref, own_ref = refs[parts - 1 : parts + 1]
    back = refs[parts + 1 : 2 * parts]
    tab, kt_tab, acc, s_buf, dp_buf, sem = refs[2 * parts :]
    nblk = n * bpd
    slots = (parts - 1) * cap
    copies = [
        pltpu.make_async_copy(recv_ref.at[j, pl.ds(0, bpd)], tab.at[pl.ds(j * bpd, bpd)], sem.at[j])
        for j in range(n)
    ]
    for k in range(1, parts):
        copies.append(
            pltpu.make_async_copy(borrowed[k - 1], tab.at[pl.ds(nblk + (k - 1) * cap, cap)], sem.at[n + k])
        )
    for c in copies:
        c.start()
    acc[...] = jnp.zeros_like(acc)
    for c in copies:
        c.wait()

    def flip(t, _):
        kt_tab[t] = tab[t].astype(f32).T[:HD].astype(bf16)
        return 0

    lax.fori_loop(0, nblk + slots, flip, 0)
    lane = lax.broadcasted_iota(jnp.int32, (BS, 2 * HD), 1)
    low = lane < HD
    zero = jnp.zeros((BS, 2 * HD), bf16)

    def one(r, g, rb):
        qg = recv_ref[g, bpd + rb]
        both = jnp.concatenate([jnp.where(low, qg, zero), jnp.where(low, zero, qg)], 0)
        top = None
        where = [idx_ref[r * NBR + i] for i in range(NBR)]
        for i in range(NBR):
            e = where[i]
            kv = tab[e]
            res = lax.dot_general(kv, both, (((1,), (1,)), ((), ())), preferred_element_type=f32)
            s = res[:, :BS]
            s_buf[rb, i] = s
            dp_buf[rb, i] = res[:, BS:]
            m8 = jnp.max(s.reshape(BS // 8, 8, BS), axis=0)
            top = m8 if top is None else jnp.maximum(top, m8)
        m = jnp.max(top, axis=0, keepdims=True)
        tau = tau_ref[pl.ds(r, 1), :]
        c = tau * LOG2E
        total = weighted = None
        for i in range(NBR):
            ex = jnp.exp2((s_buf[rb, i] - m) * c)
            s_buf[rb, i] = ex
            l8 = jnp.sum(ex.reshape(BS // 8, 8, BS), axis=0)
            d8 = jnp.sum((ex * dp_buf[rb, i]).reshape(BS // 8, 8, BS), axis=0)
            total = l8 if total is None else total + l8
            weighted = d8 if weighted is None else weighted + d8
        norm = jnp.sum(total, axis=0, keepdims=True)
        inv = 1.0 / norm
        delta = jnp.sum(weighted, axis=0, keepdims=True) * inv
        dq = None
        for i in range(0, NBR, 2):
            us = []
            for j in (i, i + 1):
                e = where[j]
                p = s_buf[rb, j] * inv
                u = (p * (dp_buf[rb, j] - delta) * tau).astype(bf16)
                us.append(u)
                part = jnp.dot(jnp.concatenate([u, p.astype(bf16)], 1), both, preferred_element_type=f32)
                acc[e] += part
            kt = jnp.concatenate([kt_tab[where[i]], kt_tab[where[i + 1]]], 1)
            d = jnp.dot(kt, jnp.concatenate(us, 0), preferred_element_type=f32)
            dq = d if dq is None else dq + d
        return dq

    def pair(g, _):
        dqs = [one(g * bpd + rb, g, rb) for rb in range(bpd)]
        dq_ref[g] = jnp.concatenate(dqs, 0).T.astype(bf16)
        return 0

    lax.fori_loop(0, n, pair, 0)
    own_ref[...] = acc[pl.ds(0, nblk)]
    for k in range(1, parts):
        back[k - 1][...] = acc[pl.ds(nblk + (k - 1) * cap, cap)].astype(bf16)


def attend(idx, recv, tau, borrowed, parts, cap, n, bpd):
    nblk = n * bpd
    slots = (parts - 1) * cap
    width = 2 * HD
    return pl.pallas_call(
        functools.partial(attend_kernel, parts, cap, n, bpd),
        out_shape=[
            jax.ShapeDtypeStruct((n, BS, width), bf16),
            jax.ShapeDtypeStruct((nblk, BS, width), f32),
        ]
        + [jax.ShapeDtypeStruct((cap, BS, width), bf16)] * (parts - 1),
        in_specs=[SMEM, VMEM, VMEM] + [VMEM] * (parts - 1),
        out_specs=[VMEM] * (parts + 1),
        scratch_shapes=[
            pltpu.VMEM((nblk + slots, BS, width), bf16),
            pltpu.VMEM((nblk + slots, HD, BS), bf16),
            pltpu.VMEM((nblk + slots, BS, width), f32),
            pltpu.VMEM((bpd, NBR, BS, BS), f32),
            pltpu.VMEM((bpd, NBR, BS, BS), f32),
            pltpu.SemaphoreType.DMA((n + parts,)),
        ],
        compiler_params=params(),
        cost_estimate=cost(nblk * NBR * BS * BS * HD * 2 * 5 * 2, 6 << 20),
        name="attend",
    )(idx, recv, tau, *borrowed)


def gather_kernel(parts, cap, bpd, lists_ref, dq_ref, own_ref, *refs):
    returned, out_ref, total = refs[: parts - 1], refs[parts - 1], refs[parts]
    n = dq_ref.shape[0]
    total[...] = own_ref[...]
    for k in range(1, parts):
        for s in range(cap):
            b = lists_ref[k * cap + s]
            total[b] += returned[k - 1][s].astype(f32)
    for j in range(n):
        out_ref[j, pl.ds(0, BS)] = dq_ref[j]
        for b in range(bpd):
            out_ref[j, pl.ds((1 + b) * BS, BS)] = total[j * bpd + b].astype(bf16)


def collect(lists, dq, own, returned, parts, cap, bpd):
    n = dq.shape[0]
    return pl.pallas_call(
        functools.partial(gather_kernel, parts, cap, bpd),
        out_shape=jax.ShapeDtypeStruct((n, (1 + bpd) * BS, 2 * HD), bf16),
        in_specs=[SMEM] + [VMEM] * (parts + 1),
        out_specs=VMEM,
        scratch_shapes=[pltpu.VMEM(own.shape, f32)],
        compiler_params=params(),
        cost_estimate=cost(0, 4 << 20),
        name="collect",
    )(lists, dq, own, *returned)


def unpack_kernel(n, phases, bpd, *refs):
    recv = refs[:phases]
    gq, gk, gv = refs[phases:]
    rows = bpd * BS
    for f in range(phases):
        for j in range(n):
            cols = pl.ds((f * n + j) * HD, HD)
            for b in range(bpd):
                gq[pl.ds(b * BS, BS), cols] = recv[f][j, pl.ds(0, BS), pl.ds(b * HD, HD)]
            gk[:, cols] = recv[f][j, pl.ds(BS, rows), pl.ds(0, HD)]
            gv[:, cols] = recv[f][j, pl.ds(BS, rows), pl.ds(HD, HD)]


def unpack(recv, n, bpd):
    rows = bpd * BS
    return pl.pallas_call(
        functools.partial(unpack_kernel, n, len(recv), bpd),
        out_shape=[jax.ShapeDtypeStruct((rows, D), bf16)] * 3,
        in_specs=[VMEM] * len(recv),
        out_specs=[VMEM] * 3,
        compiler_params=params(),
        cost_estimate=cost(0, 4 << 20),
        name="unpack",
    )(*recv)


def swap(x, k, parts):
    return lax.ppermute(x, "dom", [(i, i ^ k) for i in range(parts)])


def body(node_queries, node_keys, node_values, out_grad, degrees, neighbor_blocks, send_slots):
    n = lax.axis_size("head")
    parts = lax.axis_size("dom")
    cap = send_slots.shape[2]
    phases = H // n
    rows = node_queries.shape[0]
    bpd = rows // BS
    nblk = n * bpd
    me = lax.axis_index("dom")
    hop = jnp.arange(parts, dtype=jnp.int32)
    mine = jnp.maximum(lax.dynamic_index_in_dim(send_slots, me, 0, keepdims=False), 0)
    pick = (hop[:, None] == (hop[None, :] ^ me)).astype(jnp.int32)
    lists = jnp.sum(pick[:, :, None] * mine[None], axis=1).reshape(-1)
    away = neighbor_blocks - nblk
    moved = nblk + ((away // cap) ^ me) * cap + away % cap - cap
    idx = jnp.where(away < 0, neighbor_blocks, moved).reshape(-1)
    tau = (jnp.log(degrees.astype(f32)) / math.log(64.0) / math.sqrt(HD)).reshape(nblk, BS)

    sent = [pack(node_queries, node_keys, node_values, out_grad, f, n) for f in range(phases)]
    recv = []
    for f in range(phases):
        recv.append(
            lax.all_to_all(sent[f], "head", split_axis=0, concat_axis=0, tiled=True).reshape(
                n, 2 * bpd, BS, 2 * HD
            )
        )
    outs = []
    for f in range(phases):
        lent = lend(lists, recv[f], parts, cap, bpd)
        borrowed = [
            swap(lent[k - 1], k, parts) for k in range(1, parts)
        ]
        dq, own, *back = attend(idx, recv[f], tau, borrowed, parts, cap, n, bpd)
        returned = [swap(back[k - 1], k, parts) for k in range(1, parts)]
        total = collect(lists, dq, own, returned, parts, cap, bpd)
        outs.append(lax.all_to_all(total, "head", split_axis=0, concat_axis=0, tiled=True))
    return tuple(unpack(outs, n, bpd))


def solution(mesh):
    placed = (
        P(("dom", "head"), None),
        P(("dom", "head"), None),
        P(("dom", "head"), None),
        P(("dom", "head"), None),
        P("dom"),
        P("dom", None),
        P(),
    )
    return jax.shard_map(
        body,
        mesh=mesh,
        in_specs=placed,
        out_specs=(P(("dom", "head"), None), P(("dom", "head"), None), P(("dom", "head"), None)),
        check_vma=False,
    )
```

time: 535 us -> 174 us (0.33)
  matrix products: 200 us -> 0 us
  local copies, waits for them, and re-layouts: 89.5 us -> 5.28 us
  other arithmetic: 85.2 us -> 1.41 us
  Pallas kernels: 0 us -> 65.5 us
  waiting for transfers between devices: 102 us -> 45.9 us
  blocking collectives: 16.9 us -> 25.4 us
  loops' own time: 5.52 us -> 0 us
    dot_general x33 -> x0, matrix products: 170 us -> none  [the longest x8 68.3 us: group(): jnp.einsum('gij,gid->gjd', dscores, query_one, preferred_element_type=jnp...]
    all_to_all x8 -> x3, waiting for transfers between devices: 102 us -> 23.5 us  [the longest x2 23.5 us: body(): lax.all_to_all(sent[f], 'head', split_axis=0, concat_axis=0, tiled=True)]
    pallas_call x0 -> x9, Pallas kernels: none -> 65.5 us  [the longest x2 46.7 us: attend(): pl.pallas_call(functools.partial(attend_kernel, parts, cap, n, bpd), out_...]
    scatter-add x4 -> x0, other arithmetic: 58.8 us -> none  [group(): acc = acc.at[picks].add(contrib)]
    sub x8 -> x0, matrix products: 29.9 us -> none  [group(): expo = jnp.exp(scores - top)]
    gather x9 -> x0, local copies, waits for them, and re-layouts: 29.2 us -> none  [the longest x8 28.6 us: group(): gathered = jnp.take(table, picks, axis=0).reshape(4, span, 2 * width)]
    concatenate x8 -> x0, local copies, waits for them, and re-layouts: 26.8 us -> none  [the longest x4 26.3 us: group(): jnp.concatenate(grad_k_heads + grad_v_heads, -1)]
    ppermute x0 -> x12, waiting for transfers between devices: none -> 22.4 us  [swap(): return lax.ppermute(x, 'dom', [(i, i ^ k) for i in range(parts)])]
  transfers between devices with their start and end apart: 8 -> 15, of which waited for: 8 -> 11; matrix products, arithmetic and copies ran while one was open for 3% -> 2% of each run, Pallas kernels for 0% -> 34%
where the time goes in v1:
time: 174 us; the launch traced here: 173 us
  Pallas kernels  65.5 us (38%)
  waiting for transfers between devices  45.9 us (26%)
  starting transfers between devices  28.5 us (16%)
  blocking collectives  25.4 us (15%)
  local copies, waits for them, and re-layouts  5.28 us (3%)
    pallas_call x2, Pallas kernels, attend(): pl.pallas_call(functools.partial(attend_kernel, parts, cap, n, bpd), out_...  46.7 us
    all_to_all x1, blocking collectives, body(): lax.all_to_all(total, 'head', split_axis=0, concat_axis=0, tiled=True)  25.4 us
    all_to_all x2, waiting for transfers between devices, body(): lax.all_to_all(sent[f], 'head', split_axis=0, concat_axis=0, tiled=True)  23.5 us
    ppermute x12, waiting for transfers between devices, swap(): return lax.ppermute(x, 'dom', [(i, i ^ k) for i in range(parts)])  22.4 us
    ppermute x12, starting transfers between devices, swap(): return lax.ppermute(x, 'dom', [(i, i ^ k) for i in range(parts)])  14.1 us
    all_to_all x2, starting transfers between devices, body(): lax.all_to_all(sent[f], 'head', split_axis=0, concat_axis=0, tiled=True)  9.88 us
    pallas_call x2, Pallas kernels, pack(): pl.pallas_call(functools.partial(pack_kernel, phase * n, n), out_shape=ja...  6.18 us
    pallas_call x2, Pallas kernels, collect(): pl.pallas_call(functools.partial(gather_kernel, parts, cap, bpd), out_sha...  5 us
  transfers between devices with their start and end apart: 15, of which 11 were waited for; matrix products, arithmetic and copies ran while one was open for 2% of the time, Pallas kernels for 34%

profile of v1, /device:TPU:0, one launch (start us, length us, event | category | flops | bytes accessed | tf_op | source)
XLA Modules:
  0.0 172.8 jit_solution(8336626222477119533)
XLA Ops:
  0.6 3.1 %pack.3 = bf16[8,512,128]{2,1,0:T(8,128)(2,1)} custom-call(bf16[256,1024]{1,0:T(8,128)(2,1)} %q_ref.3, bf16[256,1024]{1,0:T(8,128)(2,1)} %k_ref.3, bf16[256,1024]{1,0:T(8,128)(2,1)} %v_ref.3, bf16[256,1024]{1,0:T(8,128)(2,1)} %g_ref.3), custom_call_target="tpu_custom_call" | custom-call | bytes 3145728 | tf_op jit(solution)/shard_map/pack/pallas_call | solution.py:48
  3.7 6.3 %all-to-all-start.2 = ((bf16[8,512,128]{2,1,0:T(8,128)(2,1)}), bf16[8,512,128]{2,1,0:T(8,128)(2,1)S(1)}, u32[]{:S(2)}, u32[]{:S(2)}) async-start(bf16[8,512,128]{2,1,0:T(8,128)(2,1)} %pack.3), calls=%async_computation.2 | async-start | bytes 2097152 | tf_op jit(solution)/shard_map/all_to_all | solution.py:269
  10.0 3.1 %pack.2 = bf16[8,512,128]{2,1,0:T(8,128)(2,1)} custom-call(bf16[256,1024]{1,0:T(8,128)(2,1)} %q_ref.3, bf16[256,1024]{1,0:T(8,128)(2,1)} %k_ref.3, bf16[256,1024]{1,0:T(8,128)(2,1)} %v_ref.3, bf16[256,1024]{1,0:T(8,128)(2,1)} %g_ref.3), custom_call_target="tpu_custom_call" | custom-call | bytes 3145728 | tf_op jit(solution)/shard_map/pack/pallas_call | solution.py:48
  13.1 23.5 %all-to-all-done.2 = bf16[8,512,128]{2,1,0:T(8,128)(2,1)S(1)} async-done(((bf16[8,512,128]{2,1,0:T(8,128)(2,1)}), bf16[8,512,128]{2,1,0:T(8,128)(2,1)S(1)}, u32[]{:S(2)}, u32[]{:S(2)}) %all-to-all-start.2) | async-done | bytes 1048608 | tf_op jit(solution)/shard_map/all_to_all | solution.py:269
  36.6 3.6 %all-to-all-start = ((bf16[8,512,128]{2,1,0:T(8,128)(2,1)}), bf16[8,512,128]{2,1,0:T(8,128)(2,1)S(1)}, u32[]{:S(2)}, u32[]{:S(2)}) async-start(bf16[8,512,128]{2,1,0:T(8,128)(2,1)} %pack.2), calls=%async_computation | async-start | bytes 2097152 | tf_op jit(solution)/shard_map/all_to_all | solution.py:269
  40.2 0.0 copy-start.9
  40.2 0.7 maximum_bitcast_fusion
  40.9 0.1 multiply_reduce_fusion
  41.0 0.7 reshape.46.lists_ref
  41.7 0.7 reshape.47.idx_ref
  42.4 2.0 %lend.3 = (bf16[4,128,128]{2,1,0:T(8,128)(2,1)}, bf16[4,128,128]{2,1,0:T(8,128)(2,1)}, bf16[4,128,128]{2,1,0:T(8,128)(2,1)}) custom-call(s32[16]{0:T(128)} %reshape.46.lists_ref, bf16[8,4,128,128]{3,2,1,0:T(8,128)(2,1)} %bitcast.8), custom_call_target="tpu_custom_call" | custom-call | bytes 1048576 | tf_op jit(solution)/shard_map/lend/pallas_call | solution.py:67
  44.4 1.5 collective-permute-start.6
  45.9 1.5 collective-permute-start.7
  47.5 0.5 collective-permute-start.8
  47.9 0.6 multiply_bitcast_fusion.tau_ref
  48.6 2.2 %collective-permute-done.6.refs_0_ = bf16[4,128,128]{2,1,0:T(8,128)(2,1)S(1)} collective-permute-done((bf16[4,128,128]{2,1,0:T(8,128)(2,1)}, bf16[4,128,128]{2,1,0:T(8,128)(2,1)S(1)}, u32[]{:S(2)}, u32[]{:S(2)}) %collective-permute-start.6) | collective-permute-done | bytes 131104 | tf_op jit(solution)/shard_map/ppermute | solution.py:244
  50.8 3.7 %collective-permute-done.7.refs_1_ = bf16[4,128,128]{2,1,0:T(8,128)(2,1)S(1)} collective-permute-done((bf16[4,128,128]{2,1,0:T(8,128)(2,1)}, bf16[4,128,128]{2,1,0:T(8,128)(2,1)S(1)}, u32[]{:S(2)}, u32[]{:S(2)}) %collective-permute-start.7) | collective-permute-done | bytes 131104 | tf_op jit(solution)/shard_map/ppermute | solution.py:244
  54.5 0.6 copy-done.14
  55.1 0.7 copy-done.16
  55.8 23.4 %attend.3 = (bf16[8,128,128]{2,1,0:T(8,128)(2,1)}, f32[16,128,128]{2,1,0:T(8,128)}, bf16[4,128,128]{2,1,0:T(8,128)(2,1)}, bf16[4,128,128]{2,1,0:T(8,128)(2,1)}, bf16[4,128,128]{2,1,0:T(8,128)(2,1)}) custom-call(s32[192]{0:T(256)} %reshape.47.idx_ref, bf16[8,4,128,128]{3,2,1,0:T(8,128)(2,1)} %bitcast.9, f32[16,128]{1,0:T(8,128)} %multiply_bitcast_fusion.tau_ref, ...), custom_call_target="tpu_custom_call" | custom-call | flops 4026531840 | bytes 6291456 | tf_op jit(solution)/shard_map/attend/pallas_call | solution.py:166
  79.1 0.7 collective-permute-start.9
  79.8 1.5 collective-permute-start.10
  81.3 1.4 collective-permute-start.11
  82.7 3.0 %collective-permute-done.9.refs_0_ = bf16[4,128,128]{2,1,0:T(8,128)(2,1)S(1)} collective-permute-done((bf16[4,128,128]{2,1,0:T(8,128)(2,1)}, bf16[4,128,128]{2,1,0:T(8,128)(2,1)S(1)}, u32[]{:S(2)}, u32[]{:S(2)}) %collective-permute-start.9) | collective-permute-done | bytes 131104 | tf_op jit(solution)/shard_map/ppermute | solution.py:244
  85.7 0.9 collective-permute-done.10.refs_1_
  86.7 1.2 collective-permute-done.11.refs_2_
  87.8 0.6 copy-done.8
  88.5 2.5 %collect.3 = bf16[8,384,128]{2,1,0:T(8,128)(2,1)} custom-call(s32[16]{0:T(128)} %reshape.46.lists_ref, bf16[8,128,128]{2,1,0:T(8,128)(2,1)} %get-tuple-element.30.dq_ref, f32[16,128,128]{2,1,0:T(8,128)} %get-tuple-element.31.own_ref, bf16[4,128,128]{2,1,0:T(8,128)(2,1)} %copy-done.4, bf16[4,128,128]{2,1,0:T(8,128)(2,1)} %copy-done.6, ...), custom_call_target="tpu_custom_call" | custom-call | bytes 4194304 | tf_op jit(solution)/shard_map/collect/pallas_call | solution.py:205
  91.0 4.5 %all-to-all-start.3 = ((bf16[8,384,128]{2,1,0:T(8,128)(2,1)}), bf16[8,384,128]{2,1,0:T(8,128)(2,1)S(1)}, u32[]{:S(2)}, u32[]{:S(2)}) async-start(bf16[8,384,128]{2,1,0:T(8,128)(2,1)} %collect.3), calls=%async_computation.3 | async-start | bytes 1572864 | tf_op jit(solution)/shard_map/all_to_all | solution.py:282
  95.5 2.0 %lend.2 = (bf16[4,128,128]{2,1,0:T(8,128)(2,1)}, bf16[4,128,128]{2,1,0:T(8,128)(2,1)}, bf16[4,128,128]{2,1,0:T(8,128)(2,1)}) custom-call(s32[16]{0:T(128)} %reshape.46.lists_ref, bf16[8,4,128,128]{3,2,1,0:T(8,128)(2,1)} %bitcast.6), custom_call_target="tpu_custom_call" | custom-call | bytes 1048576 | tf_op jit(solution)/shard_map/lend/pallas_call | solution.py:67
  97.5 1.6 collective-permute-start
  99.1 0.9 collective-permute-start.1
  100.1 1.0 collective-permute-start.2
  101.0 2.9 %collective-permute-done.refs_0_ = bf16[4,128,128]{2,1,0:T(8,128)(2,1)S(1)} collective-permute-done((bf16[4,128,128]{2,1,0:T(8,128)(2,1)}, bf16[4,128,128]{2,1,0:T(8,128)(2,1)S(1)}, u32[]{:S(2)}, u32[]{:S(2)}) %collective-permute-start) | collective-permute-done | bytes 131104 | tf_op jit(solution)/shard_map/ppermute | solution.py:244
  103.9 3.9 %collective-permute-done.1.refs_1_ = bf16[4,128,128]{2,1,0:T(8,128)(2,1)S(1)} collective-permute-done((bf16[4,128,128]{2,1,0:T(8,128)(2,1)}, bf16[4,128,128]{2,1,0:T(8,128)(2,1)S(1)}, u32[]{:S(2)}, u32[]{:S(2)}) %collective-permute-start.1) | collective-permute-done | bytes 131104 | tf_op jit(solution)/shard_map/ppermute | solution.py:244
  107.8 0.6 copy-done.13
  108.4 0.7 copy-done.15
  109.1 23.4 %attend.2 = (bf16[8,128,128]{2,1,0:T(8,128)(2,1)}, f32[16,128,128]{2,1,0:T(8,128)}, bf16[4,128,128]{2,1,0:T(8,128)(2,1)}, bf16[4,128,128]{2,1,0:T(8,128)(2,1)}, bf16[4,128,128]{2,1,0:T(8,128)(2,1)}) custom-call(s32[192]{0:T(256)} %reshape.47.idx_ref, bf16[8,4,128,128]{3,2,1,0:T(8,128)(2,1)} %bitcast.7, f32[16,128]{1,0:T(8,128)} %multiply_bitcast_fusion.tau_ref, ...), custom_call_target="tpu_custom_call" | custom-call | flops 4026531840 | bytes 6291456 | tf_op jit(solution)/shard_map/attend/pallas_call | solution.py:166
  132.5 0.1 collective-permute-start.3
  132.5 1.1 collective-permute-start.4
  133.6 2.4 %collective-permute-start.5 = (bf16[4,128,128]{2,1,0:T(8,128)(2,1)}, bf16[4,128,128]{2,1,0:T(8,128)(2,1)S(1)}, u32[]{:S(2)}, u32[]{:S(2)}) collective-permute-start(bf16[4,128,128]{2,1,0:T(8,128)(2,1)} %get-tuple-element.26), channel_id=1, source_target_pairs={{0,24},{8,16},{16,8},{24,0},{1,25},{9,17},{17,9},{25,1},{2,26},{10... | collective-permute-start | bytes 393224 | tf_op jit(solution)/shard_map/ppermute | solution.py:244
  136.0 2.8 %collective-permute-done.3.refs_0_ = bf16[4,128,128]{2,1,0:T(8,128)(2,1)S(1)} collective-permute-done((bf16[4,128,128]{2,1,0:T(8,128)(2,1)}, bf16[4,128,128]{2,1,0:T(8,128)(2,1)S(1)}, u32[]{:S(2)}, u32[]{:S(2)}) %collective-permute-start.3) | collective-permute-done | bytes 131104 | tf_op jit(solution)/shard_map/ppermute | solution.py:244
  138.8 0.4 collective-permute-done.4.refs_1_
  139.2 1.5 collective-permute-done.5.refs_2_
  140.7 0.6 copy-done.7
  141.4 2.5 %collect.2 = bf16[8,384,128]{2,1,0:T(8,128)(2,1)} custom-call(s32[16]{0:T(128)} %reshape.46.lists_ref, bf16[8,128,128]{2,1,0:T(8,128)(2,1)} %get-tuple-element.22.dq_ref, f32[16,128,128]{2,1,0:T(8,128)} %get-tuple-element.23.own_ref, bf16[4,128,128]{2,1,0:T(8,128)(2,1)} %copy-done.3, bf16[4,128,128]{2,1,0:T(8,128)(2,1)} %copy-done.5, ...), custom_call_target="tpu_custom_call" | custom-call | bytes 4194304 | tf_op jit(solution)/shard_map/collect/pallas_call | solution.py:205
  143.9 25.4 %all_to_all.20.refs_0_ = bf16[8,384,128]{2,1,0:T(8,128)(2,1)} all-to-all(bf16[8,384,128]{2,1,0:T(8,128)(2,1)} %collect.2), channel_id=1, replica_groups=mesh['dom'=4,'head'=8] {'head'}, dimensions={0} | all-to-all | bytes 1572864 | tf_op jit(solution)/shard_map/all_to_all | solution.py:282
  169.3 3.6 %unpack.1 = (bf16[256,1024]{1,0:T(8,128)(2,1)}, bf16[256,1024]{1,0:T(8,128)(2,1)}, bf16[256,1024]{1,0:T(8,128)(2,1)}) custom-call(bf16[8,384,128]{2,1,0:T(8,128)(2,1)} %all_to_all.20.refs_0_, bf16[8,384,128]{2,1,0:T(8,128)(2,1)} %copy-done.2), custom_call_target="tpu_custom_call" | custom-call | bytes 4194304 | tf_op jit(solution)/shard_map/unpack/pallas_call | solution.py:232
  (34 shorter events, 0.1 us)
Async XLA Ops:
  3.7 32.9 %all-to-all-start.2 = ((bf16[8,512,128]{2,1,0:T(8,128)(2,1)}), bf16[8,512,128]{2,1,0:T(8,128)(2,1)S(1)}, u32[]{:S(2)}, u32[]{:S(2)}) async-start(bf16[8,512,128]{2,1,0:T(8,128)(2,1)} %pack.3), calls=%async_computation.2 | async-start | bytes 2097152 | tf_op jit(solution)/shard_map/all_to_all | solution.py:269
  36.6 3.6 %copy-start.1 = (bf16[8,512,128]{2,1,0:T(8,128)(2,1)}, bf16[8,512,128]{2,1,0:T(8,128)(2,1)S(1)}, u32[]{:S(2)}) copy-start(bf16[8,512,128]{2,1,0:T(8,128)(2,1)S(1)} %all-to-all-done.2) | copy-start | bytes 3145732
  36.6 54.3 %all-to-all-start = ((bf16[8,512,128]{2,1,0:T(8,128)(2,1)}), bf16[8,512,128]{2,1,0:T(8,128)(2,1)S(1)}, u32[]{:S(2)}, u32[]{:S(2)}) async-start(bf16[8,512,128]{2,1,0:T(8,128)(2,1)} %pack.2), calls=%async_computation | async-start | bytes 2097152 | tf_op jit(solution)/shard_map/all_to_all | solution.py:269
  40.2 1.5 copy-start.9
  42.4 5.6 %copy-start.10 = (s32[2048]{0:T(1024)S(1)}, s32[2048]{0:T(1024)}, u32[]{:S(2)}) copy-start(s32[2048]{0:T(1024)} %param.11) | copy-start | bytes 24580
  44.4 6.3 %collective-permute-start.6 = (bf16[4,128,128]{2,1,0:T(8,128)(2,1)}, bf16[4,128,128]{2,1,0:T(8,128)(2,1)S(1)}, u32[]{:S(2)}, u32[]{:S(2)}) collective-permute-start(bf16[4,128,128]{2,1,0:T(8,128)(2,1)} %get-tuple-element.27), channel_id=1, source_target_pairs={{0,8},{8,0},{16,24},{24,16},{1,9},{9,1},{17,25},{25,17},{2,10},{10... | collective-permute-start | bytes 393224 | tf_op jit(solution)/shard_map/ppermute | solution.py:244
  45.9 8.5 %collective-permute-start.7 = (bf16[4,128,128]{2,1,0:T(8,128)(2,1)}, bf16[4,128,128]{2,1,0:T(8,128)(2,1)S(1)}, u32[]{:S(2)}, u32[]{:S(2)}) collective-permute-start(bf16[4,128,128]{2,1,0:T(8,128)(2,1)} %get-tuple-element.28), channel_id=1, source_target_pairs={{0,16},{8,24},{16,0},{24,8},{1,17},{9,25},{17,1},{25,9},{2,18},{10... | collective-permute-start | bytes 393224 | tf_op jit(solution)/shard_map/ppermute | solution.py:244
  47.5 7.0 %collective-permute-start.8 = (bf16[4,128,128]{2,1,0:T(8,128)(2,1)}, bf16[4,128,128]{2,1,0:T(8,128)(2,1)S(1)}, u32[]{:S(2)}, u32[]{:S(2)}) collective-permute-start(bf16[4,128,128]{2,1,0:T(8,128)(2,1)} %get-tuple-element.29), channel_id=1, source_target_pairs={{0,24},{8,16},{16,8},{24,0},{1,25},{9,17},{17,9},{25,1},{2,26},{10... | collective-permute-start | bytes 393224 | tf_op jit(solution)/shard_map/ppermute | solution.py:244
  50.8 3.7 %copy-start.12 = (bf16[4,128,128]{2,1,0:T(8,128)(2,1)}, bf16[4,128,128]{2,1,0:T(8,128)(2,1)S(1)}, u32[]{:S(2)}) copy-start(bf16[4,128,128]{2,1,0:T(8,128)(2,1)S(1)} %collective-permute-done.6.refs_0_) | copy-start | bytes 393220
  54.4 0.7 copy-start.14
  55.1 0.7 copy-start.16
  79.1 6.6 %collective-permute-start.9 = (bf16[4,128,128]{2,1,0:T(8,128)(2,1)}, bf16[4,128,128]{2,1,0:T(8,128)(2,1)S(1)}, u32[]{:S(2)}, u32[]{:S(2)}) collective-permute-start(bf16[4,128,128]{2,1,0:T(8,128)(2,1)} %get-tuple-element.32), channel_id=1, source_target_pairs={{0,8},{8,0},{16,24},{24,16},{1,9},{9,1},{17,25},{25,17},{2,10},{10... | collective-permute-start | bytes 393224 | tf_op jit(solution)/shard_map/ppermute | solution.py:244
  79.8 6.9 %collective-permute-start.10 = (bf16[4,128,128]{2,1,0:T(8,128)(2,1)}, bf16[4,128,128]{2,1,0:T(8,128)(2,1)S(1)}, u32[]{:S(2)}, u32[]{:S(2)}) collective-permute-start(bf16[4,128,128]{2,1,0:T(8,128)(2,1)} %get-tuple-element.33), channel_id=1, source_target_pairs={{0,16},{8,24},{16,0},{24,8},{1,17},{9,25},{17,1},{25,9},{2,18},{10... | collective-permute-start | bytes 393224 | tf_op jit(solution)/shard_map/ppermute | solution.py:244
  81.3 6.6 %collective-permute-start.11 = (bf16[4,128,128]{2,1,0:T(8,128)(2,1)}, bf16[4,128,128]{2,1,0:T(8,128)(2,1)S(1)}, u32[]{:S(2)}, u32[]{:S(2)}) collective-permute-start(bf16[4,128,128]{2,1,0:T(8,128)(2,1)} %get-tuple-element.34), channel_id=1, source_target_pairs={{0,24},{8,16},{16,8},{24,0},{1,25},{9,17},{17,9},{25,1},{2,26},{10... | collective-permute-start | bytes 393224 | tf_op jit(solution)/shard_map/ppermute | solution.py:244
  85.7 2.1 %copy-start.4 = (bf16[4,128,128]{2,1,0:T(8,128)(2,1)}, bf16[4,128,128]{2,1,0:T(8,128)(2,1)S(1)}, u32[]{:S(2)}) copy-start(bf16[4,128,128]{2,1,0:T(8,128)(2,1)S(1)} %collective-permute-done.9.refs_0_) | copy-start | bytes 393220
  86.7 1.2 copy-start.6
  87.8 0.7 copy-start.8
  91.0 4.5 %copy-start = (bf16[8,512,128]{2,1,0:T(8,128)(2,1)}, bf16[8,512,128]{2,1,0:T(8,128)(2,1)S(1)}, u32[]{:S(2)}) copy-start(bf16[8,512,128]{2,1,0:T(8,128)(2,1)S(1)} %all-to-all-done) | copy-start | bytes 3145732
  91.0 52.9 %all-to-all-start.3 = ((bf16[8,384,128]{2,1,0:T(8,128)(2,1)}), bf16[8,384,128]{2,1,0:T(8,128)(2,1)S(1)}, u32[]{:S(2)}, u32[]{:S(2)}) async-start(bf16[8,384,128]{2,1,0:T(8,128)(2,1)} %collect.3), calls=%async_computation.3 | async-start | bytes 1572864 | tf_op jit(solution)/shard_map/all_to_all | solution.py:282
  97.5 6.4 %collective-permute-start = (bf16[4,128,128]{2,1,0:T(8,128)(2,1)}, bf16[4,128,128]{2,1,0:T(8,128)(2,1)S(1)}, u32[]{:S(2)}, u32[]{:S(2)}) collective-permute-start(bf16[4,128,128]{2,1,0:T(8,128)(2,1)} %get-tuple-element.19), channel_id=1, source_target_pairs={{0,8},{8,0},{16,24},{24,16},{1,9},{9,1},{17,25},{25,17},{2,10},{10... | collective-permute-start | bytes 393224 | tf_op jit(solution)/shard_map/ppermute | solution.py:244
  99.1 8.6 %collective-permute-start.1 = (bf16[4,128,128]{2,1,0:T(8,128)(2,1)}, bf16[4,128,128]{2,1,0:T(8,128)(2,1)S(1)}, u32[]{:S(2)}, u32[]{:S(2)}) collective-permute-start(bf16[4,128,128]{2,1,0:T(8,128)(2,1)} %get-tuple-element.20), channel_id=1, source_target_pairs={{0,16},{8,24},{16,0},{24,8},{1,17},{9,25},{17,1},{25,9},{2,18},{10... | collective-permute-start | bytes 393224 | tf_op jit(solution)/shard_map/ppermute | solution.py:244
  100.1 7.7 %collective-permute-start.2 = (bf16[4,128,128]{2,1,0:T(8,128)(2,1)}, bf16[4,128,128]{2,1,0:T(8,128)(2,1)S(1)}, u32[]{:S(2)}, u32[]{:S(2)}) collective-permute-start(bf16[4,128,128]{2,1,0:T(8,128)(2,1)} %get-tuple-element.21), channel_id=1, source_target_pairs={{0,24},{8,16},{16,8},{24,0},{1,25},{9,17},{17,9},{25,1},{2,26},{10... | collective-permute-start | bytes 393224 | tf_op jit(solution)/shard_map/ppermute | solution.py:244
  103.9 3.9 %copy-start.11 = (bf16[4,128,128]{2,1,0:T(8,128)(2,1)}, bf16[4,128,128]{2,1,0:T(8,128)(2,1)S(1)}, u32[]{:S(2)}) copy-start(bf16[4,128,128]{2,1,0:T(8,128)(2,1)S(1)} %collective-permute-done.refs_0_) | copy-start | bytes 393220
  107.8 0.7 copy-start.13
  108.4 0.7 copy-start.15
  132.5 6.3 %collective-permute-start.3 = (bf16[4,128,128]{2,1,0:T(8,128)(2,1)}, bf16[4,128,128]{2,1,0:T(8,128)(2,1)S(1)}, u32[]{:S(2)}, u32[]{:S(2)}) collective-permute-start(bf16[4,128,128]{2,1,0:T(8,128)(2,1)} %get-tuple-element.24), channel_id=1, source_target_pairs={{0,8},{8,0},{16,24},{24,16},{1,9},{9,1},{17,25},{25,17},{2,10},{10... | collective-permute-start | bytes 393224 | tf_op jit(solution)/shard_map/ppermute | solution.py:244
  132.5 6.6 %collective-permute-start.4 = (bf16[4,128,128]{2,1,0:T(8,128)(2,1)}, bf16[4,128,128]{2,1,0:T(8,128)(2,1)S(1)}, u32[]{:S(2)}, u32[]{:S(2)}) collective-permute-start(bf16[4,128,128]{2,1,0:T(8,128)(2,1)} %get-tuple-element.25), channel_id=1, source_target_pairs={{0,16},{8,24},{16,0},{24,8},{1,17},{9,25},{17,1},{25,9},{2,18},{10... | collective-permute-start | bytes 393224 | tf_op jit(solution)/shard_map/ppermute | solution.py:244
  133.6 7.1 %collective-permute-start.5 = (bf16[4,128,128]{2,1,0:T(8,128)(2,1)}, bf16[4,128,128]{2,1,0:T(8,128)(2,1)S(1)}, u32[]{:S(2)}, u32[]{:S(2)}) collective-permute-start(bf16[4,128,128]{2,1,0:T(8,128)(2,1)} %get-tuple-element.26), channel_id=1, source_target_pairs={{0,24},{8,16},{16,8},{24,0},{1,25},{9,17},{17,9},{25,1},{2,26},{10... | collective-permute-start | bytes 393224 | tf_op jit(solution)/shard_map/ppermute | solution.py:244
  138.8 1.9 %copy-start.3 = (bf16[4,128,128]{2,1,0:T(8,128)(2,1)}, bf16[4,128,128]{2,1,0:T(8,128)(2,1)S(1)}, u32[]{:S(2)}) copy-start(bf16[4,128,128]{2,1,0:T(8,128)(2,1)S(1)} %collective-permute-done.3.refs_0_) | copy-start | bytes 393220
  139.2 1.5 copy-start.5
  140.7 0.6 copy-start.7
  143.9 25.4 %copy-start.2 = (bf16[8,384,128]{2,1,0:T(8,128)(2,1)}, bf16[8,384,128]{2,1,0:T(8,128)(2,1)S(1)}, u32[]{:S(2)}) copy-start(bf16[8,384,128]{2,1,0:T(8,128)(2,1)S(1)} %all-to-all-done.3.refs_1_) | copy-start | bytes 2359300

commit v2 on v1

v2 whole, which is shorter than its diff:
```python
import functools
import math

import jax
import jax.numpy as jnp
from jax import lax
from jax.experimental import pallas as pl
from jax.experimental.pallas import tpu as pltpu
from jax.sharding import PartitionSpec as P

D = 1024
H = 16
NBR = 12
BS = 128
HD = D // H
LOG2E = 1.4426950408889634
VMEM_LIMIT = 56 << 20

bf16 = jnp.bfloat16
f32 = jnp.float32


def params():
    return pltpu.CompilerParams(vmem_limit_bytes=VMEM_LIMIT)


def cost(flops, bytes_accessed):
    return pl.CostEstimate(flops=flops, bytes_accessed=bytes_accessed, transcendentals=0)


VMEM = pl.BlockSpec(memory_space=pltpu.VMEM)
SMEM = pl.BlockSpec(memory_space=pltpu.SMEM)
ANY = pl.BlockSpec(memory_space=pl.ANY)


def pack_kernel(first, count, n, x_ref, y_ref, out_ref):
    rows = x_ref.shape[0]
    for f in range(count):
        at = pl.ds(f * rows, rows)
        for j in range(n):
            cols = pl.ds(((first + f) * n + j) * HD, HD)
            out_ref[j, at, pl.ds(0, HD)] = x_ref[:, cols]
            out_ref[j, at, pl.ds(HD, HD)] = y_ref[:, cols]


def pack(x, y, first, count, n):
    rows = x.shape[0]
    return pl.pallas_call(
        functools.partial(pack_kernel, first, count, n),
        out_shape=jax.ShapeDtypeStruct((n, count * rows, 2 * HD), bf16),
        in_specs=[VMEM] * 2,
        out_specs=VMEM,
        compiler_params=params(),
        cost_estimate=cost(0, 8 * rows * D),
        name="pack",
    )(x, y)


def lend_kernel(phases, parts, cap, bpd, lists_ref, kv_ref, *outs):
    for k in range(1, parts):
        for s in range(cap):
            b = lists_ref[k * cap + s]
            j, o = lax.div(b, bpd), lax.rem(b, bpd)
            for f in range(phases):
                outs[k - 1][f * cap + s] = kv_ref[j, f * bpd + o]


def lend(lists, kv, phases, parts, cap, bpd):
    return pl.pallas_call(
        functools.partial(lend_kernel, phases, parts, cap, bpd),
        out_shape=[jax.ShapeDtypeStruct((phases * cap, BS, 2 * HD), bf16)] * (parts - 1),
        in_specs=[SMEM, VMEM],
        out_specs=[VMEM] * (parts - 1),
        compiler_params=params(),
        cost_estimate=cost(0, 4 * parts * cap * BS * 4 * HD),
        name="lend",
    )(lists, kv)


def attend_kernel(f, parts, cap, n, bpd, idx_ref, kv_ref, qg_ref, tau_ref, *refs):
    borrowed, refs = refs[: parts - 1], refs[parts - 1 :]
    earlier, refs = (refs[: parts - 1], refs[parts - 1 :]) if f else ((), refs)
    dq_ref, own_ref = refs[:2]
    back = refs[2 : parts + 1]
    tab, kt_tab, acc, s_buf, dp_buf, sem = refs[parts + 1 :]
    nblk = n * bpd
    slots = (parts - 1) * cap
    copies = [
        pltpu.make_async_copy(kv_ref.at[j, pl.ds(f * bpd, bpd)], tab.at[pl.ds(j * bpd, bpd)], sem.at[j])
        for j in range(n)
    ]
    for k in range(1, parts):
        copies.append(
            pltpu.make_async_copy(borrowed[k - 1].at[pl.ds(f * cap, cap)], tab.at[pl.ds(nblk + (k - 1) * cap, cap)], sem.at[n + k])
        )
    for c in copies:
        c.start()
    acc[...] = jnp.zeros_like(acc)
    for c in copies:
        c.wait()

    def flip(t, _):
        kt_tab[t] = tab[t].astype(f32).T[:HD].astype(bf16)
        return 0

    lax.fori_loop(0, nblk + slots, flip, 0, unroll=4)
    lane = lax.broadcasted_iota(jnp.int32, (BS, 2 * HD), 1)
    low = lane < HD
    zero = jnp.zeros((BS, 2 * HD), bf16)

    def fold8(x, op):
        return op(x.reshape(BS // 8, 8, BS), axis=0)

    def load(r):
        qg = qg_ref[lax.div(r, bpd), lax.rem(r, bpd)]
        both = jnp.concatenate([jnp.where(low, qg, zero), jnp.where(low, zero, qg)], 0)
        return both, [idx_ref[r * NBR + i] for i in range(NBR)]

    def step1(slot, both, where, i, top):
        rr = lax.dot_general(tab[where[i]], both, (((1,), (1,)), ((), ())), preferred_element_type=f32)
        s = rr[:, :BS]
        s_buf[slot, i] = s
        dp_buf[slot, i] = rr[:, BS:]
        m8 = fold8(s, jnp.max)
        return m8 if top is None else jnp.maximum(top, m8)

    def advance(r, slot, top, r2):
        both, where = load(r)
        both2, where2 = load(r2)
        m = jnp.max(top, axis=0, keepdims=True)
        tau = tau_ref[pl.ds(r, 1), :]
        c = tau * LOG2E
        top2 = None
        total = weighted = None
        nxt = 0
        for i in range(NBR):
            if i % 2 == 0:
                top2 = step1(1 - slot, both2, where2, nxt, top2); nxt += 1
            ex = jnp.exp2((s_buf[slot, i] - m) * c)
            s_buf[slot, i] = ex
            l8 = fold8(ex, jnp.sum)
            d8 = fold8(ex * dp_buf[slot, i], jnp.sum)
            total = l8 if total is None else total + l8
            weighted = d8 if weighted is None else weighted + d8
        norm = jnp.sum(total, axis=0, keepdims=True)
        inv = 1.0 / norm
        delta = jnp.sum(weighted, axis=0, keepdims=True) * inv
        dq = None
        for i in range(0, NBR, 2):
            us = []
            top2 = step1(1 - slot, both2, where2, nxt, top2); nxt += 1
            for j in (i, i + 1):
                p = s_buf[slot, j] * inv
                u = (p * (dp_buf[slot, j] - delta) * tau).astype(bf16)
                us.append(u)
                part = jnp.dot(jnp.concatenate([u, p.astype(bf16)], 1), both, preferred_element_type=f32)
                acc[where[j]] += part
            kt = jnp.concatenate([kt_tab[where[i]], kt_tab[where[i + 1]]], 1)
            d = jnp.dot(kt, jnp.concatenate(us, 0), preferred_element_type=f32)
            dq = d if dq is None else dq + d
        return dq, top2

    def pair(g, top):
        r = g * bpd
        dqs = []
        for rb in range(bpd):
            dq, top = advance(r + rb, rb % 2, top, jnp.minimum(r + rb + 1, nblk - 1))
            dqs.append(dq)
        dq_ref[g] = jnp.concatenate(dqs, 0).T.astype(bf16)
        return top
    both, where = load(0)
    top = None
    for i in range(NBR):
        top = step1(0, both, where, i, top)
    lax.fori_loop(0, n, pair, top)
    own_ref[...] = acc[pl.ds(0, nblk)]
    for k in range(1, parts):
        if f:
            back[k - 1][pl.ds(0, f * cap)] = earlier[k - 1][...]
        back[k - 1][pl.ds(f * cap, cap)] = acc[pl.ds(nblk + (k - 1) * cap, cap)].astype(bf16)


def attend(idx, kv, f, qg, tau, borrowed, earlier, parts, cap, n, bpd):
    nblk = n * bpd
    slots = (parts - 1) * cap
    width = 2 * HD
    return pl.pallas_call(
        functools.partial(attend_kernel, f, parts, cap, n, bpd),
        out_shape=[
            jax.ShapeDtypeStruct((n, BS, width), bf16),
            jax.ShapeDtypeStruct((nblk, BS, width), f32),
        ]
        + [jax.ShapeDtypeStruct(((f + 1) * cap, BS, width), bf16)] * (parts - 1),
        in_specs=[SMEM, VMEM, VMEM, VMEM] + [VMEM] * (len(borrowed) + len(earlier)),
        out_specs=[VMEM] * (parts + 1),
        scratch_shapes=[
            pltpu.VMEM((nblk + slots, BS, width), bf16),
            pltpu.VMEM((nblk + slots, HD, BS), bf16),
            pltpu.VMEM((nblk + slots, BS, width), f32),
            pltpu.VMEM((bpd, NBR, BS, BS), f32),
            pltpu.VMEM((bpd, NBR, BS, BS), f32),
            pltpu.SemaphoreType.DMA((n + parts,)),
        ],
        compiler_params=params(),
        cost_estimate=cost(nblk * NBR * BS * BS * HD * 100, 6 << 20),
        name="attend",
    )(idx, kv, qg, tau, *borrowed, *earlier)


def collect_kernel(phases, parts, cap, bpd, lists_ref, *refs):
    own, returned = refs[:phases], refs[phases : phases + parts - 1]
    out_ref, total = refs[phases + parts - 1 :]
    nblk = total.shape[0]
    for f in range(phases):
        total[...] = own[f][...]
        for k in range(1, parts):
            for s in range(cap):
                total[lists_ref[k * cap + s]] += returned[k - 1][f * cap + s].astype(f32)
        for b in range(nblk):
            out_ref[b // bpd, pl.ds((f * bpd + b % bpd) * BS, BS)] = total[b].astype(bf16)


def collect(lists, own, returned, phases, parts, cap, n, bpd):
    return pl.pallas_call(
        functools.partial(collect_kernel, phases, parts, cap, bpd),
        out_shape=jax.ShapeDtypeStruct((n, phases * bpd * BS, 2 * HD), bf16),
        in_specs=[SMEM] + [VMEM] * (phases + parts - 1),
        out_specs=VMEM,
        scratch_shapes=[pltpu.VMEM(own[0].shape, f32)],
        compiler_params=params(),
        cost_estimate=cost(0, 4 << 20),
        name="collect",
    )(lists, *own, *returned)


def unpack_kernel(n, phases, bpd, *refs):
    dqs, dkv = refs[:phases], refs[phases]
    gq, gk, gv = refs[phases + 1 :]
    rows = bpd * BS
    for f in range(phases):
        for j in range(n):
            cols = pl.ds((f * n + j) * HD, HD)
            for b in range(bpd):
                gq[pl.ds(b * BS, BS), cols] = dqs[f][j, :, pl.ds(b * HD, HD)]
            gk[:, cols] = dkv[j, pl.ds(f * rows, rows), pl.ds(0, HD)]
            gv[:, cols] = dkv[j, pl.ds(f * rows, rows), pl.ds(HD, HD)]


def unpack(dqs, dkv, n, bpd):
    rows = bpd * BS
    return pl.pallas_call(
        functools.partial(unpack_kernel, n, len(dqs), bpd),
        out_shape=[jax.ShapeDtypeStruct((rows, D), bf16)] * 3,
        in_specs=[VMEM] * (len(dqs) + 1),
        out_specs=[VMEM] * 3,
        compiler_params=params(),
        cost_estimate=cost(0, 4 << 20),
        name="unpack",
    )(*dqs, dkv)


def swap(x, k, parts):
    return lax.ppermute(x, "dom", [(i, i ^ k) for i in range(parts)])


def body(node_queries, node_keys, node_values, out_grad, degrees, neighbor_blocks, send_slots):
    n = lax.axis_size("head")
    parts = lax.axis_size("dom")
    cap = send_slots.shape[2]
    phases = H // n
    rows = node_queries.shape[0]
    bpd = rows // BS
    nblk = n * bpd
    me = lax.axis_index("dom")
    hop = jnp.arange(parts, dtype=jnp.int32)
    mine = jnp.maximum(lax.dynamic_index_in_dim(send_slots, me, 0, keepdims=False), 0)
    pick = (hop[:, None] == (hop[None, :] ^ me)).astype(jnp.int32)
    lists = jnp.sum(pick[:, :, None] * mine[None], axis=1).reshape(-1)
    away = neighbor_blocks - nblk
    moved = nblk + ((away // cap) ^ me) * cap + away % cap - cap
    idx = jnp.where(away < 0, neighbor_blocks, moved).reshape(-1)
    tau = (jnp.log(degrees.astype(f32)) / math.log(64.0) / math.sqrt(HD)).reshape(nblk, BS)

    def spread(x):
        return lax.all_to_all(x, "head", split_axis=0, concat_axis=0, tiled=True)

    kv = spread(pack(node_keys, node_values, 0, phases, n)).reshape(n, phases * bpd, BS, 2 * HD)
    sent = [pack(node_queries, out_grad, f, 1, n) for f in range(phases)]
    sent[0], kv = lax.optimization_barrier((sent[0], kv))
    qg = [spread(sent[0])]
    lent = lend(lists, kv, phases, parts, cap, bpd)
    borrowed = [swap(lent[k - 1], k, parts) for k in range(1, parts)]
    for f in range(1, phases):
        sent[f], qg[f - 1], borrowed = lax.optimization_barrier((sent[f], qg[f - 1], borrowed))
        qg.append(spread(sent[f]))
    dqs, owns, back = [], [], []
    for f in range(phases):
        block = qg[f].reshape(n, bpd, BS, 2 * HD)
        dq, own, *back = attend(idx, kv, f, block, tau, borrowed, back, parts, cap, n, bpd)
        if f + 1 < phases:
            dq, qg[f + 1] = lax.optimization_barrier((dq, qg[f + 1]))
        if f:
            dq, dqs[f - 1] = lax.optimization_barrier((dq, dqs[f - 1]))
        dqs.append(spread(dq))
        owns.append(own)
    returned = [swap(back[k - 1], k, parts) for k in range(1, parts)]
    total = collect(lists, owns, returned, phases, parts, cap, n, bpd)
    total, dqs = lax.optimization_barrier((total, dqs))
    return tuple(unpack(dqs, spread(total), n, bpd))


def solution(mesh):
    placed = (
        P(("dom", "head"), None),
        P(("dom", "head"), None),
        P(("dom", "head"), None),
        P(("dom", "head"), None),
        P("dom"),
        P("dom", None),
        P(),
    )
    return jax.shard_map(
        body,
        mesh=mesh,
        in_specs=placed,
        out_specs=(P(("dom", "head"), None), P(("dom", "head"), None), P(("dom", "head"), None)),
        check_vma=False,
    )
```

time: 174 us -> 167 us (0.960)
  Pallas kernels: 65.5 us -> 52.1 us
  blocking collectives: 25.4 us -> 31.4 us
  starting transfers between devices: 28.5 us -> 31.8 us
    pallas_call x9 -> x8, Pallas kernels: 65.5 us -> 52.1 us  [the longest x2 35.7 us: attend(): pl.pallas_call(functools.partial(attend_kernel, f, parts, cap, n, bpd), o...]
    all_to_all x3 -> x5, starting transfers between devices: 14.4 us -> 24.8 us  [spread(): return lax.all_to_all(x, 'head', split_axis=0, concat_axis=0, tiled=True)]
    ppermute x12 -> x6, starting transfers between devices: 14.1 us -> 7 us  [swap(): return lax.ppermute(x, 'dom', [(i, i ^ k) for i in range(parts)])]
    all_to_all x1, blocking collectives: 25.4 us -> 31.4 us  [spread(): return lax.all_to_all(x, 'head', split_axis=0, concat_axis=0, tiled=True)]
    ppermute x12 -> x6, waiting for transfers between devices: 22.4 us -> 20.4 us  [swap(): return lax.ppermute(x, 'dom', [(i, i ^ k) for i in range(parts)])]
    unnamed x34 -> x30, local copies, waits for them, and re-layouts: 3.93 us -> 2.29 us
    all_to_all x3 -> x5, waiting for transfers between devices: 23.5 us -> 24.3 us  [spread(): return lax.all_to_all(x, 'head', split_axis=0, concat_axis=0, tiled=True)]
  transfers between devices with their start and end apart: 15 -> 11, of which waited for: 11 -> 6; matrix products, arithmetic and copies ran while one was open for 2% -> 2% of each run, Pallas kernels for 34% -> 28%
where the time goes in v2:
time: 167 us; the launch traced here: 166 us
  Pallas kernels  52.1 us (31%)
  waiting for transfers between devices  44.7 us (27%)
  starting transfers between devices  31.8 us (19%)
  blocking collectives  31.4 us (19%)
  local copies, waits for them, and re-layouts  3.64 us (2%)
    pallas_call x2, Pallas kernels, attend(): pl.pallas_call(functools.partial(attend_kernel, f, parts, cap, n, bpd), o...  35.7 us
    all_to_all x1, blocking collectives, spread(): return lax.all_to_all(x, 'head', split_axis=0, concat_axis=0, tiled=True)  31.4 us
    all_to_all x5, starting transfers between devices, spread(): return lax.all_to_all(x, 'head', split_axis=0, concat_axis=0, tiled=True)  24.8 us
    all_to_all x5, waiting for transfers between devices, spread(): return lax.all_to_all(x, 'head', split_axis=0, concat_axis=0, tiled=True)  24.3 us
    ppermute x6, waiting for transfers between devices, swap(): return lax.ppermute(x, 'dom', [(i, i ^ k) for i in range(parts)])  20.4 us
    pallas_call x3, Pallas kernels, pack(): pl.pallas_call(functools.partial(pack_kernel, first, count, n), out_shape...  7.48 us
    ppermute x6, starting transfers between devices, swap(): return lax.ppermute(x, 'dom', [(i, i ^ k) for i in range(parts)])  7 us
    pallas_call x1, Pallas kernels, unpack(): pl.pallas_call(functools.partial(unpack_kernel, n, len(dqs), bpd), out_sh...  3.57 us
  transfers between devices with their start and end apart: 11, of which 6 were waited for; matrix products, arithmetic and copies ran while one was open for 2% of the time, Pallas kernels for 28%

profile of v2, /device:TPU:0, one launch (start us, length us, event | category | flops | bytes accessed | tf_op | source)
XLA Modules:
  0.0 165.8 jit_solution(2580112866365450587)
XLA Ops:
  0.6 2.8 %pack.4 = bf16[8,512,128]{2,1,0:T(8,128)(2,1)} custom-call(bf16[256,1024]{1,0:T(8,128)(2,1)} %x_ref.4, bf16[256,1024]{1,0:T(8,128)(2,1)} %y_ref.4), custom_call_target="tpu_custom_call" | custom-call | bytes 2097152 | tf_op jit(solution)/shard_map/pack/pallas_call | solution.py:48
  3.4 6.3 %all-to-all-start = ((bf16[8,512,128]{2,1,0:T(8,128)(2,1)}), bf16[8,512,128]{2,1,0:T(8,128)(2,1)S(1)}, u32[]{:S(2)}, u32[]{:S(2)}) async-start(bf16[8,512,128]{2,1,0:T(8,128)(2,1)} %pack.4), calls=%async_computation | async-start | bytes 2097152 | tf_op jit(solution)/shard_map/all_to_all | solution.py:285
  9.8 2.3 %pack.3 = bf16[8,256,128]{2,1,0:T(8,128)(2,1)} custom-call(bf16[256,1024]{1,0:T(8,128)(2,1)} %x_ref.5, bf16[256,1024]{1,0:T(8,128)(2,1)} %y_ref.5), custom_call_target="tpu_custom_call" | custom-call | bytes 2097152 | tf_op jit(solution)/shard_map/pack/pallas_call | solution.py:48
  12.1 24.3 %all-to-all-done = bf16[8,512,128]{2,1,0:T(8,128)(2,1)S(1)} async-done(((bf16[8,512,128]{2,1,0:T(8,128)(2,1)}), bf16[8,512,128]{2,1,0:T(8,128)(2,1)S(1)}, u32[]{:S(2)}, u32[]{:S(2)}) %all-to-all-start) | async-done | bytes 1048608 | tf_op jit(solution)/shard_map/all_to_all | solution.py:285
  36.4 3.5 %all-to-all-start.1 = ((bf16[8,256,128]{2,1,0:T(8,128)(2,1)}), bf16[8,256,128]{2,1,0:T(8,128)(2,1)S(1)}, u32[]{:S(2)}, u32[]{:S(2)}) async-start(bf16[8,256,128]{2,1,0:T(8,128)(2,1)} %pack.3), calls=%async_computation.1 | async-start | bytes 1048576 | tf_op jit(solution)/shard_map/all_to_all | solution.py:285
  39.9 0.7 maximum_bitcast_fusion
  40.6 0.1 multiply_reduce_fusion
  40.7 0.7 reshape.49.lists_ref
  41.3 0.0 copy-done
  41.3 2.2 %lend.1 = (bf16[8,128,128]{2,1,0:T(8,128)(2,1)}, bf16[8,128,128]{2,1,0:T(8,128)(2,1)}, bf16[8,128,128]{2,1,0:T(8,128)(2,1)}) custom-call(s32[16]{0:T(128)} %reshape.49.lists_ref, bf16[8,4,128,128]{3,2,1,0:T(8,128)(2,1)} %bitcast.7), custom_call_target="tpu_custom_call" | custom-call | bytes 2097152 | tf_op jit(solution)/shard_map/lend/pallas_call | solution.py:69
  43.5 1.5 collective-permute-start
  45.0 1.5 collective-permute-start.1
  46.5 0.5 collective-permute-start.2
  47.0 0.0 copy-done.8
  47.1 2.3 %pack.5 = bf16[8,256,128]{2,1,0:T(8,128)(2,1)} custom-call(bf16[256,1024]{1,0:T(8,128)(2,1)} %x_ref.5, bf16[256,1024]{1,0:T(8,128)(2,1)} %y_ref.5), custom_call_target="tpu_custom_call" | custom-call | bytes 2097152 | tf_op jit(solution)/shard_map/pack/pallas_call | solution.py:48
  49.4 0.7 reshape.50.idx_ref
  50.1 0.0 copy-done.9
  50.1 0.6 multiply_bitcast_fusion.tau_ref
  50.7 2.2 %collective-permute-done.refs_0_ = bf16[8,128,128]{2,1,0:T(8,128)(2,1)S(1)} collective-permute-done((bf16[8,128,128]{2,1,0:T(8,128)(2,1)}, bf16[8,128,128]{2,1,0:T(8,128)(2,1)S(1)}, u32[]{:S(2)}, u32[]{:S(2)}) %collective-permute-start) | collective-permute-done | bytes 262176 | tf_op jit(solution)/shard_map/ppermute | solution.py:263
  52.9 6.3 %collective-permute-done.1.refs_1_ = bf16[8,128,128]{2,1,0:T(8,128)(2,1)S(1)} collective-permute-done((bf16[8,128,128]{2,1,0:T(8,128)(2,1)}, bf16[8,128,128]{2,1,0:T(8,128)(2,1)S(1)}, u32[]{:S(2)}, u32[]{:S(2)}) %collective-permute-start.1) | collective-permute-done | bytes 262176 | tf_op jit(solution)/shard_map/ppermute | solution.py:263
  59.2 0.0 collective-permute-done.2.refs_2_
  59.2 0.0 all-to-all-done.1
  59.2 0.0 copy-start.3
  59.2 0.0 copy-done.10
  59.2 0.9 copy-done.11
  60.0 4.8 %all-to-all-start.2 = ((bf16[8,256,128]{2,1,0:T(8,128)(2,1)}), bf16[8,256,128]{2,1,0:T(8,128)(2,1)S(1)}, u32[]{:S(2)}, u32[]{:S(2)}) async-start(bf16[8,256,128]{2,1,0:T(8,128)(2,1)} %pack.5), calls=%async_computation.2 | async-start | bytes 1048576 | tf_op jit(solution)/shard_map/all_to_all | solution.py:285
  64.8 0.0 copy-done.12
  64.8 17.7 %attend.2 = (bf16[8,128,128]{2,1,0:T(8,128)(2,1)}, f32[16,128,128]{2,1,0:T(8,128)}, bf16[4,128,128]{2,1,0:T(8,128)(2,1)}, bf16[4,128,128]{2,1,0:T(8,128)(2,1)}, bf16[4,128,128]{2,1,0:T(8,128)(2,1)}) custom-call(s32[192]{0:T(256)} %reshape.50.idx_ref, bf16[8,4,128,128]{3,2,1,0:T(8,128)(2,1)} %bitcast.8, bf16[8,2,128,128]{3,2,1,0:T(8,128)(2,1)} %bitcast.10, ...), custom_call_target="tpu_custom_call" | custom-call | flops 20132659200 | bytes 6291456 | tf_op jit(solution)/shard_map/attend/pallas_call | solution.py:187
  82.5 0.0 all-to-all-done.2
  82.5 0.0 copy-start.4
  82.6 5.1 %all-to-all-start.3 = ((bf16[8,128,128]{2,1,0:T(8,128)(2,1)}), bf16[8,128,128]{2,1,0:T(8,128)(2,1)S(1)}, u32[]{:S(2)}, u32[]{:S(2)}) async-start(bf16[8,128,128]{2,1,0:T(8,128)(2,1)} %get-tuple-element.51), calls=%async_computation.3 | async-start | bytes 524288 | tf_op jit(solution)/shard_map/all_to_all | solution.py:285
  87.7 18.0 %attend.3 = (bf16[8,128,128]{2,1,0:T(8,128)(2,1)}, f32[16,128,128]{2,1,0:T(8,128)}, bf16[8,128,128]{2,1,0:T(8,128)(2,1)}, bf16[8,128,128]{2,1,0:T(8,128)(2,1)}, bf16[8,128,128]{2,1,0:T(8,128)(2,1)}) custom-call(s32[192]{0:T(256)} %reshape.50.idx_ref, bf16[8,4,128,128]{3,2,1,0:T(8,128)(2,1)} %bitcast.9, bf16[8,2,128,128]{3,2,1,0:T(8,128)(2,1)} %bitcast.11, ...), custom_call_target="tpu_custom_call" | custom-call | flops 20132659200 | bytes 6291456 | tf_op jit(solution)/shard_map/attend/pallas_call | solution.py:187
  105.6 0.0 all-to-all-done.3.refs_0_
  105.7 0.7 copy-done.1
  106.4 5.1 %all-to-all-start.4 = ((bf16[8,128,128]{2,1,0:T(8,128)(2,1)}), bf16[8,128,128]{2,1,0:T(8,128)(2,1)S(1)}, u32[]{:S(2)}, u32[]{:S(2)}) async-start(bf16[8,128,128]{2,1,0:T(8,128)(2,1)} %get-tuple-element.53), calls=%async_computation.4 | async-start | bytes 524288 | tf_op jit(solution)/shard_map/all_to_all | solution.py:285
  111.5 1.2 collective-permute-start.3
  112.6 0.9 collective-permute-start.4
  113.5 0.0 copy-done.13
  113.5 1.4 collective-permute-start.5
  115.0 5.8 %collective-permute-done.3.refs_2_ = bf16[8,128,128]{2,1,0:T(8,128)(2,1)S(1)} collective-permute-done((bf16[8,128,128]{2,1,0:T(8,128)(2,1)}, bf16[8,128,128]{2,1,0:T(8,128)(2,1)S(1)}, u32[]{:S(2)}, u32[]{:S(2)}) %collective-permute-start.3) | collective-permute-done | bytes 262176 | tf_op jit(solution)/shard_map/ppermute | solution.py:263
  120.8 0.4 collective-permute-done.4.refs_3_
  121.2 5.8 %collective-permute-done.5.refs_4_ = bf16[8,128,128]{2,1,0:T(8,128)(2,1)S(1)} collective-permute-done((bf16[8,128,128]{2,1,0:T(8,128)(2,1)S(1)}, bf16[8,128,128]{2,1,0:T(8,128)(2,1)S(1)}, u32[]{:S(2)}, u32[]{:S(2)}) %collective-permute-start.5) | collective-permute-done | bytes 262176 | tf_op jit(solution)/shard_map/ppermute | solution.py:263
  127.0 0.0 copy-done.6
  127.0 0.7 copy-done.7
  127.7 3.2 %collect.1 = bf16[8,512,128]{2,1,0:T(8,128)(2,1)} custom-call(s32[16]{0:T(128)} %reshape.49.lists_ref, f32[16,128,128]{2,1,0:T(8,128)} %get-tuple-element.39.refs_0_, f32[16,128,128]{2,1,0:T(8,128)} %get-tuple-element.46.refs_1_, bf16[8,128,128]{2,1,0:T(8,128)(2,1)} %copy-done.5, bf16[8,128,128]{2,1,0:T(8,128)(2,1)} %copy-done.6, bf16[8,128,128]{2,1,0:T(8,128)(2,1)} %copy-done.7), custom_call_target="tpu_custom_call" | custom-call | bytes 4194304 | tf_op jit(solution)/shard_map/collect/pallas_call | solution.py:224
  130.8 0.0 all-to-all-done.4.refs_1_
  130.8 31.4 %all_to_all.30.refs_2_ = bf16[8,512,128]{2,1,0:T(8,128)(2,1)} all-to-all(bf16[8,512,128]{2,1,0:T(8,128)(2,1)} %collect.1), channel_id=1, replica_groups=mesh['dom'=4,'head'=8] {'head'}, dimensions={0} | all-to-all | bytes 2097152 | tf_op jit(solution)/shard_map/all_to_all | solution.py:285
  162.3 3.6 %unpack.1 = (bf16[256,1024]{1,0:T(8,128)(2,1)}, bf16[256,1024]{1,0:T(8,128)(2,1)}, bf16[256,1024]{1,0:T(8,128)(2,1)}) custom-call(bf16[8,128,128]{2,1,0:T(8,128)(2,1)} %copy-done.1, bf16[8,128,128]{2,1,0:T(8,128)(2,1)} %copy-done.2, bf16[8,512,128]{2,1,0:T(8,128)(2,1)} %all_to_all.30.refs_2_), custom_call_target="tpu_custom_call" | custom-call | bytes 4194304 | tf_op jit(solution)/shard_map/unpack/pallas_call | solution.py:251
  (21 shorter events, 0.1 us)
Async XLA Ops:
  3.4 32.9 %all-to-all-start = ((bf16[8,512,128]{2,1,0:T(8,128)(2,1)}), bf16[8,512,128]{2,1,0:T(8,128)(2,1)S(1)}, u32[]{:S(2)}, u32[]{:S(2)}) async-start(bf16[8,512,128]{2,1,0:T(8,128)(2,1)} %pack.4), calls=%async_computation | async-start | bytes 2097152 | tf_op jit(solution)/shard_map/all_to_all | solution.py:285
  36.4 5.0 %copy-start = (bf16[8,512,128]{2,1,0:T(8,128)(2,1)}, bf16[8,512,128]{2,1,0:T(8,128)(2,1)S(1)}, u32[]{:S(2)}) copy-start(bf16[8,512,128]{2,1,0:T(8,128)(2,1)S(1)} %all-to-all-done) | copy-start | bytes 3145732
  36.4 22.8 %all-to-all-start.1 = ((bf16[8,256,128]{2,1,0:T(8,128)(2,1)}), bf16[8,256,128]{2,1,0:T(8,128)(2,1)S(1)}, u32[]{:S(2)}, u32[]{:S(2)}) async-start(bf16[8,256,128]{2,1,0:T(8,128)(2,1)} %pack.3), calls=%async_computation.1 | async-start | bytes 1048576 | tf_op jit(solution)/shard_map/all_to_all | solution.py:285
  41.3 5.7 %copy-start.8 = (s32[16,12]{1,0:T(8,128)S(1)}, s32[16,12]{1,0:T(8,128)}, u32[]{:S(2)}) copy-start(s32[16,12]{1,0:T(8,128)} %param.12) | copy-start | bytes 2308
  43.5 9.4 %collective-permute-start = (bf16[8,128,128]{2,1,0:T(8,128)(2,1)}, bf16[8,128,128]{2,1,0:T(8,128)(2,1)S(1)}, u32[]{:S(2)}, u32[]{:S(2)}) collective-permute-start(bf16[8,128,128]{2,1,0:T(8,128)(2,1)} %get-tuple-element.32), channel_id=1, source_target_pairs={{0,8},{8,0},{16,24},{24,16},{1,9},{9,1},{17,25},{25,17},{2,10},{10... | collective-permute-start | bytes 786440 | tf_op jit(solution)/shard_map/ppermute | solution.py:263
  45.0 14.1 %collective-permute-start.1 = (bf16[8,128,128]{2,1,0:T(8,128)(2,1)}, bf16[8,128,128]{2,1,0:T(8,128)(2,1)S(1)}, u32[]{:S(2)}, u32[]{:S(2)}) collective-permute-start(bf16[8,128,128]{2,1,0:T(8,128)(2,1)} %get-tuple-element.33), channel_id=1, source_target_pairs={{0,16},{8,24},{16,0},{24,8},{1,17},{9,25},{17,1},{25,9},{2,18},{10... | collective-permute-start | bytes 786440 | tf_op jit(solution)/shard_map/ppermute | solution.py:263
  46.5 12.6 %collective-permute-start.2 = (bf16[8,128,128]{2,1,0:T(8,128)(2,1)}, bf16[8,128,128]{2,1,0:T(8,128)(2,1)S(1)}, u32[]{:S(2)}, u32[]{:S(2)}) collective-permute-start(bf16[8,128,128]{2,1,0:T(8,128)(2,1)} %get-tuple-element.34), channel_id=1, source_target_pairs={{0,24},{8,16},{16,8},{24,0},{1,25},{9,17},{17,9},{25,1},{2,26},{10... | collective-permute-start | bytes 786440 | tf_op jit(solution)/shard_map/ppermute | solution.py:263
  49.4 0.7 copy-start.9
  52.9 6.3 %copy-start.10 = (bf16[8,128,128]{2,1,0:T(8,128)(2,1)}, bf16[8,128,128]{2,1,0:T(8,128)(2,1)S(1)}, u32[]{:S(2)}) copy-start(bf16[8,128,128]{2,1,0:T(8,128)(2,1)S(1)} %collective-permute-done.refs_0_) | copy-start | bytes 786436
  59.2 0.9 copy-start.11
  59.2 5.7 %copy-start.12 = (bf16[8,128,128]{2,1,0:T(8,128)(2,1)}, bf16[8,128,128]{2,1,0:T(8,128)(2,1)S(1)}, u32[]{:S(2)}) copy-start(bf16[8,128,128]{2,1,0:T(8,128)(2,1)S(1)} %collective-permute-done.2.refs_2_) | copy-start | bytes 786436
  59.2 0.9 copy-start.3
  60.0 22.5 %all-to-all-start.2 = ((bf16[8,256,128]{2,1,0:T(8,128)(2,1)}), bf16[8,256,128]{2,1,0:T(8,128)(2,1)S(1)}, u32[]{:S(2)}, u32[]{:S(2)}) async-start(bf16[8,256,128]{2,1,0:T(8,128)(2,1)} %pack.5), calls=%async_computation.2 | async-start | bytes 1048576 | tf_op jit(solution)/shard_map/all_to_all | solution.py:285
  82.5 5.1 %copy-start.4 = (bf16[8,256,128]{2,1,0:T(8,128)(2,1)}, bf16[8,256,128]{2,1,0:T(8,128)(2,1)S(1)}, u32[]{:S(2)}) copy-start(bf16[8,256,128]{2,1,0:T(8,128)(2,1)S(1)} %all-to-all-done.2) | copy-start | bytes 1572868
  82.6 23.1 %all-to-all-start.3 = ((bf16[8,128,128]{2,1,0:T(8,128)(2,1)}), bf16[8,128,128]{2,1,0:T(8,128)(2,1)S(1)}, u32[]{:S(2)}, u32[]{:S(2)}) async-start(bf16[8,128,128]{2,1,0:T(8,128)(2,1)} %get-tuple-element.51), calls=%async_computation.3 | async-start | bytes 524288 | tf_op jit(solution)/shard_map/all_to_all | solution.py:285
  105.7 0.7 copy-start.1
  105.7 7.0 %copy-start.14 = (bf16[8,128,128]{2,1,0:T(8,128)(2,1)S(1)}, bf16[8,128,128]{2,1,0:T(8,128)(2,1)}, u32[]{:S(2)}) copy-start(bf16[8,128,128]{2,1,0:T(8,128)(2,1)} %get-tuple-element.48) | copy-start | bytes 786436
  105.7 7.8 %copy-start.13 = (bf16[8,128,128]{2,1,0:T(8,128)(2,1)S(1)}, bf16[8,128,128]{2,1,0:T(8,128)(2,1)}, u32[]{:S(2)}) copy-start(bf16[8,128,128]{2,1,0:T(8,128)(2,1)} %get-tuple-element.49) | copy-start | bytes 786436
  106.4 24.5 %all-to-all-start.4 = ((bf16[8,128,128]{2,1,0:T(8,128)(2,1)}), bf16[8,128,128]{2,1,0:T(8,128)(2,1)S(1)}, u32[]{:S(2)}, u32[]{:S(2)}) async-start(bf16[8,128,128]{2,1,0:T(8,128)(2,1)} %get-tuple-element.53), calls=%async_computation.4 | async-start | bytes 524288 | tf_op jit(solution)/shard_map/all_to_all | solution.py:285
  111.5 9.3 %collective-permute-start.3 = (bf16[8,128,128]{2,1,0:T(8,128)(2,1)}, bf16[8,128,128]{2,1,0:T(8,128)(2,1)S(1)}, u32[]{:S(2)}, u32[]{:S(2)}) collective-permute-start(bf16[8,128,128]{2,1,0:T(8,128)(2,1)} %get-tuple-element.47), channel_id=1, source_target_pairs={{0,8},{8,0},{16,24},{24,16},{1,9},{9,1},{17,25},{25,17},{2,10},{10... | collective-permute-start | bytes 786440 | tf_op jit(solution)/shard_map/ppermute | solution.py:263
  112.6 8.5 %collective-permute-start.4 = (bf16[8,128,128]{2,1,0:T(8,128)(2,1)S(1)}, bf16[8,128,128]{2,1,0:T(8,128)(2,1)S(1)}, u32[]{:S(2)}, u32[]{:S(2)}) collective-permute-start(bf16[8,128,128]{2,1,0:T(8,128)(2,1)S(1)} %copy-done.14), channel_id=1, source_target_pairs={{0,16},{8,24},{16,0},{24,8},{1,17},{9,25},{17,1},{25,9},{2,18},{10... | collective-permute-start | bytes 786440 | tf_op jit(solution)/shard_map/ppermute | solution.py:263
  113.5 13.4 %collective-permute-start.5 = (bf16[8,128,128]{2,1,0:T(8,128)(2,1)S(1)}, bf16[8,128,128]{2,1,0:T(8,128)(2,1)S(1)}, u32[]{:S(2)}, u32[]{:S(2)}) collective-permute-start(bf16[8,128,128]{2,1,0:T(8,128)(2,1)S(1)} %copy-done.13), channel_id=1, source_target_pairs={{0,24},{8,16},{16,8},{24,0},{1,25},{9,17},{17,9},{25,1},{2,26},{10... | collective-permute-start | bytes 786440 | tf_op jit(solution)/shard_map/ppermute | solution.py:263
  120.8 6.2 %copy-start.5 = (bf16[8,128,128]{2,1,0:T(8,128)(2,1)}, bf16[8,128,128]{2,1,0:T(8,128)(2,1)S(1)}, u32[]{:S(2)}) copy-start(bf16[8,128,128]{2,1,0:T(8,128)(2,1)S(1)} %collective-permute-done.3.refs_2_) | copy-start | bytes 786436
  121.2 5.8 %copy-start.6 = (bf16[8,128,128]{2,1,0:T(8,128)(2,1)}, bf16[8,128,128]{2,1,0:T(8,128)(2,1)S(1)}, u32[]{:S(2)}) copy-start(bf16[8,128,128]{2,1,0:T(8,128)(2,1)S(1)} %collective-permute-done.4.refs_3_) | copy-start | bytes 786436
  127.0 0.7 copy-start.7
  130.8 31.4 %copy-start.2 = (bf16[8,128,128]{2,1,0:T(8,128)(2,1)}, bf16[8,128,128]{2,1,0:T(8,128)(2,1)S(1)}, u32[]{:S(2)}) copy-start(bf16[8,128,128]{2,1,0:T(8,128)(2,1)S(1)} %all-to-all-done.4.refs_1_) | copy-start | bytes 786436

commit v3 on v2

v3 whole, which is shorter than its diff:
```python
import functools
import math

import jax
import jax.numpy as jnp
from jax import lax
from jax.experimental import pallas as pl
from jax.experimental.pallas import tpu as pltpu
from jax.sharding import PartitionSpec as P

D = 1024
H = 16
NBR = 12
BS = 128
HD = D // H
LOG2E = 1.4426950408889634
VMEM_LIMIT = 56 << 20

bf16 = jnp.bfloat16
f32 = jnp.float32


def params():
    return pltpu.CompilerParams(vmem_limit_bytes=VMEM_LIMIT)


def cost(flops, bytes_accessed):
    return pl.CostEstimate(flops=flops, bytes_accessed=bytes_accessed, transcendentals=0)


VMEM = pl.BlockSpec(memory_space=pltpu.VMEM)
SMEM = pl.BlockSpec(memory_space=pltpu.SMEM)
ANY = pl.BlockSpec(memory_space=pl.ANY)


def pack_kernel(first, n, x_ref, y_ref, out_ref):
    for j in range(n):
        cols = pl.ds((first * n + j) * HD, HD)
        out_ref[j, :, pl.ds(0, HD)] = x_ref[:, cols]
        out_ref[j, :, pl.ds(HD, HD)] = y_ref[:, cols]


def pack(x, y, first, n):
    rows = x.shape[0]
    return pl.pallas_call(
        functools.partial(pack_kernel, first, n),
        out_shape=jax.ShapeDtypeStruct((n, rows, 2 * HD), bf16),
        in_specs=[VMEM] * 2,
        out_specs=VMEM,
        compiler_params=params(),
        cost_estimate=cost(0, 8 * rows * D),
        name="pack",
    )(x, y)


def tile(at):
    return pl.ds(pl.multiple_of(at * 2 * HD, 2 * HD), 2 * HD)


def pieces_kernel(count, n, h_ref, x_ref, y_ref, *outs):
    rows = x_ref.shape[0]
    h = h_ref[0]
    odd = jnp.broadcast_to(h & 1, (rows, 2 * HD)) == 1
    for k in range(0, n, 2):
        for f in range(count):
            cols = tile(f * (n // 2) + ((h ^ k) >> 1))
            x, y = x_ref[:, cols], y_ref[:, cols]
            even_head = jnp.concatenate([x[:, :HD], y[:, :HD]], 1)
            odd_head = jnp.concatenate([x[:, HD:], y[:, HD:]], 1)
            at = pl.ds(f * rows, rows)
            outs[k][at] = jnp.where(odd, odd_head, even_head)
            outs[k + 1][at] = jnp.where(odd, even_head, odd_head)


def pieces(x, y, count, n, h):
    rows = x.shape[0]
    return pl.pallas_call(
        functools.partial(pieces_kernel, count, n),
        out_shape=[jax.ShapeDtypeStruct((count * rows, 2 * HD), bf16)] * n,
        in_specs=[SMEM] + [VMEM] * 2,
        out_specs=[VMEM] * n,
        compiler_params=params(),
        cost_estimate=cost(0, 8 * rows * D),
        name="pieces",
    )(h, x, y)


def lend_kernel(phases, parts, cap, bpd, lists_ref, *refs):
    outs = refs[-(parts - 1) :]
    kv_ref = refs[-parts]
    for k, piece in enumerate(refs[:-parts]):
        kv_ref[k] = piece[...]
    for k in range(1, parts):
        for s in range(cap):
            b = lists_ref[k * cap + s]
            j, o = lax.div(b, bpd), lax.rem(b, bpd)
            for f in range(phases):
                outs[k - 1][f * cap + s] = kv_ref[j, f * bpd + o]


def lend(lists, kv, phases, parts, cap, bpd):
    n = len(kv)
    return pl.pallas_call(
        functools.partial(lend_kernel, phases, parts, cap, bpd),
        out_shape=[jax.ShapeDtypeStruct((n, phases * bpd, BS, 2 * HD), bf16)]
        + [jax.ShapeDtypeStruct((phases * cap, BS, 2 * HD), bf16)] * (parts - 1),
        in_specs=[SMEM] + [VMEM] * n,
        out_specs=[VMEM] * parts,
        compiler_params=params(),
        cost_estimate=cost(0, 4 * parts * cap * BS * 4 * HD),
        name="lend",
    )(lists, *kv)


def attend_kernel(f, paired, parts, cap, n, bpd, idx_ref, h_ref, kv_ref, tau_ref, *refs):
    qg, refs = (refs[:n], refs[n:]) if paired else (refs[:1], refs[1:])
    h = h_ref[0]
    borrowed, refs = refs[: parts - 1], refs[parts - 1 :]
    dq_out, own_ref, refs = refs[0], refs[1], refs[2:]
    back = refs[: parts - 1]
    tab, qg_tab, kt_tab, acc, s_buf, dp_buf, sem = refs[parts - 1 :]
    nblk = n * bpd
    slots = (parts - 1) * cap
    copies = [
        pltpu.make_async_copy(kv_ref.at[j, pl.ds(f * bpd, bpd)], tab.at[pl.ds(j * bpd, bpd)], sem.at[j])
        for j in range(n)
    ]
    for k in range(1, parts):
        copies.append(
            pltpu.make_async_copy(borrowed[k - 1].at[pl.ds(f * cap, cap)], tab.at[pl.ds(nblk + (k - 1) * cap, cap)], sem.at[n + k])
        )
    for k in range(n):
        src = qg[k] if paired else qg[0].at[k ^ h]
        copies.append(pltpu.make_async_copy(src, qg_tab.at[pl.ds(k * bpd, bpd)], sem.at[n + parts + k]))
    for c in copies:
        c.start()
    acc[...] = jnp.zeros_like(acc)
    for c in copies:
        c.wait()

    def flip(t, _):
        kt_tab[t] = tab[t].astype(f32).T[:HD].astype(bf16)
        return 0

    lax.fori_loop(0, nblk + slots, flip, 0, unroll=4)
    lane = lax.broadcasted_iota(jnp.int32, (BS, 2 * HD), 1)
    low = lane < HD
    zero = jnp.zeros((BS, 2 * HD), bf16)

    def fold8(x, op):
        return op(x.reshape(BS // 8, 8, BS), axis=0)

    def load(r):
        qg = qg_tab[r]
        both = jnp.concatenate([jnp.where(low, qg, zero), jnp.where(low, zero, qg)], 0)
        return both, [idx_ref[r * NBR + i] for i in range(NBR)]

    def step1(slot, both, where, i, top):
        rr = lax.dot_general(tab[where[i]], both, (((1,), (1,)), ((), ())), preferred_element_type=f32)
        s = rr[:, :BS]
        s_buf[slot, i] = s
        dp_buf[slot, i] = rr[:, BS:]
        m8 = fold8(s, jnp.max)
        return m8 if top is None else jnp.maximum(top, m8)

    def advance(r, slot, top, r2):
        both, where = load(r)
        both2, where2 = load(r2)
        m = jnp.max(top, axis=0, keepdims=True)
        tau = tau_ref[pl.ds(r, 1), :]
        c = tau * LOG2E
        top2 = None
        total = weighted = None
        nxt = 0
        for i in range(NBR):
            if i % 2 == 0:
                top2 = step1(1 - slot, both2, where2, nxt, top2); nxt += 1
            ex = jnp.exp2((s_buf[slot, i] - m) * c)
            s_buf[slot, i] = ex
            l8 = fold8(ex, jnp.sum)
            d8 = fold8(ex * dp_buf[slot, i], jnp.sum)
            total = l8 if total is None else total + l8
            weighted = d8 if weighted is None else weighted + d8
        norm = jnp.sum(total, axis=0, keepdims=True)
        inv = 1.0 / norm
        delta = jnp.sum(weighted, axis=0, keepdims=True) * inv
        dq = None
        for i in range(0, NBR, 2):
            us = []
            top2 = step1(1 - slot, both2, where2, nxt, top2); nxt += 1
            for j in (i, i + 1):
                p = s_buf[slot, j] * inv
                u = (p * (dp_buf[slot, j] - delta) * tau).astype(bf16)
                us.append(u)
                part = jnp.dot(jnp.concatenate([u, p.astype(bf16)], 1), both, preferred_element_type=f32)
                acc[where[j]] += part
            kt = jnp.concatenate([kt_tab[where[i]], kt_tab[where[i + 1]]], 1)
            d = jnp.dot(kt, jnp.concatenate(us, 0), preferred_element_type=f32)
            dq = d if dq is None else dq + d
        return dq, top2

    def pair(g, top):
        r = g * bpd
        dqs = []
        for rb in range(bpd):
            dq, top = advance(r + rb, rb % 2, top, jnp.minimum(r + rb + 1, nblk - 1))
            dqs.append(dq)
        turned = jnp.concatenate(dqs, 0).T.astype(bf16)
        dq_out[g ^ h] = turned
        return top

    both, where = load(0)
    top = None
    for i in range(NBR):
        top = step1(0, both, where, i, top)
    lax.fori_loop(0, n, pair, top)
    own_ref[...] = acc[pl.ds(0, nblk)]
    for k in range(1, parts):
        back[k - 1][...] = acc[pl.ds(nblk + (k - 1) * cap, cap)].astype(bf16)


def attend(idx, h, kv, f, qg, tau, borrowed, parts, cap, n, bpd):
    nblk = n * bpd
    slots = (parts - 1) * cap
    width = 2 * HD
    paired = isinstance(qg, list)
    qg = qg if paired else [qg]
    out = pl.pallas_call(
        functools.partial(attend_kernel, f, paired, parts, cap, n, bpd),
        out_shape=[
            jax.ShapeDtypeStruct((n, BS, width), bf16),
            jax.ShapeDtypeStruct((nblk, BS, width), f32),
        ]
        + [jax.ShapeDtypeStruct((cap, BS, width), bf16)] * (parts - 1),
        in_specs=[SMEM, SMEM] + [VMEM] * (2 + len(qg) + len(borrowed)),
        out_specs=[VMEM] * (1 + parts),
        scratch_shapes=[
            pltpu.VMEM((nblk + slots, BS, width), bf16),
            pltpu.VMEM((nblk, BS, width), bf16),
            pltpu.VMEM((nblk + slots, HD, BS), bf16),
            pltpu.VMEM((nblk + slots, BS, width), f32),
            pltpu.VMEM((bpd, NBR, BS, BS), f32),
            pltpu.VMEM((bpd, NBR, BS, BS), f32),
            pltpu.SemaphoreType.DMA((2 * n + parts,)),
        ],
        compiler_params=params(),
        cost_estimate=cost(nblk * NBR * BS * BS * HD * 100, 6 << 20),
        name="attend",
    )(idx, h, kv, tau, *qg, *borrowed)
    return out[0], out[1], out[2:]


def collect_kernel(parts, cap, n, bpd, lists_ref, own, *refs):
    returned, outs, total = refs[: parts - 1], refs[parts - 1 : -1], refs[-1]
    total[...] = own[...]
    for k in range(1, parts):
        for s in range(cap):
            total[lists_ref[k * cap + s]] += returned[k - 1][s].astype(f32)
    for k in range(n):
        for b in range(bpd):
            outs[k][pl.ds(b * BS, BS)] = total[k * bpd + b].astype(bf16)


def collect(lists, own, returned, parts, cap, n, bpd):
    return pl.pallas_call(
        functools.partial(collect_kernel, parts, cap, n, bpd),
        out_shape=[jax.ShapeDtypeStruct((bpd * BS, 2 * HD), bf16)] * n,
        in_specs=[SMEM] + [VMEM] * parts,
        out_specs=[VMEM] * n,
        scratch_shapes=[pltpu.VMEM(own.shape, f32)],
        compiler_params=params(),
        cost_estimate=cost(0, 4 << 20),
        name="collect",
    )(lists, own, *returned)


def by_head(odd, one, two):
    low, high = jnp.where(odd, two, one), jnp.where(odd, one, two)
    return (
        jnp.concatenate([low[:, :HD], high[:, :HD]], 1),
        jnp.concatenate([low[:, HD:], high[:, HD:]], 1),
    )


def unpack_q_kernel(n, bpd, *refs):
    dqs, gq = refs[:-1], refs[-1]
    never = jnp.zeros((BS, 2 * HD), jnp.int32) == 1
    for f, dq in enumerate(dqs):
        for j in range(0, n, 2):
            for b, part in enumerate(by_head(never, dq[j], dq[j + 1])):
                gq[pl.ds(b * BS, BS), tile((f * n + j) // 2)] = part


def unpack_kv_kernel(n, phases, bpd, h_ref, *refs):
    dkv, gk, gv = refs[:-2], refs[-2], refs[-1]
    h = h_ref[0]
    rows = bpd * BS
    odd = jnp.broadcast_to(h & 1, (rows, 2 * HD)) == 1
    for f in range(phases):
        for k in range(0, n, 2):
            cols = tile(f * (n // 2) + ((h ^ k) >> 1))
            one, two = dkv[f * n + k], dkv[f * n + k + 1]
            gk[:, cols], gv[:, cols] = by_head(odd, one[...], two[...])


def unpack(kernel, count, name, rows, arrays):
    shape = jax.ShapeDtypeStruct((rows, D), bf16)
    return pl.pallas_call(
        kernel,
        out_shape=[shape] * count,
        in_specs=[VMEM if a.ndim > 1 else SMEM for a in arrays],
        out_specs=[VMEM] * count,
        compiler_params=params(),
        cost_estimate=cost(0, 4 << 20),
        name=name,
    )(*arrays)


def swap(x, k, axis, size):
    return lax.ppermute(x, axis, [(i, i ^ k) for i in range(size)])


def body(node_queries, node_keys, node_values, out_grad, degrees, neighbor_blocks, send_slots):
    n = lax.axis_size("head")
    parts = lax.axis_size("dom")
    cap = send_slots.shape[2]
    phases = H // n
    rows = node_queries.shape[0]
    bpd = rows // BS
    nblk = n * bpd
    me = lax.axis_index("dom")
    head = lax.axis_index("head")
    h = head.astype(jnp.int32).reshape(1)
    hop = jnp.arange(parts, dtype=jnp.int32)
    pick = (hop[:, None] == (hop[None, :] ^ me)).astype(jnp.int32)
    step = jnp.arange(n, dtype=jnp.int32)
    turn = (step[:, None] == (step[None, :] ^ head)).astype(jnp.int32)

    def local(b):
        return ((b // bpd) ^ head) * bpd + b % bpd

    def turned(x):
        y = x.reshape(n, -1)
        return jnp.sum(turn[:, :, None] * y[None], axis=1).reshape(x.shape)

    mine = jnp.maximum(lax.dynamic_index_in_dim(send_slots, me, 0, keepdims=False), 0)
    lists = local(jnp.sum(pick[:, :, None] * mine[None], axis=1).reshape(-1))
    away = neighbor_blocks - nblk
    moved = nblk + ((away // cap) ^ me) * cap + away % cap - cap
    idx = turned(jnp.where(away < 0, local(neighbor_blocks), moved)).reshape(-1)
    count = turned(degrees.reshape(nblk, BS))
    tau = jnp.log(count.astype(f32)) / math.log(64.0) / math.sqrt(HD)

    def spread(x):
        return lax.all_to_all(x, "head", split_axis=0, concat_axis=0, tiled=True)

    def trade(x):
        return [x[0]] + [swap(x[k], k, "head", n) for k in range(1, n)]

    kv = [x.reshape(phases * bpd, BS, 2 * HD) for x in trade(pieces(node_keys, node_values, phases, n, h))]
    sent = pieces(node_queries, out_grad, 1, n, h)
    qg = [[x.reshape(bpd, BS, 2 * HD) for x in trade(sent)]]
    kv_all, *lent = lend(lists, kv, phases, parts, cap, bpd)
    borrowed = [swap(lent[k - 1], k, "dom", parts) for k in range(1, parts)]
    for f in range(1, phases):
        sent, qg[f - 1], borrowed = lax.optimization_barrier(
            (pack(node_queries, out_grad, f, n), qg[f - 1], borrowed)
        )
        qg.append(spread(sent).reshape(n, bpd, BS, 2 * HD))
    dqs, total, owns, returns = [], [], [], []
    for f in range(phases):
        dq, own, back = attend(idx, h, kv_all, f, qg[f], tau, borrowed, parts, cap, n, bpd)
        if f + 1 < phases:
            dq, qg[f + 1] = lax.optimization_barrier((dq, qg[f + 1]))
        if f:
            dq, own, back, dqs[f - 1], returns[f - 1], owns[f - 1] = lax.optimization_barrier(
                (dq, own, back, dqs[f - 1], returns[f - 1], owns[f - 1])
            )
        dqs.append(spread(dq))
        owns.append(own)
        returns.append([swap(back[k - 1], k, "dom", parts) for k in range(1, parts)])
    for f in range(phases):
        total += trade(collect(lists, owns[f], returns[f], parts, cap, n, bpd))
    (grad_q,) = unpack(functools.partial(unpack_q_kernel, n, bpd), 1, "unpack_q", rows, dqs)
    grad_k, grad_v = unpack(
        functools.partial(unpack_kv_kernel, n, phases, bpd), 2, "unpack_kv", rows, [h, *total]
    )
    return grad_q, grad_k, grad_v


def solution(mesh):
    placed = (
        P(("dom", "head"), None),
        P(("dom", "head"), None),
        P(("dom", "head"), None),
        P(("dom", "head"), None),
        P("dom"),
        P("dom", None),
        P(),
    )
    return jax.shard_map(
        body,
        mesh=mesh,
        in_specs=placed,
        out_specs=(P(("dom", "head"), None), P(("dom", "head"), None), P(("dom", "head"), None)),
        check_vma=False,
    )
```

time: 167 us -> 150 us (0.90)
  starting transfers between devices: 31.8 us -> 69.7 us
  blocking collectives: 31.4 us -> 0 us
  waiting for transfers between devices: 44.7 us -> 15.8 us
  Pallas kernels: 52.1 us -> 55.9 us
    ppermute x6 -> x37, starting transfers between devices: 7 us -> 56.2 us  [swap(): return lax.ppermute(x, axis, [(i, i ^ k) for i in range(size)])]
    all_to_all x1 -> x0, blocking collectives: 31.4 us -> none  [spread(): return lax.all_to_all(x, 'head', split_axis=0, concat_axis=0, tiled=True)]
    all_to_all x5 -> x3, waiting for transfers between devices: 24.3 us -> 0.01 us  [spread(): return lax.all_to_all(x, 'head', split_axis=0, concat_axis=0, tiled=True)]
    all_to_all x5 -> x3, starting transfers between devices: 24.8 us -> 13.6 us  [spread(): return lax.all_to_all(x, 'head', split_axis=0, concat_axis=0, tiled=True)]
    ppermute x6 -> x37, waiting for transfers between devices: 20.4 us -> 15.7 us  [swap(): return lax.ppermute(x, axis, [(i, i ^ k) for i in range(size)])]
    pallas_call x7 -> x9, Pallas kernels: 49.9 us -> 53.3 us  [the longest x2 37.2 us: attend(): pl.pallas_call(functools.partial(attend_kernel, f, paired, parts, cap, n,...]
  transfers between devices with their start and end apart: 11 -> 40, of which waited for: 6 -> 8; matrix products, arithmetic and copies ran while one was open for 2% -> 2% of each run, Pallas kernels for 28% -> 35%
where the time goes in v3:
time: 150 us; the launch traced here: 149 us
  starting transfers between devices  69.7 us (46%)
  Pallas kernels  55.9 us (37%)
  waiting for transfers between devices  15.8 us (11%)
  local copies, waits for them, and re-layouts  4.72 us (3%)
  other arithmetic  1.62 us (1%)
    ppermute x37, starting transfers between devices, swap(): return lax.ppermute(x, axis, [(i, i ^ k) for i in range(size)])  56.2 us
    pallas_call x2, Pallas kernels, attend(): pl.pallas_call(functools.partial(attend_kernel, f, paired, parts, cap, n,...  37.2 us
    ppermute x37, waiting for transfers between devices, swap(): return lax.ppermute(x, axis, [(i, i ^ k) for i in range(size)])  15.7 us
    all_to_all x3, starting transfers between devices, spread(): return lax.all_to_all(x, 'head', split_axis=0, concat_axis=0, tiled=True)  13.6 us
    pallas_call x2, Pallas kernels, unpack(): pl.pallas_call(kernel, out_shape=[shape] * count, in_specs=[VMEM if a.ndi...  4.66 us
    pallas_call x2, Pallas kernels, collect(): pl.pallas_call(functools.partial(collect_kernel, parts, cap, n, bpd), out...  4.61 us
    pallas_call x2, Pallas kernels, pieces(): pl.pallas_call(functools.partial(pieces_kernel, count, n), out_shape=[jax...  4.51 us
    unnamed x98, local copies, waits for them, and re-layouts  3.3 us
  transfers between devices with their start and end apart: 40, of which 8 were waited for; matrix products, arithmetic and copies ran while one was open for 2% of the time, Pallas kernels for 35%

profile of v3, /device:TPU:0, one launch (start us, length us, event | category | flops | bytes accessed | tf_op | source)
XLA Modules:
  0.0 148.9 jit_solution(15207590495888553032)
XLA Ops:
  0.6 2.3 %pieces.2 = (bf16[512,128]{1,0:T(8,128)(2,1)}, bf16[512,128]{1,0:T(8,128)(2,1)}, bf16[512,128]{1,0:T(8,128)(2,1)}, bf16[512,128]{1,0:T(8,128)(2,1)}, bf16[512,12...) custom-call(s32[1]{0:T(128)} %bitcast.h_ref, ...), custom_call_target="tpu_custom_call" | custom-call | bytes 2097152 | tf_op jit(solution)/shard_map/pieces/pallas_call | solution.py:77
  3.4 2.6 %collective-permute-start.1 = (bf16[512,128]{1,0:T(8,128)(2,1)}, bf16[512,128]{1,0:T(8,128)(2,1)S(1)}, u32[]{:S(2)}, u32[]{:S(2)}) collective-permute-start(bf16[512,128]{1,0:T(8,128)(2,1)} %get-tuple-element.77), channel_id=1, source_target_pairs={{0,2},{1,3},{2,0},{3,1},{4,6},{5,7},{6,4},{7,5},{8,10},{9,11},{10,... | collective-permute-start | bytes 393224 | tf_op jit(solution)/shard_map/ppermute | solution.py:320
  6.2 2.7 %collective-permute-start.3 = (bf16[512,128]{1,0:T(8,128)(2,1)}, bf16[512,128]{1,0:T(8,128)(2,1)S(1)}, u32[]{:S(2)}, u32[]{:S(2)}) collective-permute-start(bf16[512,128]{1,0:T(8,128)(2,1)} %get-tuple-element.79), channel_id=1, source_target_pairs={{0,4},{1,5},{2,6},{3,7},{4,0},{5,1},{6,2},{7,3},{8,12},{9,13},{10,... | collective-permute-start | bytes 393224 | tf_op jit(solution)/shard_map/ppermute | solution.py:320
  8.9 0.7 maximum_bitcast_fusion
  9.9 3.6 %collective-permute-start.5 = (bf16[512,128]{1,0:T(8,128)(2,1)}, bf16[512,128]{1,0:T(8,128)(2,1)S(1)}, u32[]{:S(2)}, u32[]{:S(2)}) collective-permute-start(bf16[512,128]{1,0:T(8,128)(2,1)} %get-tuple-element.81), channel_id=1, source_target_pairs={{0,6},{1,7},{2,4},{3,5},{4,2},{5,3},{6,0},{7,1},{8,14},{9,15},{10,... | collective-permute-start | bytes 393224 | tf_op jit(solution)/shard_map/ppermute | solution.py:320
  13.5 2.1 %collective-permute-done.1 = bf16[512,128]{1,0:T(8,128)(2,1)S(1)} collective-permute-done((bf16[512,128]{1,0:T(8,128)(2,1)}, bf16[512,128]{1,0:T(8,128)(2,1)S(1)}, u32[]{:S(2)}, u32[]{:S(2)}) %collective-permute-start.1) | collective-permute-done | bytes 131104 | tf_op jit(solution)/shard_map/ppermute | solution.py:320
  16.2 2.2 %pieces.3 = (bf16[256,128]{1,0:T(8,128)(2,1)}, bf16[256,128]{1,0:T(8,128)(2,1)}, bf16[256,128]{1,0:T(8,128)(2,1)}, bf16[256,128]{1,0:T(8,128)(2,1)}, bf16[256,12...) custom-call(s32[1]{0:T(128)} %bitcast.h_ref, ...), custom_call_target="tpu_custom_call" | custom-call | bytes 2097152 | tf_op jit(solution)/shard_map/pieces/pallas_call | solution.py:77
  18.4 2.0 %collective-permute-start.7 = (bf16[256,128]{1,0:T(8,128)(2,1)}, bf16[256,128]{1,0:T(8,128)(2,1)S(1)}, u32[]{:S(2)}, u32[]{:S(2)}) collective-permute-start(bf16[256,128]{1,0:T(8,128)(2,1)} %get-tuple-element.85), channel_id=1, source_target_pairs={{0,1},{1,0},{2,3},{3,2},{4,5},{5,4},{6,7},{7,6},{8,9},{9,8},{10,11... | collective-permute-start | bytes 196616 | tf_op jit(solution)/shard_map/ppermute | solution.py:320
  20.4 5.2 %collective-permute-start.8 = (bf16[256,128]{1,0:T(8,128)(2,1)}, bf16[256,128]{1,0:T(8,128)(2,1)S(1)}, u32[]{:S(2)}, u32[]{:S(2)}) collective-permute-start(bf16[256,128]{1,0:T(8,128)(2,1)} %get-tuple-element.86), channel_id=1, source_target_pairs={{0,2},{1,3},{2,0},{3,1},{4,6},{5,7},{6,4},{7,5},{8,10},{9,11},{10,... | collective-permute-start | bytes 196616 | tf_op jit(solution)/shard_map/ppermute | solution.py:320
  25.7 1.5 collective-permute-done.4
  27.3 6.0 %collective-permute-start.10 = (bf16[256,128]{1,0:T(8,128)(2,1)}, bf16[256,128]{1,0:T(8,128)(2,1)S(1)}, u32[]{:S(2)}, u32[]{:S(2)}) collective-permute-start(bf16[256,128]{1,0:T(8,128)(2,1)} %get-tuple-element.88), channel_id=1, source_target_pairs={{0,4},{1,5},{2,6},{3,7},{4,0},{5,1},{6,2},{7,3},{8,12},{9,13},{10,... | collective-permute-start | bytes 196616 | tf_op jit(solution)/shard_map/ppermute | solution.py:320
  33.4 2.9 %collective-permute-start.11 = (bf16[256,128]{1,0:T(8,128)(2,1)}, bf16[256,128]{1,0:T(8,128)(2,1)S(1)}, u32[]{:S(2)}, u32[]{:S(2)}) collective-permute-start(bf16[256,128]{1,0:T(8,128)(2,1)} %get-tuple-element.89), channel_id=1, source_target_pairs={{0,5},{1,4},{2,7},{3,6},{4,1},{5,0},{6,3},{7,2},{8,13},{9,12},{10,... | collective-permute-start | bytes 196616 | tf_op jit(solution)/shard_map/ppermute | solution.py:320
  36.3 2.6 %lend.1 = (bf16[8,4,128,128]{3,2,1,0:T(8,128)(2,1)}, bf16[8,128,128]{2,1,0:T(8,128)(2,1)}, bf16[8,128,128]{2,1,0:T(8,128)(2,1)}, bf16[8,128,128]{2,1,0:T(8,128)(2,1)}) custom-call(s32[16]{0:T(128)} %fusion.19.lists_ref, bf16[4,128,128]{2,1,0:T(8,128)(2,1)} %bitcast.21, bf16[4,128,128]{2,1,0:T(8,128)(2,1)} %bitcast.22, bf16[4,128,128]{2,1,0:T(8,128)(2,1)} %bitcast.23, ...), custom_call_target="tpu_custom_call" | custom-call | bytes 2097152 | tf_op jit(solution)/shard_map/lend/pallas_call | solution.py:103
  38.9 1.6 %collective-permute-start.14 = (bf16[8,128,128]{2,1,0:T(8,128)(2,1)}, bf16[8,128,128]{2,1,0:T(8,128)(2,1)S(1)}, u32[]{:S(2)}, u32[]{:S(2)}) collective-permute-start(bf16[8,128,128]{2,1,0:T(8,128)(2,1)} %get-tuple-element.92), channel_id=1, source_target_pairs={{0,8},{8,0},{16,24},{24,16},{1,9},{9,1},{17,25},{25,17},{2,10},{10... | collective-permute-start | bytes 786440 | tf_op jit(solution)/shard_map/ppermute | solution.py:320
  40.5 1.5 %collective-permute-start.15 = (bf16[8,128,128]{2,1,0:T(8,128)(2,1)}, bf16[8,128,128]{2,1,0:T(8,128)(2,1)S(1)}, u32[]{:S(2)}, u32[]{:S(2)}) collective-permute-start(bf16[8,128,128]{2,1,0:T(8,128)(2,1)} %get-tuple-element.93), channel_id=1, source_target_pairs={{0,16},{8,24},{16,0},{24,8},{1,17},{9,25},{17,1},{25,9},{2,18},{10... | collective-permute-start | bytes 786440 | tf_op jit(solution)/shard_map/ppermute | solution.py:320
  42.5 2.4 %pack.1 = bf16[8,256,128]{2,1,0:T(8,128)(2,1)} custom-call(bf16[256,1024]{1,0:T(8,128)(2,1)} %x_ref.5, bf16[256,1024]{1,0:T(8,128)(2,1)} %y_ref.5), custom_call_target="tpu_custom_call" | custom-call | bytes 2097152 | tf_op jit(solution)/shard_map/pack/pallas_call | solution.py:45
  45.1 1.1 collective-permute-start.13
  46.2 0.7 reshape_reshape.3.idx_ref
  47.5 3.8 %collective-permute-done.12 = bf16[256,128]{1,0:T(8,128)(2,1)S(1)} collective-permute-done((bf16[256,128]{1,0:T(8,128)(2,1)S(1)}, bf16[256,128]{1,0:T(8,128)(2,1)S(1)}, u32[]{:S(2)}, u32[]{:S(2)}) %collective-permute-start.12) | collective-permute-done | bytes 65568 | tf_op jit(solution)/shard_map/ppermute | solution.py:320
  51.4 1.6 %collective-permute-done.15.refs_9_.refs_2_ = bf16[8,128,128]{2,1,0:T(8,128)(2,1)S(1)} collective-permute-done((bf16[8,128,128]{2,1,0:T(8,128)(2,1)}, bf16[8,128,128]{2,1,0:T(8,128)(2,1)S(1)}, u32[]{:S(2)}, u32[]{:S(2)}) %collective-permute-start.15) | collective-permute-done | bytes 262176 | tf_op jit(solution)/shard_map/ppermute | solution.py:320
  53.0 0.6 copy-done.33
  53.8 3.5 %all-to-all-start = ((bf16[8,256,128]{2,1,0:T(8,128)(2,1)}), bf16[8,256,128]{2,1,0:T(8,128)(2,1)S(1)}, u32[]{:S(2)}, u32[]{:S(2)}) async-start(bf16[8,256,128]{2,1,0:T(8,128)(2,1)} %pack.1), calls=%async_computation | async-start | bytes 1048576 | tf_op jit(solution)/shard_map/all_to_all | solution.py:355
  57.3 18.6 %attend.2 = (bf16[8,128,128]{2,1,0:T(8,128)(2,1)}, f32[16,128,128]{2,1,0:T(8,128)}, bf16[4,128,128]{2,1,0:T(8,128)(2,1)}, bf16[4,128,128]{2,1,0:T(8,128)(2,1)}, bf16[4,128,128]{2,1,0:T(8,128)(2,1)}) custom-call(s32[192]{0:T(256)} %reshape_reshape.3.idx_ref, s32[1]{0:T(128)} %bitcast.h_ref, bf16[8,4,128,128]{3,2,1,0:T(8,128)(2,1)} %get-tuple-element.83.kv_ref, ...), custom_call_target="tpu_custom_call" | custom-call | flops 20132659200 | bytes 6291456 | tf_op jit(solution)/shard_map/attend/pallas_call | solution.py:228
  75.9 1.2 collective-permute-start.17
  77.1 1.2 collective-permute-start.18
  78.3 1.2 collective-permute-start.19
  79.5 5.0 %all-to-all-start.1 = ((bf16[8,128,128]{2,1,0:T(8,128)(2,1)}), bf16[8,128,128]{2,1,0:T(8,128)(2,1)S(1)}, u32[]{:S(2)}, u32[]{:S(2)}) async-start(bf16[8,128,128]{2,1,0:T(8,128)(2,1)} %get-tuple-element.114), calls=%async_computation.1 | async-start | bytes 524288 | tf_op jit(solution)/shard_map/all_to_all | solution.py:355
  84.5 18.5 %attend.3 = (bf16[8,128,128]{2,1,0:T(8,128)(2,1)}, f32[16,128,128]{2,1,0:T(8,128)}, bf16[4,128,128]{2,1,0:T(8,128)(2,1)}, bf16[4,128,128]{2,1,0:T(8,128)(2,1)}, bf16[4,128,128]{2,1,0:T(8,128)(2,1)}) custom-call(s32[192]{0:T(256)} %reshape_reshape.3.idx_ref, s32[1]{0:T(128)} %bitcast.h_ref, bf16[8,4,128,128]{3,2,1,0:T(8,128)(2,1)} %get-tuple-element.83.kv_ref, ...), custom_call_target="tpu_custom_call" | custom-call | flops 20132659200 | bytes 6291456 | tf_op jit(solution)/shard_map/attend/pallas_call | solution.py:228
  103.9 5.1 %all-to-all-start.2 = ((bf16[8,128,128]{2,1,0:T(8,128)(2,1)}), bf16[8,128,128]{2,1,0:T(8,128)(2,1)S(1)}, u32[]{:S(2)}, u32[]{:S(2)}) async-start(bf16[8,128,128]{2,1,0:T(8,128)(2,1)} %get-tuple-element.120), calls=%async_computation.2 | async-start | bytes 524288 | tf_op jit(solution)/shard_map/all_to_all | solution.py:355
  109.0 1.2 collective-permute-start.27
  110.2 1.2 collective-permute-start.28
  111.4 1.1 collective-permute-start.29
  112.5 2.3 %collect.2 = (bf16[256,128]{1,0:T(8,128)(2,1)}, bf16[256,128]{1,0:T(8,128)(2,1)}, bf16[256,128]{1,0:T(8,128)(2,1)}, bf16[256,128]{1,0:T(8,128)(2,1)}, bf16[256,1...) custom-call(s32[16]{0:T(128)} %fusion.19.lists_ref, ...), custom_call_target="tpu_custom_call" | custom-call | bytes 4194304 | tf_op jit(solution)/shard_map/collect/pallas_call | solution.py:265
  114.8 2.0 %collective-permute-start.21 = (bf16[256,128]{1,0:T(8,128)(2,1)}, bf16[256,128]{1,0:T(8,128)(2,1)S(1)}, u32[]{:S(2)}, u32[]{:S(2)}) collective-permute-start(bf16[256,128]{1,0:T(8,128)(2,1)} %get-tuple-element.127), channel_id=1, source_target_pairs={{0,2},{1,3},{2,0},{3,1},{4,6},{5,7},{6,4},{7,5},{8,10},{9,11},{10,... | collective-permute-start | bytes 196616 | tf_op jit(solution)/shard_map/ppermute | solution.py:320
  117.3 2.6 %collective-permute-start.23 = (bf16[256,128]{1,0:T(8,128)(2,1)}, bf16[256,128]{1,0:T(8,128)(2,1)S(1)}, u32[]{:S(2)}, u32[]{:S(2)}) collective-permute-start(bf16[256,128]{1,0:T(8,128)(2,1)} %get-tuple-element.129), channel_id=1, source_target_pairs={{0,4},{1,5},{2,6},{3,7},{4,0},{5,1},{6,2},{7,3},{8,12},{9,13},{10,... | collective-permute-start | bytes 196616 | tf_op jit(solution)/shard_map/ppermute | solution.py:320
  120.6 2.3 %collect.3 = (bf16[256,128]{1,0:T(8,128)(2,1)}, bf16[256,128]{1,0:T(8,128)(2,1)}, bf16[256,128]{1,0:T(8,128)(2,1)}, bf16[256,128]{1,0:T(8,128)(2,1)}, bf16[256,1...) custom-call(s32[16]{0:T(128)} %fusion.19.lists_ref, ...), custom_call_target="tpu_custom_call" | custom-call | bytes 4194304 | tf_op jit(solution)/shard_map/collect/pallas_call | solution.py:265
  122.9 2.6 %collective-permute-start.25 = (bf16[256,128]{1,0:T(8,128)(2,1)S(1)}, bf16[256,128]{1,0:T(8,128)(2,1)S(1)}, u32[]{:S(2)}, u32[]{:S(2)}) collective-permute-start(bf16[256,128]{1,0:T(8,128)(2,1)S(1)} %copy-done.46), channel_id=1, source_target_pairs={{0,6},{1,7},{2,4},{3,5},{4,2},{5,3},{6,0},{7,1},{8,14},{9,15},{10,... | collective-permute-start | bytes 196616 | tf_op jit(solution)/shard_map/ppermute | solution.py:320
  125.5 1.4 collective-permute-start.26
  127.5 1.3 collective-permute-start.32
  128.8 0.8 collective-permute-done.25.refs_6_
  129.6 4.1 %collective-permute-start.33 = (bf16[256,128]{1,0:T(8,128)(2,1)}, bf16[256,128]{1,0:T(8,128)(2,1)S(1)}, u32[]{:S(2)}, u32[]{:S(2)}) collective-permute-start(bf16[256,128]{1,0:T(8,128)(2,1)} %get-tuple-element.141), channel_id=1, source_target_pairs={{0,4},{1,5},{2,6},{3,7},{4,0},{5,1},{6,2},{7,3},{8,12},{9,13},{10,... | collective-permute-start | bytes 196616 | tf_op jit(solution)/shard_map/ppermute | solution.py:320
  133.7 0.8 collective-permute-start.34
  134.6 1.2 collective-permute-start.35
  135.7 2.1 %collective-permute-start.36 = (bf16[256,128]{1,0:T(8,128)(2,1)}, bf16[256,128]{1,0:T(8,128)(2,1)S(1)}, u32[]{:S(2)}, u32[]{:S(2)}) collective-permute-start(bf16[256,128]{1,0:T(8,128)(2,1)} %get-tuple-element.144), channel_id=1, source_target_pairs={{0,7},{1,6},{2,5},{3,4},{4,3},{5,2},{6,1},{7,0},{8,15},{9,14},{10,... | collective-permute-start | bytes 196616 | tf_op jit(solution)/shard_map/ppermute | solution.py:320
  137.8 5.0 %collective-permute-done.34.refs_13_ = bf16[256,128]{1,0:T(8,128)(2,1)S(1)} collective-permute-done((bf16[256,128]{1,0:T(8,128)(2,1)}, bf16[256,128]{1,0:T(8,128)(2,1)S(1)}, u32[]{:S(2)}, u32[]{:S(2)}) %collective-permute-start.34) | collective-permute-done | bytes 65568 | tf_op jit(solution)/shard_map/ppermute | solution.py:320
  143.5 2.6 %unpack_kv.1 = (bf16[256,1024]{1,0:T(8,128)(2,1)}, bf16[256,1024]{1,0:T(8,128)(2,1)}) custom-call(s32[1]{0:T(128)} %bitcast.h_ref, bf16[256,128]{1,0:T(8,128)(2,1)} %get-tuple-element.125.refs_0_, bf16[256,128]{1,0:T(8,128)(2,1)} %copy-done.16, bf16[256,128]{1,0:T(8,128)(2,1)} %copy-done.17, bf16[256,128]{1,0:T(8,128)(2,1)} %copy-done.18, ...), custom_call_target="tpu_custom_call" | custom-call | bytes 4194304 | tf_op jit(solution)/shard_map/unpack_kv/pallas_call | solution.py:308
  146.2 0.7 copy-done.1
  146.9 2.0 %unpack_q.1 = bf16[256,1024]{1,0:T(8,128)(2,1)} custom-call(bf16[8,128,128]{2,1,0:T(8,128)(2,1)} %copy-done, bf16[8,128,128]{2,1,0:T(8,128)(2,1)} %copy-done.1), custom_call_target="tpu_custom_call" | custom-call | bytes 4194304 | tf_op jit(solution)/shard_map/unpack_q/pallas_call | solution.py:308
  (156 shorter events, 6.2 us)
Async XLA Ops:
  3.0 6.9 %collective-permute-start = (bf16[512,128]{1,0:T(8,128)(2,1)}, bf16[512,128]{1,0:T(8,128)(2,1)S(1)}, u32[]{:S(2)}, u32[]{:S(2)}) collective-permute-start(bf16[512,128]{1,0:T(8,128)(2,1)} %get-tuple-element.76), channel_id=1, source_target_pairs={{0,1},{1,0},{2,3},{3,2},{4,5},{5,4},{6,7},{7,6},{8,9},{9,8},{10,11... | collective-permute-start | bytes 393224 | tf_op jit(solution)/shard_map/ppermute | solution.py:320
  3.4 12.2 %collective-permute-start.1 = (bf16[512,128]{1,0:T(8,128)(2,1)}, bf16[512,128]{1,0:T(8,128)(2,1)S(1)}, u32[]{:S(2)}, u32[]{:S(2)}) collective-permute-start(bf16[512,128]{1,0:T(8,128)(2,1)} %get-tuple-element.77), channel_id=1, source_target_pairs={{0,2},{1,3},{2,0},{3,1},{4,6},{5,7},{6,4},{7,5},{8,10},{9,11},{10,... | collective-permute-start | bytes 393224 | tf_op jit(solution)/shard_map/ppermute | solution.py:320
  6.0 12.4 %collective-permute-start.2 = (bf16[512,128]{1,0:T(8,128)(2,1)}, bf16[512,128]{1,0:T(8,128)(2,1)S(1)}, u32[]{:S(2)}, u32[]{:S(2)}) collective-permute-start(bf16[512,128]{1,0:T(8,128)(2,1)} %get-tuple-element.78), channel_id=1, source_target_pairs={{0,3},{1,2},{2,1},{3,0},{4,7},{5,6},{6,5},{7,4},{8,11},{9,10},{10,... | collective-permute-start | bytes 393224 | tf_op jit(solution)/shard_map/ppermute | solution.py:320
  6.2 14.3 %collective-permute-start.3 = (bf16[512,128]{1,0:T(8,128)(2,1)}, bf16[512,128]{1,0:T(8,128)(2,1)S(1)}, u32[]{:S(2)}, u32[]{:S(2)}) collective-permute-start(bf16[512,128]{1,0:T(8,128)(2,1)} %get-tuple-element.79), channel_id=1, source_target_pairs={{0,4},{1,5},{2,6},{3,7},{4,0},{5,1},{6,2},{7,3},{8,12},{9,13},{10,... | collective-permute-start | bytes 393224 | tf_op jit(solution)/shard_map/ppermute | solution.py:320
  8.9 18.3 %collective-permute-start.4 = (bf16[512,128]{1,0:T(8,128)(2,1)}, bf16[512,128]{1,0:T(8,128)(2,1)S(1)}, u32[]{:S(2)}, u32[]{:S(2)}) collective-permute-start(bf16[512,128]{1,0:T(8,128)(2,1)} %get-tuple-element.80), channel_id=1, source_target_pairs={{0,5},{1,4},{2,7},{3,6},{4,1},{5,0},{6,3},{7,2},{8,13},{9,12},{10,... | collective-permute-start | bytes 393224 | tf_op jit(solution)/shard_map/ppermute | solution.py:320
  9.9 17.5 %collective-permute-start.5 = (bf16[512,128]{1,0:T(8,128)(2,1)}, bf16[512,128]{1,0:T(8,128)(2,1)S(1)}, u32[]{:S(2)}, u32[]{:S(2)}) collective-permute-start(bf16[512,128]{1,0:T(8,128)(2,1)} %get-tuple-element.81), channel_id=1, source_target_pairs={{0,6},{1,7},{2,4},{3,5},{4,2},{5,3},{6,0},{7,1},{8,14},{9,15},{10,... | collective-permute-start | bytes 393224 | tf_op jit(solution)/shard_map/ppermute | solution.py:320
  15.6 17.8 %collective-permute-start.6 = (bf16[512,128]{1,0:T(8,128)(2,1)}, bf16[512,128]{1,0:T(8,128)(2,1)S(1)}, u32[]{:S(2)}, u32[]{:S(2)}) collective-permute-start(bf16[512,128]{1,0:T(8,128)(2,1)} %get-tuple-element.82), channel_id=1, source_target_pairs={{0,7},{1,6},{2,5},{3,4},{4,3},{5,2},{6,1},{7,0},{8,15},{9,14},{10,... | collective-permute-start | bytes 393224 | tf_op jit(solution)/shard_map/ppermute | solution.py:320
  18.4 17.9 %copy-start.5 = (bf16[512,128]{1,0:T(8,128)(2,1)}, bf16[512,128]{1,0:T(8,128)(2,1)S(1)}, u32[]{:S(2)}) copy-start(bf16[512,128]{1,0:T(8,128)(2,1)S(1)} %collective-permute-done.2) | copy-start | bytes 393220
  18.4 20.5 %collective-permute-start.7 = (bf16[256,128]{1,0:T(8,128)(2,1)}, bf16[256,128]{1,0:T(8,128)(2,1)S(1)}, u32[]{:S(2)}, u32[]{:S(2)}) collective-permute-start(bf16[256,128]{1,0:T(8,128)(2,1)} %get-tuple-element.85), channel_id=1, source_target_pairs={{0,1},{1,0},{2,3},{3,2},{4,5},{5,4},{6,7},{7,6},{8,9},{9,8},{10,11... | collective-permute-start | bytes 196616 | tf_op jit(solution)/shard_map/ppermute | solution.py:320
  20.4 15.9 %copy-start.6 = (bf16[512,128]{1,0:T(8,128)(2,1)}, bf16[512,128]{1,0:T(8,128)(2,1)S(1)}, u32[]{:S(2)}) copy-start(bf16[512,128]{1,0:T(8,128)(2,1)S(1)} %collective-permute-done.3) | copy-start | bytes 393220
  20.4 20.0 %collective-permute-start.8 = (bf16[256,128]{1,0:T(8,128)(2,1)}, bf16[256,128]{1,0:T(8,128)(2,1)S(1)}, u32[]{:S(2)}, u32[]{:S(2)}) collective-permute-start(bf16[256,128]{1,0:T(8,128)(2,1)} %get-tuple-element.86), channel_id=1, source_target_pairs={{0,2},{1,3},{2,0},{3,1},{4,6},{5,7},{6,4},{7,5},{8,10},{9,11},{10,... | collective-permute-start | bytes 196616 | tf_op jit(solution)/shard_map/ppermute | solution.py:320
  27.1 14.9 %collective-permute-start.9 = (bf16[256,128]{1,0:T(8,128)(2,1)}, bf16[256,128]{1,0:T(8,128)(2,1)S(1)}, u32[]{:S(2)}, u32[]{:S(2)}) collective-permute-start(bf16[256,128]{1,0:T(8,128)(2,1)} %get-tuple-element.87), channel_id=1, source_target_pairs={{0,3},{1,2},{2,1},{3,0},{4,7},{5,6},{6,5},{7,4},{8,11},{9,10},{10,... | collective-permute-start | bytes 196616 | tf_op jit(solution)/shard_map/ppermute | solution.py:320
  27.3 17.7 %collective-permute-start.10 = (bf16[256,128]{1,0:T(8,128)(2,1)}, bf16[256,128]{1,0:T(8,128)(2,1)S(1)}, u32[]{:S(2)}, u32[]{:S(2)}) collective-permute-start(bf16[256,128]{1,0:T(8,128)(2,1)} %get-tuple-element.88), channel_id=1, source_target_pairs={{0,4},{1,5},{2,6},{3,7},{4,0},{5,1},{6,2},{7,3},{8,12},{9,13},{10,... | collective-permute-start | bytes 196616 | tf_op jit(solution)/shard_map/ppermute | solution.py:320
  33.4 11.7 %collective-permute-start.11 = (bf16[256,128]{1,0:T(8,128)(2,1)}, bf16[256,128]{1,0:T(8,128)(2,1)S(1)}, u32[]{:S(2)}, u32[]{:S(2)}) collective-permute-start(bf16[256,128]{1,0:T(8,128)(2,1)} %get-tuple-element.89), channel_id=1, source_target_pairs={{0,5},{1,4},{2,7},{3,6},{4,1},{5,0},{6,3},{7,2},{8,13},{9,12},{10,... | collective-permute-start | bytes 196616 | tf_op jit(solution)/shard_map/ppermute | solution.py:320
  38.9 12.4 %collective-permute-start.14 = (bf16[8,128,128]{2,1,0:T(8,128)(2,1)}, bf16[8,128,128]{2,1,0:T(8,128)(2,1)S(1)}, u32[]{:S(2)}, u32[]{:S(2)}) collective-permute-start(bf16[8,128,128]{2,1,0:T(8,128)(2,1)} %get-tuple-element.92), channel_id=1, source_target_pairs={{0,8},{8,0},{16,24},{24,16},{1,9},{9,1},{17,25},{25,17},{2,10},{10... | collective-permute-start | bytes 786440 | tf_op jit(solution)/shard_map/ppermute | solution.py:320
  40.5 12.5 %collective-permute-start.15 = (bf16[8,128,128]{2,1,0:T(8,128)(2,1)}, bf16[8,128,128]{2,1,0:T(8,128)(2,1)S(1)}, u32[]{:S(2)}, u32[]{:S(2)}) collective-permute-start(bf16[8,128,128]{2,1,0:T(8,128)(2,1)} %get-tuple-element.93), channel_id=1, source_target_pairs={{0,16},{8,24},{16,0},{24,8},{1,17},{9,25},{17,1},{25,9},{2,18},{10... | collective-permute-start | bytes 786440 | tf_op jit(solution)/shard_map/ppermute | solution.py:320
  42.0 11.0 %collective-permute-start.16 = (bf16[8,128,128]{2,1,0:T(8,128)(2,1)}, bf16[8,128,128]{2,1,0:T(8,128)(2,1)S(1)}, u32[]{:S(2)}, u32[]{:S(2)}) collective-permute-start(bf16[8,128,128]{2,1,0:T(8,128)(2,1)} %get-tuple-element.94), channel_id=1, source_target_pairs={{0,24},{8,16},{16,8},{24,0},{1,25},{9,17},{17,9},{25,1},{2,26},{10... | collective-permute-start | bytes 786440 | tf_op jit(solution)/shard_map/ppermute | solution.py:320
  45.0 6.4 %collective-permute-start.12 = (bf16[256,128]{1,0:T(8,128)(2,1)S(1)}, bf16[256,128]{1,0:T(8,128)(2,1)S(1)}, u32[]{:S(2)}, u32[]{:S(2)}) collective-permute-start(bf16[256,128]{1,0:T(8,128)(2,1)S(1)} %copy-done.42), channel_id=1, source_target_pairs={{0,6},{1,7},{2,4},{3,5},{4,2},{5,3},{6,0},{7,1},{8,14},{9,15},{10,... | collective-permute-start | bytes 196616 | tf_op jit(solution)/shard_map/ppermute | solution.py:320
  45.1 6.3 %collective-permute-start.13 = (bf16[256,128]{1,0:T(8,128)(2,1)S(1)}, bf16[256,128]{1,0:T(8,128)(2,1)S(1)}, u32[]{:S(2)}, u32[]{:S(2)}) collective-permute-start(bf16[256,128]{1,0:T(8,128)(2,1)S(1)} %copy-done.41), channel_id=1, source_target_pairs={{0,7},{1,6},{2,5},{3,4},{4,3},{5,2},{6,1},{7,0},{8,15},{9,14},{10,... | collective-permute-start | bytes 196616 | tf_op jit(solution)/shard_map/ppermute | solution.py:320
  53.8 25.7 %all-to-all-start = ((bf16[8,256,128]{2,1,0:T(8,128)(2,1)}), bf16[8,256,128]{2,1,0:T(8,128)(2,1)S(1)}, u32[]{:S(2)}, u32[]{:S(2)}) async-start(bf16[8,256,128]{2,1,0:T(8,128)(2,1)} %pack.1), calls=%async_computation | async-start | bytes 1048576 | tf_op jit(solution)/shard_map/all_to_all | solution.py:355
  75.9 27.1 %collective-permute-start.17 = (bf16[4,128,128]{2,1,0:T(8,128)(2,1)}, bf16[4,128,128]{2,1,0:T(8,128)(2,1)S(1)}, u32[]{:S(2)}, u32[]{:S(2)}) collective-permute-start(bf16[4,128,128]{2,1,0:T(8,128)(2,1)} %get-tuple-element.115), channel_id=1, source_target_pairs={{0,8},{8,0},{16,24},{24,16},{1,9},{9,1},{17,25},{25,17},{2,10},{10... | collective-permute-start | bytes 393224 | tf_op jit(solution)/shard_map/ppermute | solution.py:320
  77.1 25.9 %collective-permute-start.18 = (bf16[4,128,128]{2,1,0:T(8,128)(2,1)}, bf16[4,128,128]{2,1,0:T(8,128)(2,1)S(1)}, u32[]{:S(2)}, u32[]{:S(2)}) collective-permute-start(bf16[4,128,128]{2,1,0:T(8,128)(2,1)} %get-tuple-element.116), channel_id=1, source_target_pairs={{0,16},{8,24},{16,0},{24,8},{1,17},{9,25},{17,1},{25,9},{2,18},{10... | collective-permute-start | bytes 393224 | tf_op jit(solution)/shard_map/ppermute | solution.py:320
  78.3 24.8 %collective-permute-start.19 = (bf16[4,128,128]{2,1,0:T(8,128)(2,1)}, bf16[4,128,128]{2,1,0:T(8,128)(2,1)S(1)}, u32[]{:S(2)}, u32[]{:S(2)}) collective-permute-start(bf16[4,128,128]{2,1,0:T(8,128)(2,1)} %get-tuple-element.117), channel_id=1, source_target_pairs={{0,24},{8,16},{16,8},{24,0},{1,25},{9,17},{17,9},{25,1},{2,26},{10... | collective-permute-start | bytes 393224 | tf_op jit(solution)/shard_map/ppermute | solution.py:320
  79.5 23.6 %all-to-all-start.1 = ((bf16[8,128,128]{2,1,0:T(8,128)(2,1)}), bf16[8,128,128]{2,1,0:T(8,128)(2,1)S(1)}, u32[]{:S(2)}, u32[]{:S(2)}) async-start(bf16[8,128,128]{2,1,0:T(8,128)(2,1)} %get-tuple-element.114), calls=%async_computation.1 | async-start | bytes 524288 | tf_op jit(solution)/shard_map/all_to_all | solution.py:355
  103.9 42.3 %all-to-all-start.2 = ((bf16[8,128,128]{2,1,0:T(8,128)(2,1)}), bf16[8,128,128]{2,1,0:T(8,128)(2,1)S(1)}, u32[]{:S(2)}, u32[]{:S(2)}) async-start(bf16[8,128,128]{2,1,0:T(8,128)(2,1)} %get-tuple-element.120), calls=%async_computation.2 | async-start | bytes 524288 | tf_op jit(solution)/shard_map/all_to_all | solution.py:355
  109.0 7.9 %collective-permute-start.27 = (bf16[4,128,128]{2,1,0:T(8,128)(2,1)S(1)}, bf16[4,128,128]{2,1,0:T(8,128)(2,1)S(1)}, u32[]{:S(2)}, u32[]{:S(2)}) collective-permute-start(bf16[4,128,128]{2,1,0:T(8,128)(2,1)S(1)} %copy-done.37), channel_id=1, source_target_pairs={{0,8},{8,0},{16,24},{24,16},{1,9},{9,1},{17,25},{25,17},{2,10},{10... | collective-permute-start | bytes 393224 | tf_op jit(solution)/shard_map/ppermute | solution.py:320
  110.2 7.2 %collective-permute-start.28 = (bf16[4,128,128]{2,1,0:T(8,128)(2,1)S(1)}, bf16[4,128,128]{2,1,0:T(8,128)(2,1)S(1)}, u32[]{:S(2)}, u32[]{:S(2)}) collective-permute-start(bf16[4,128,128]{2,1,0:T(8,128)(2,1)S(1)} %copy-done.36), channel_id=1, source_target_pairs={{0,16},{8,24},{16,0},{24,8},{1,17},{9,25},{17,1},{25,9},{2,18},{10... | collective-permute-start | bytes 393224 | tf_op jit(solution)/shard_map/ppermute | solution.py:320
  111.4 8.5 %collective-permute-start.29 = (bf16[4,128,128]{2,1,0:T(8,128)(2,1)S(1)}, bf16[4,128,128]{2,1,0:T(8,128)(2,1)S(1)}, u32[]{:S(2)}, u32[]{:S(2)}) collective-permute-start(bf16[4,128,128]{2,1,0:T(8,128)(2,1)S(1)} %copy-done.35), channel_id=1, source_target_pairs={{0,24},{8,16},{16,8},{24,0},{1,25},{9,17},{17,9},{25,1},{2,26},{10... | collective-permute-start | bytes 393224 | tf_op jit(solution)/shard_map/ppermute | solution.py:320
  114.8 8.0 %collective-permute-start.20 = (bf16[256,128]{1,0:T(8,128)(2,1)}, bf16[256,128]{1,0:T(8,128)(2,1)S(1)}, u32[]{:S(2)}, u32[]{:S(2)}) collective-permute-start(bf16[256,128]{1,0:T(8,128)(2,1)} %get-tuple-element.126), channel_id=1, source_target_pairs={{0,1},{1,0},{2,3},{3,2},{4,5},{5,4},{6,7},{7,6},{8,9},{9,8},{10,11... | collective-permute-start | bytes 196616 | tf_op jit(solution)/shard_map/ppermute | solution.py:320
  114.8 10.7 %collective-permute-start.21 = (bf16[256,128]{1,0:T(8,128)(2,1)}, bf16[256,128]{1,0:T(8,128)(2,1)S(1)}, u32[]{:S(2)}, u32[]{:S(2)}) collective-permute-start(bf16[256,128]{1,0:T(8,128)(2,1)} %get-tuple-element.127), channel_id=1, source_target_pairs={{0,2},{1,3},{2,0},{3,1},{4,6},{5,7},{6,4},{7,5},{8,10},{9,11},{10,... | collective-permute-start | bytes 196616 | tf_op jit(solution)/shard_map/ppermute | solution.py:320
  116.9 10.1 %collective-permute-start.22 = (bf16[256,128]{1,0:T(8,128)(2,1)}, bf16[256,128]{1,0:T(8,128)(2,1)S(1)}, u32[]{:S(2)}, u32[]{:S(2)}) collective-permute-start(bf16[256,128]{1,0:T(8,128)(2,1)} %get-tuple-element.128), channel_id=1, source_target_pairs={{0,3},{1,2},{2,1},{3,0},{4,7},{5,6},{6,5},{7,4},{8,11},{9,10},{10,... | collective-permute-start | bytes 196616 | tf_op jit(solution)/shard_map/ppermute | solution.py:320
  117.3 9.6 %collective-permute-start.23 = (bf16[256,128]{1,0:T(8,128)(2,1)}, bf16[256,128]{1,0:T(8,128)(2,1)S(1)}, u32[]{:S(2)}, u32[]{:S(2)}) collective-permute-start(bf16[256,128]{1,0:T(8,128)(2,1)} %get-tuple-element.129), channel_id=1, source_target_pairs={{0,4},{1,5},{2,6},{3,7},{4,0},{5,1},{6,2},{7,3},{8,12},{9,13},{10,... | collective-permute-start | bytes 196616 | tf_op jit(solution)/shard_map/ppermute | solution.py:320
  119.9 7.6 %collective-permute-start.24 = (bf16[256,128]{1,0:T(8,128)(2,1)}, bf16[256,128]{1,0:T(8,128)(2,1)S(1)}, u32[]{:S(2)}, u32[]{:S(2)}) collective-permute-start(bf16[256,128]{1,0:T(8,128)(2,1)} %get-tuple-element.130), channel_id=1, source_target_pairs={{0,5},{1,4},{2,7},{3,6},{4,1},{5,0},{6,3},{7,2},{8,13},{9,12},{10,... | collective-permute-start | bytes 196616 | tf_op jit(solution)/shard_map/ppermute | solution.py:320
  122.9 20.0 %copy-start.16 = (bf16[256,128]{1,0:T(8,128)(2,1)}, bf16[256,128]{1,0:T(8,128)(2,1)S(1)}, u32[]{:S(2)}) copy-start(bf16[256,128]{1,0:T(8,128)(2,1)S(1)} %collective-permute-done.20.refs_1_) | copy-start | bytes 196612
  122.9 6.7 %collective-permute-start.25 = (bf16[256,128]{1,0:T(8,128)(2,1)S(1)}, bf16[256,128]{1,0:T(8,128)(2,1)S(1)}, u32[]{:S(2)}, u32[]{:S(2)}) collective-permute-start(bf16[256,128]{1,0:T(8,128)(2,1)S(1)} %copy-done.46), channel_id=1, source_target_pairs={{0,6},{1,7},{2,4},{3,5},{4,2},{5,3},{6,0},{7,1},{8,14},{9,15},{10,... | collective-permute-start | bytes 196616 | tf_op jit(solution)/shard_map/ppermute | solution.py:320
  125.5 17.4 %copy-start.17 = (bf16[256,128]{1,0:T(8,128)(2,1)}, bf16[256,128]{1,0:T(8,128)(2,1)S(1)}, u32[]{:S(2)}) copy-start(bf16[256,128]{1,0:T(8,128)(2,1)S(1)} %collective-permute-done.21.refs_2_) | copy-start | bytes 196612
  125.5 8.2 %collective-permute-start.26 = (bf16[256,128]{1,0:T(8,128)(2,1)S(1)}, bf16[256,128]{1,0:T(8,128)(2,1)S(1)}, u32[]{:S(2)}, u32[]{:S(2)}) collective-permute-start(bf16[256,128]{1,0:T(8,128)(2,1)S(1)} %copy-done.45), channel_id=1, source_target_pairs={{0,7},{1,6},{2,5},{3,4},{4,3},{5,2},{6,1},{7,0},{8,15},{9,14},{10,... | collective-permute-start | bytes 196616 | tf_op jit(solution)/shard_map/ppermute | solution.py:320
  126.9 16.0 %copy-start.18 = (bf16[256,128]{1,0:T(8,128)(2,1)}, bf16[256,128]{1,0:T(8,128)(2,1)S(1)}, u32[]{:S(2)}) copy-start(bf16[256,128]{1,0:T(8,128)(2,1)S(1)} %collective-permute-done.22.refs_3_) | copy-start | bytes 196612
  126.9 7.7 %collective-permute-start.30 = (bf16[256,128]{1,0:T(8,128)(2,1)}, bf16[256,128]{1,0:T(8,128)(2,1)S(1)}, u32[]{:S(2)}, u32[]{:S(2)}) collective-permute-start(bf16[256,128]{1,0:T(8,128)(2,1)} %get-tuple-element.138), channel_id=1, source_target_pairs={{0,1},{1,0},{2,3},{3,2},{4,5},{5,4},{6,7},{7,6},{8,9},{9,8},{10,11... | collective-permute-start | bytes 196616 | tf_op jit(solution)/shard_map/ppermute | solution.py:320
  127.0 16.0 %copy-start.19 = (bf16[256,128]{1,0:T(8,128)(2,1)}, bf16[256,128]{1,0:T(8,128)(2,1)S(1)}, u32[]{:S(2)}) copy-start(bf16[256,128]{1,0:T(8,128)(2,1)S(1)} %collective-permute-done.23.refs_4_) | copy-start | bytes 196612
  127.0 8.8 %collective-permute-start.31 = (bf16[256,128]{1,0:T(8,128)(2,1)}, bf16[256,128]{1,0:T(8,128)(2,1)S(1)}, u32[]{:S(2)}, u32[]{:S(2)}) collective-permute-start(bf16[256,128]{1,0:T(8,128)(2,1)} %get-tuple-element.139), channel_id=1, source_target_pairs={{0,2},{1,3},{2,0},{3,1},{4,6},{5,7},{6,4},{7,5},{8,10},{9,11},{10,... | collective-permute-start | bytes 196616 | tf_op jit(solution)/shard_map/ppermute | solution.py:320
  127.5 15.5 %copy-start.20 = (bf16[256,128]{1,0:T(8,128)(2,1)}, bf16[256,128]{1,0:T(8,128)(2,1)S(1)}, u32[]{:S(2)}) copy-start(bf16[256,128]{1,0:T(8,128)(2,1)S(1)} %collective-permute-done.24.refs_5_) | copy-start | bytes 196612
  127.5 10.3 %collective-permute-start.32 = (bf16[256,128]{1,0:T(8,128)(2,1)}, bf16[256,128]{1,0:T(8,128)(2,1)S(1)}, u32[]{:S(2)}, u32[]{:S(2)}) collective-permute-start(bf16[256,128]{1,0:T(8,128)(2,1)} %get-tuple-element.140), channel_id=1, source_target_pairs={{0,3},{1,2},{2,1},{3,0},{4,7},{5,6},{6,5},{7,4},{8,11},{9,10},{10,... | collective-permute-start | bytes 196616 | tf_op jit(solution)/shard_map/ppermute | solution.py:320
  129.6 13.3 %copy-start.21 = (bf16[256,128]{1,0:T(8,128)(2,1)}, bf16[256,128]{1,0:T(8,128)(2,1)S(1)}, u32[]{:S(2)}) copy-start(bf16[256,128]{1,0:T(8,128)(2,1)S(1)} %collective-permute-done.25.refs_6_) | copy-start | bytes 196612
  129.6 8.2 %collective-permute-start.33 = (bf16[256,128]{1,0:T(8,128)(2,1)}, bf16[256,128]{1,0:T(8,128)(2,1)S(1)}, u32[]{:S(2)}, u32[]{:S(2)}) collective-permute-start(bf16[256,128]{1,0:T(8,128)(2,1)} %get-tuple-element.141), channel_id=1, source_target_pairs={{0,4},{1,5},{2,6},{3,7},{4,0},{5,1},{6,2},{7,3},{8,12},{9,13},{10,... | collective-permute-start | bytes 196616 | tf_op jit(solution)/shard_map/ppermute | solution.py:320
  133.7 9.1 %collective-permute-start.34 = (bf16[256,128]{1,0:T(8,128)(2,1)}, bf16[256,128]{1,0:T(8,128)(2,1)S(1)}, u32[]{:S(2)}, u32[]{:S(2)}) collective-permute-start(bf16[256,128]{1,0:T(8,128)(2,1)} %get-tuple-element.142), channel_id=1, source_target_pairs={{0,5},{1,4},{2,7},{3,6},{4,1},{5,0},{6,3},{7,2},{8,13},{9,12},{10,... | collective-permute-start | bytes 196616 | tf_op jit(solution)/shard_map/ppermute | solution.py:320
  134.6 8.3 %collective-permute-start.35 = (bf16[256,128]{1,0:T(8,128)(2,1)}, bf16[256,128]{1,0:T(8,128)(2,1)S(1)}, u32[]{:S(2)}, u32[]{:S(2)}) collective-permute-start(bf16[256,128]{1,0:T(8,128)(2,1)} %get-tuple-element.143), channel_id=1, source_target_pairs={{0,6},{1,7},{2,4},{3,5},{4,2},{5,3},{6,0},{7,1},{8,14},{9,15},{10,... | collective-permute-start | bytes 196616 | tf_op jit(solution)/shard_map/ppermute | solution.py:320
  135.7 7.1 %collective-permute-start.36 = (bf16[256,128]{1,0:T(8,128)(2,1)}, bf16[256,128]{1,0:T(8,128)(2,1)S(1)}, u32[]{:S(2)}, u32[]{:S(2)}) collective-permute-start(bf16[256,128]{1,0:T(8,128)(2,1)} %get-tuple-element.144), channel_id=1, source_target_pairs={{0,7},{1,6},{2,5},{3,4},{4,3},{5,2},{6,1},{7,0},{8,15},{9,14},{10,... | collective-permute-start | bytes 196616 | tf_op jit(solution)/shard_map/ppermute | solution.py:320
  (41 other events, 171.2 us)

commit v4 on v3

--- a/solution.py
+++ b/solution.py
@@ -33,50 +33,71 @@
 ANY = pl.BlockSpec(memory_space=pl.ANY)
 
 
-def pack_kernel(first, n, x_ref, y_ref, out_ref):
-    for j in range(n):
-        cols = pl.ds((first * n + j) * HD, HD)
-        out_ref[j, :, pl.ds(0, HD)] = x_ref[:, cols]
-        out_ref[j, :, pl.ds(HD, HD)] = y_ref[:, cols]
-
-
-def pack(x, y, first, n):
+def pack_kernel(first, n, q_ref, k_ref, v_ref, g_ref, out_ref):
+    rows = q_ref.shape[0]
+    for i in range(0, n, 2):
+        cols = tile((first * n + i) // 2)
+        for at, (x, y) in ((0, (k_ref[:, cols], v_ref[:, cols])), (rows, (q_ref[:, cols], g_ref[:, cols]))):
+            out_ref[i, pl.ds(at, rows)] = jnp.concatenate([x[:, :HD], y[:, :HD]], 1)
+            out_ref[i + 1, pl.ds(at, rows)] = jnp.concatenate([x[:, HD:], y[:, HD:]], 1)
+
+
+def pack(queries, keys, values, grads, first, n):
+    rows = queries.shape[0]
+    return pl.pallas_call(
+        functools.partial(pack_kernel, first, n),
+        out_shape=jax.ShapeDtypeStruct((n, 2 * rows, 2 * HD), bf16),
+        in_specs=[VMEM] * 4,
+        out_specs=VMEM,
+        compiler_params=params(),
+        cost_estimate=cost(0, 8 * rows * D),
+        name="pack",
+    )(queries, keys, values, grads)
+
+
+def tile(at):
+    return pl.ds(pl.multiple_of(at * 2 * HD, 2 * HD), 2 * HD)
+
+
+def pack_one_kernel(n, x_ref, y_ref, out_ref):
+    for i in range(0, n, 2):
+        cols = tile(i // 2)
+        x, y = x_ref[:, cols], y_ref[:, cols]
+        out_ref[i] = jnp.concatenate([x[:, :HD], y[:, :HD]], 1)
+        out_ref[i + 1] = jnp.concatenate([x[:, HD:], y[:, HD:]], 1)
+
+
+def pack_one(x, y, n):
     rows = x.shape[0]
     return pl.pallas_call(
-        functools.partial(pack_kernel, first, n),
+        functools.partial(pack_one_kernel, n),
         out_shape=jax.ShapeDtypeStruct((n, rows, 2 * HD), bf16),
         in_specs=[VMEM] * 2,
         out_specs=VMEM,
         compiler_params=params(),
         cost_estimate=cost(0, 8 * rows * D),
-        name="pack",
+        name="pack_one",
     )(x, y)
 
 
-def tile(at):
-    return pl.ds(pl.multiple_of(at * 2 * HD, 2 * HD), 2 * HD)
-
-
-def pieces_kernel(count, n, h_ref, x_ref, y_ref, *outs):
+def pieces_kernel(n, h_ref, x_ref, y_ref, *outs):
     rows = x_ref.shape[0]
     h = h_ref[0]
     odd = jnp.broadcast_to(h & 1, (rows, 2 * HD)) == 1
     for k in range(0, n, 2):
-        for f in range(count):
-            cols = tile(f * (n // 2) + ((h ^ k) >> 1))
-            x, y = x_ref[:, cols], y_ref[:, cols]
-            even_head = jnp.concatenate([x[:, :HD], y[:, :HD]], 1)
-            odd_head = jnp.concatenate([x[:, HD:], y[:, HD:]], 1)
-            at = pl.ds(f * rows, rows)
-            outs[k][at] = jnp.where(odd, odd_head, even_head)
-            outs[k + 1][at] = jnp.where(odd, even_head, odd_head)
-
-
-def pieces(x, y, count, n, h):
+        cols = tile((h ^ k) >> 1)
+        x, y = x_ref[:, cols], y_ref[:, cols]
+        even_head = jnp.concatenate([x[:, :HD], y[:, :HD]], 1)
+        odd_head = jnp.concatenate([x[:, HD:], y[:, HD:]], 1)
+        outs[k][...] = jnp.where(odd, odd_head, even_head)
+        outs[k + 1][...] = jnp.where(odd, even_head, odd_head)
+
+
+def pieces(x, y, n, h):
     rows = x.shape[0]
     return pl.pallas_call(
-        functools.partial(pieces_kernel, count, n),
-        out_shape=[jax.ShapeDtypeStruct((count * rows, 2 * HD), bf16)] * n,
+        functools.partial(pieces_kernel, n),
+        out_shape=[jax.ShapeDtypeStruct((rows, 2 * HD), bf16)] * n,
         in_specs=[SMEM] + [VMEM] * 2,
         out_specs=[VMEM] * n,
         compiler_params=params(),
@@ -85,35 +106,37 @@
     )(h, x, y)
 
 
-def lend_kernel(phases, parts, cap, bpd, lists_ref, *refs):
+def lend_kernel(parts, cap, bpd, lists_ref, h_ref, *refs):
     outs = refs[-(parts - 1) :]
-    kv_ref = refs[-parts]
-    for k, piece in enumerate(refs[:-parts]):
-        kv_ref[k] = piece[...]
+    kvs = refs[: -(parts - 1)]
+    h = h_ref[0]
+    if len(kvs) > 1:
+        source, h = kvs[-1], 0
+        for k, piece in enumerate(kvs[:-1]):
+            source[k] = piece[...]
+    else:
+        source = kvs[0]
     for k in range(1, parts):
         for s in range(cap):
             b = lists_ref[k * cap + s]
-            j, o = lax.div(b, bpd), lax.rem(b, bpd)
-            for f in range(phases):
-                outs[k - 1][f * cap + s] = kv_ref[j, f * bpd + o]
-
-
-def lend(lists, kv, phases, parts, cap, bpd):
-    n = len(kv)
+            outs[k - 1][s] = source[lax.div(b, bpd) ^ h, lax.rem(b, bpd)]
+
+
+def lend(lists, h, kv, parts, cap, bpd):
+    whole = [] if len(kv) == 1 else [jax.ShapeDtypeStruct((len(kv), bpd, BS, 2 * HD), bf16)]
     return pl.pallas_call(
-        functools.partial(lend_kernel, phases, parts, cap, bpd),
-        out_shape=[jax.ShapeDtypeStruct((n, phases * bpd, BS, 2 * HD), bf16)]
-        + [jax.ShapeDtypeStruct((phases * cap, BS, 2 * HD), bf16)] * (parts - 1),
-        in_specs=[SMEM] + [VMEM] * n,
-        out_specs=[VMEM] * parts,
+        functools.partial(lend_kernel, parts, cap, bpd),
+        out_shape=whole + [jax.ShapeDtypeStruct((cap, BS, 2 * HD), bf16)] * (parts - 1),
+        in_specs=[SMEM, SMEM] + [VMEM] * len(kv),
+        out_specs=[VMEM] * (len(whole) + parts - 1),
         compiler_params=params(),
         cost_estimate=cost(0, 4 * parts * cap * BS * 4 * HD),
         name="lend",
-    )(lists, *kv)
-
-
-def attend_kernel(f, paired, parts, cap, n, bpd, idx_ref, h_ref, kv_ref, tau_ref, *refs):
-    qg, refs = (refs[:n], refs[n:]) if paired else (refs[:1], refs[1:])
+    )(lists, h, *kv)
+
+
+def attend_kernel(paired, parts, cap, n, bpd, idx_ref, h_ref, kv_ref, tau_ref, *refs):
+    qg, refs = (refs[0], refs[1:]) if paired else (None, refs)
     h = h_ref[0]
     borrowed, refs = refs[: parts - 1], refs[parts - 1 :]
     dq_out, own_ref, refs = refs[0], refs[1], refs[2:]
@@ -121,17 +144,16 @@
     tab, qg_tab, kt_tab, acc, s_buf, dp_buf, sem = refs[parts - 1 :]
     nblk = n * bpd
     slots = (parts - 1) * cap
-    copies = [
-        pltpu.make_async_copy(kv_ref.at[j, pl.ds(f * bpd, bpd)], tab.at[pl.ds(j * bpd, bpd)], sem.at[j])
-        for j in range(n)
-    ]
+    copies = []
+    for k in range(n):
+        j = k if paired else k ^ h
+        src = qg.at[k ^ h] if paired else kv_ref.at[j, pl.ds(bpd, bpd)]
+        copies.append(pltpu.make_async_copy(kv_ref.at[j, pl.ds(0, bpd)], tab.at[pl.ds(k * bpd, bpd)], sem.at[k]))
+        copies.append(pltpu.make_async_copy(src, qg_tab.at[pl.ds(k * bpd, bpd)], sem.at[n + parts + k]))
     for k in range(1, parts):
         copies.append(
-            pltpu.make_async_copy(borrowed[k - 1].at[pl.ds(f * cap, cap)], tab.at[pl.ds(nblk + (k - 1) * cap, cap)], sem.at[n + k])
+            pltpu.make_async_copy(borrowed[k - 1], tab.at[pl.ds(nblk + (k - 1) * cap, cap)], sem.at[n + k])
         )
-    for k in range(n):
-        src = qg[k] if paired else qg[0].at[k ^ h]
-        copies.append(pltpu.make_async_copy(src, qg_tab.at[pl.ds(k * bpd, bpd)], sem.at[n + parts + k]))
     for c in copies:
         c.start()
     acc[...] = jnp.zeros_like(acc)
@@ -219,14 +241,12 @@
         back[k - 1][...] = acc[pl.ds(nblk + (k - 1) * cap, cap)].astype(bf16)
 
 
-def attend(idx, h, kv, f, qg, tau, borrowed, parts, cap, n, bpd):
+def attend(idx, h, kv, qg, tau, borrowed, parts, cap, n, bpd):
     nblk = n * bpd
     slots = (parts - 1) * cap
     width = 2 * HD
-    paired = isinstance(qg, list)
-    qg = qg if paired else [qg]
     out = pl.pallas_call(
-        functools.partial(attend_kernel, f, paired, parts, cap, n, bpd),
+        functools.partial(attend_kernel, bool(qg), parts, cap, n, bpd),
         out_shape=[
             jax.ShapeDtypeStruct((n, BS, width), bf16),
             jax.ShapeDtypeStruct((nblk, BS, width), f32),
@@ -250,28 +270,42 @@
     return out[0], out[1], out[2:]
 
 
-def collect_kernel(parts, cap, n, bpd, lists_ref, own, *refs):
-    returned, outs, total = refs[: parts - 1], refs[parts - 1 : -1], refs[-1]
+def collect_kernel(last, parts, cap, n, bpd, lists_ref, h_ref, own, *refs):
+    returned, refs = refs[: parts - 1], refs[parts - 1 :]
+    total = refs[-1]
     total[...] = own[...]
     for k in range(1, parts):
         for s in range(cap):
             total[lists_ref[k * cap + s]] += returned[k - 1][s].astype(f32)
+    if not last:
+        dq, out = refs[0], refs[1]
+        out[:, pl.ds(0, BS)] = dq[...]
     for k in range(n):
         for b in range(bpd):
-            outs[k][pl.ds(b * BS, BS)] = total[k * bpd + b].astype(bf16)
-
-
-def collect(lists, own, returned, parts, cap, n, bpd):
+            block = total[k * bpd + b].astype(bf16)
+            if last:
+                refs[k][pl.ds(b * BS, BS)] = block
+            else:
+                out[k ^ h_ref[0], pl.ds((1 + b) * BS, BS)] = block
+
+
+def collect(lists, h, own, returned, dq, parts, cap, n, bpd):
+    last = dq is None
+    if last:
+        out = [jax.ShapeDtypeStruct((bpd * BS, 2 * HD), bf16)] * n
+    else:
+        out = [jax.ShapeDtypeStruct((n, (1 + bpd) * BS, 2 * HD), bf16)]
+    more = [] if last else [dq]
     return pl.pallas_call(
-        functools.partial(collect_kernel, parts, cap, n, bpd),
-        out_shape=[jax.ShapeDtypeStruct((bpd * BS, 2 * HD), bf16)] * n,
-        in_specs=[SMEM] + [VMEM] * parts,
-        out_specs=[VMEM] * n,
+        functools.partial(collect_kernel, last, parts, cap, n, bpd),
+        out_shape=out,
+        in_specs=[SMEM, SMEM] + [VMEM] * (parts + len(more)),
+        out_specs=[VMEM] * len(out),
         scratch_shapes=[pltpu.VMEM(own.shape, f32)],
         compiler_params=params(),
         cost_estimate=cost(0, 4 << 20),
         name="collect",
-    )(lists, own, *returned)
+    )(lists, h, own, *returned, *more)
 
 
 def by_head(odd, one, two):
@@ -282,38 +316,55 @@
     )
 
 
-def unpack_q_kernel(n, bpd, *refs):
-    dqs, gq = refs[:-1], refs[-1]
-    never = jnp.zeros((BS, 2 * HD), jnp.int32) == 1
-    for f, dq in enumerate(dqs):
+def unpack_early_kernel(n, bpd, *refs):
+    *arrived, last_q, gq, gk, gv = refs
+    rows = bpd * BS
+    never = jnp.zeros((rows, 2 * HD), jnp.int32) == 1
+    never_q = jnp.zeros((BS, 2 * HD), jnp.int32) == 1
+    top, tail = pl.ds(0, BS), pl.ds(BS, rows)
+    for f, got in enumerate([*arrived, last_q]):
         for j in range(0, n, 2):
-            for b, part in enumerate(by_head(never, dq[j], dq[j + 1])):
-                gq[pl.ds(b * BS, BS), tile((f * n + j) // 2)] = part
-
-
-def unpack_kv_kernel(n, phases, bpd, h_ref, *refs):
-    dkv, gk, gv = refs[:-2], refs[-2], refs[-1]
+            cols = tile((f * n + j) // 2)
+            for b, part in enumerate(by_head(never_q, got[j, top], got[j + 1, top])):
+                gq[pl.ds(b * BS, BS), cols] = part
+            if f < len(arrived):
+                gk[:, cols], gv[:, cols] = by_head(never, got[j, tail], got[j + 1, tail])
+
+
+def unpack_last_kernel(n, h_ref, *refs):
+    last, gk, gv = refs[:n], refs[-2], refs[-1]
     h = h_ref[0]
+    odd = jnp.broadcast_to(h & 1, last[0].shape) == 1
+    for k in range(0, n, 2):
+        cols = tile((h ^ k) >> 1)
+        gk[:, cols], gv[:, cols] = by_head(odd, last[k][...], last[k + 1][...])
+
+
+def unpack(arrived, last_q, total, h, phases, n, bpd):
     rows = bpd * BS
-    odd = jnp.broadcast_to(h & 1, (rows, 2 * HD)) == 1
-    for f in range(phases):
-        for k in range(0, n, 2):
-            cols = tile(f * (n // 2) + ((h ^ k) >> 1))
-            one, two = dkv[f * n + k], dkv[f * n + k + 1]
-            gk[:, cols], gv[:, cols] = by_head(odd, one[...], two[...])
-
-
-def unpack(kernel, count, name, rows, arrays):
     shape = jax.ShapeDtypeStruct((rows, D), bf16)
-    return pl.pallas_call(
-        kernel,
-        out_shape=[shape] * count,
-        in_specs=[VMEM if a.ndim > 1 else SMEM for a in arrays],
-        out_specs=[VMEM] * count,
-        compiler_params=params(),
-        cost_estimate=cost(0, 4 << 20),
-        name=name,
-    )(*arrays)
+    gq, gk, gv = pl.pallas_call(
+        functools.partial(unpack_early_kernel, n, bpd),
+        out_shape=[shape] * 3,
+        in_specs=[VMEM] * (len(arrived) + 1),
+        out_specs=[VMEM] * 3,
+        compiler_params=params(),
+        cost_estimate=cost(0, 8 << 20),
+        name="unpack_early",
+    )(*arrived, last_q)
+    part = pl.BlockSpec((rows, n * HD), lambda i: (0, phases - 1))
+    gk, gv = pl.pallas_call(
+        functools.partial(unpack_last_kernel, n),
+        grid=(1,),
+        out_shape=[shape] * 2,
+        in_specs=[SMEM] + [VMEM] * n + [ANY] * 2,
+        out_specs=[part] * 2,
+        input_output_aliases={n + 1: 0, n + 2: 1},
+        compiler_params=params(),
+        cost_estimate=cost(0, 2 << 20),
+        name="unpack_last",
+    )(h, *total, gk, gv)
+    return gq, gk, gv
 
 
 def swap(x, k, axis, size):
@@ -357,35 +408,36 @@
     def trade(x):
         return [x[0]] + [swap(x[k], k, "head", n) for k in range(1, n)]
 
-    kv = [x.reshape(phases * bpd, BS, 2 * HD) for x in trade(pieces(node_keys, node_values, phases, n, h))]
-    sent = pieces(node_queries, out_grad, 1, n, h)
-    qg = [[x.reshape(bpd, BS, 2 * HD) for x in trade(sent)]]
-    kv_all, *lent = lend(lists, kv, phases, parts, cap, bpd)
-    borrowed = [swap(lent[k - 1], k, "dom", parts) for k in range(1, parts)]
+    kv = [x.reshape(bpd, BS, 2 * HD) for x in trade(pieces(node_keys, node_values, n, h))]
+    early = 1 + n // 4
+    first, kv[1:early] = lax.optimization_barrier((pack_one(node_queries, out_grad, n), kv[1:early]))
+    qg = [spread(first).reshape(n, bpd, BS, 2 * HD)]
+    later = []
     for f in range(1, phases):
-        sent, qg[f - 1], borrowed = lax.optimization_barrier(
-            (pack(node_queries, out_grad, f, n), qg[f - 1], borrowed)
-        )
-        qg.append(spread(sent).reshape(n, bpd, BS, 2 * HD))
-    dqs, total, owns, returns = [], [], [], []
+        sent, qg = lax.optimization_barrier((pack(node_queries, node_keys, node_values, out_grad, f, n), qg))
+        later.append(spread(sent).reshape(n, 2 * bpd, BS, 2 * HD))
+    arrived, total, sent = [], [], None
     for f in range(phases):
-        dq, own, back = attend(idx, h, kv_all, f, qg[f], tau, borrowed, parts, cap, n, bpd)
-        if f + 1 < phases:
-            dq, qg[f + 1] = lax.optimization_barrier((dq, qg[f + 1]))
+        last = f + 1 == phases
         if f:
-            dq, own, back, dqs[f - 1], returns[f - 1], owns[f - 1] = lax.optimization_barrier(
-                (dq, own, back, dqs[f - 1], returns[f - 1], owns[f - 1])
-            )
-        dqs.append(spread(dq))
-        owns.append(own)
-        returns.append([swap(back[k - 1], k, "dom", parts) for k in range(1, parts)])
-    for f in range(phases):
-        total += trade(collect(lists, owns[f], returns[f], parts, cap, n, bpd))
-    (grad_q,) = unpack(functools.partial(unpack_q_kernel, n, bpd), 1, "unpack_q", rows, dqs)
-    grad_k, grad_v = unpack(
-        functools.partial(unpack_kv_kernel, n, phases, bpd), 2, "unpack_kv", rows, [h, *total]
-    )
-    return grad_q, grad_k, grad_v
+            kv, qg = [later[f - 1]], []
+        lent = lend(lists, h, kv, parts, cap, bpd)
+        borrowed = [swap(x, k + 1, "dom", parts) for k, x in enumerate(lent[-(parts - 1) :])]
+        if f:
+            borrowed, _ = lax.optimization_barrier((borrowed, sent))
+            arrived.append(spread(sent))
+        dq, own, back = attend(idx, h, lent[0] if f == 0 else kv[0], qg, tau, borrowed, parts, cap, n, bpd)
+        returned = [swap(back[k - 1], k, "dom", parts) for k in range(1, parts)]
+        if f:
+            dq, arrived[-1], returned = lax.optimization_barrier((dq, arrived[-1], returned))
+        if last:
+            dq_all = spread(dq)
+        out = collect(lists, h, own, returned, None if last else dq, parts, cap, n, bpd)
+        if last:
+            total = trade(out)
+        else:
+            sent = out[0]
+    return tuple(unpack(arrived, dq_all, total, h, phases, n, bpd))
 
 
 def solution(mesh):

time: 150 us -> 136 us (0.907)
  starting transfers between devices: 69.7 us -> 47.7 us
  local copies, waits for them, and re-layouts: 4.72 us -> 8.48 us
  waiting for transfers between devices: 15.8 us -> 18.3 us
    ppermute x37 -> x26, starting transfers between devices: 56.2 us -> 32.3 us  [swap(): return lax.ppermute(x, axis, [(i, i ^ k) for i in range(size)])]
    all_to_all x3 -> x4, waiting for transfers between devices: 0.01 us -> 7.86 us  [spread(): return lax.all_to_all(x, 'head', split_axis=0, concat_axis=0, tiled=True)]
    ppermute x37 -> x26, waiting for transfers between devices: 15.7 us -> 10.4 us  [swap(): return lax.ppermute(x, axis, [(i, i ^ k) for i in range(size)])]
    unnamed x98 -> x68, local copies, waits for them, and re-layouts: 3.3 us -> 7.07 us
    all_to_all x3 -> x4, starting transfers between devices: 13.6 us -> 15.4 us  [spread(): return lax.all_to_all(x, 'head', split_axis=0, concat_axis=0, tiled=True)]
    pallas_call x9 -> x10, Pallas kernels: 53.5 us -> 54.4 us  [the longest x2 36.5 us: attend(): pl.pallas_call(functools.partial(attend_kernel, bool(qg), parts, cap, n,...]
  transfers between devices with their start and end apart: 40 -> 30, of which waited for: 8 -> 6; matrix products, arithmetic and copies ran while one was open for 2% -> 2% of each run, Pallas kernels for 35% -> 40%
where the time goes in v4:
time: 136 us; the launch traced here: 134 us
  Pallas kernels  57.3 us (42%)
  starting transfers between devices  47.7 us (35%)
  waiting for transfers between devices  18.3 us (13%)
  local copies, waits for them, and re-layouts  8.48 us (6%)
  other arithmetic  1.6 us (1%)
    pallas_call x2, Pallas kernels, attend(): pl.pallas_call(functools.partial(attend_kernel, bool(qg), parts, cap, n,...  36.5 us
    ppermute x26, starting transfers between devices, swap(): return lax.ppermute(x, axis, [(i, i ^ k) for i in range(size)])  32.3 us
    all_to_all x4, starting transfers between devices, spread(): return lax.all_to_all(x, 'head', split_axis=0, concat_axis=0, tiled=True)  15.4 us
    ppermute x26, waiting for transfers between devices, swap(): return lax.ppermute(x, axis, [(i, i ^ k) for i in range(size)])  10.4 us
    all_to_all x4, waiting for transfers between devices, spread(): return lax.all_to_all(x, 'head', split_axis=0, concat_axis=0, tiled=True)  7.86 us
    unnamed x68, local copies, waits for them, and re-layouts  7.07 us
    pallas_call x2, Pallas kernels, collect(): pl.pallas_call(functools.partial(collect_kernel, last, parts, cap, n, bpd...  4.83 us
    pallas_call x2, Pallas kernels, lend(): pl.pallas_call(functools.partial(lend_kernel, parts, cap, bpd), out_shape...  4.07 us
  transfers between devices with their start and end apart: 30, of which 6 were waited for; matrix products, arithmetic and copies ran while one was open for 2% of the time, Pallas kernels for 40%

profile of v4, /device:TPU:0, one launch (start us, length us, event | category | flops | bytes accessed | tf_op | source)
XLA Modules:
  0.0 134.3 jit_solution(7625710282269846253)
XLA Ops:
  0.6 2.1 %pieces.1 = (bf16[256,128]{1,0:T(8,128)(2,1)}, bf16[256,128]{1,0:T(8,128)(2,1)}, bf16[256,128]{1,0:T(8,128)(2,1)}, bf16[256,128]{1,0:T(8,128)(2,1)}, bf16[256,12...) custom-call(s32[1]{0:T(128)} %bitcast.h_ref, ...), custom_call_target="tpu_custom_call" | custom-call | bytes 2097152 | tf_op jit(solution)/shard_map/pieces/pallas_call | solution.py:98
  3.2 2.6 %collective-permute-start.1 = (bf16[256,128]{1,0:T(8,128)(2,1)}, bf16[256,128]{1,0:T(8,128)(2,1)S(1)}, u32[]{:S(2)}, u32[]{:S(2)}) collective-permute-start(bf16[256,128]{1,0:T(8,128)(2,1)} %get-tuple-element.55), channel_id=1, source_target_pairs={{0,2},{1,3},{2,0},{3,1},{4,6},{5,7},{6,4},{7,5},{8,10},{9,11},{10,... | collective-permute-start | bytes 196616 | tf_op jit(solution)/shard_map/ppermute | solution.py:371
  5.8 2.5 %collective-permute-start.8 = (bf16[256,128]{1,0:T(8,128)(2,1)}, bf16[256,128]{1,0:T(8,128)(2,1)S(1)}, u32[]{:S(2)}, u32[]{:S(2)}) collective-permute-start(bf16[256,128]{1,0:T(8,128)(2,1)} %get-tuple-element.67), channel_id=1, source_target_pairs={{0,6},{1,7},{2,4},{3,5},{4,2},{5,3},{6,0},{7,1},{8,14},{9,15},{10,... | collective-permute-start | bytes 196616 | tf_op jit(solution)/shard_map/ppermute | solution.py:371
  8.3 0.9 collective-permute-start.9
  9.2 2.2 %pack_one.1 = bf16[8,256,128]{2,1,0:T(8,128)(2,1)} custom-call(bf16[256,1024]{1,0:T(8,128)(2,1)} %x_ref.2, bf16[256,1024]{1,0:T(8,128)(2,1)} %y_ref.2), custom_call_target="tpu_custom_call" | custom-call | bytes 2097152 | tf_op jit(solution)/shard_map/pack_one/pallas_call | solution.py:72
  11.5 0.7 maximum_bitcast_fusion
  12.3 3.3 %collective-permute-start.6 = (bf16[256,128]{1,0:T(8,128)(2,1)S(1)}, bf16[256,128]{1,0:T(8,128)(2,1)S(1)}, u32[]{:S(2)}, u32[]{:S(2)}) collective-permute-start(bf16[256,128]{1,0:T(8,128)(2,1)S(1)} %copy-done.33), channel_id=1, source_target_pairs={{0,4},{1,5},{2,6},{3,7},{4,0},{5,1},{6,2},{7,3},{8,12},{9,13},{10,... | collective-permute-start | bytes 196616 | tf_op jit(solution)/shard_map/ppermute | solution.py:371
  16.2 3.5 %all-to-all-start = ((bf16[8,256,128]{2,1,0:T(8,128)(2,1)}), bf16[8,256,128]{2,1,0:T(8,128)(2,1)S(1)}, u32[]{:S(2)}, u32[]{:S(2)}) async-start(bf16[8,256,128]{2,1,0:T(8,128)(2,1)} %pack_one.1), calls=%async_computation | async-start | bytes 1048576 | tf_op jit(solution)/shard_map/all_to_all | solution.py:406
  19.7 2.9 %pack.1 = bf16[8,512,128]{2,1,0:T(8,128)(2,1)} custom-call(bf16[256,1024]{1,0:T(8,128)(2,1)} %x_ref.2, bf16[256,1024]{1,0:T(8,128)(2,1)} %x_ref.3, bf16[256,1024]{1,0:T(8,128)(2,1)} %y_ref.3, bf16[256,1024]{1,0:T(8,128)(2,1)} %y_ref.2), custom_call_target="tpu_custom_call" | custom-call | bytes 2097152 | tf_op jit(solution)/shard_map/pack/pallas_call | solution.py:47
  22.8 0.7 reshape_reshape.3.idx_ref
  23.5 0.6 fusion.19.lists_ref
  24.9 2.0 %lend.3 = (bf16[8,2,128,128]{3,2,1,0:T(8,128)(2,1)}, bf16[4,128,128]{2,1,0:T(8,128)(2,1)}, bf16[4,128,128]{2,1,0:T(8,128)(2,1)}, bf16[4,128,128]{2,1,0:T(8,128)(2,1)}) custom-call(s32[16]{0:T(128)} %fusion.19.lists_ref, s32[1]{0:T(128)} %bitcast.h_ref, bf16[2,128,128]{2,1,0:T(8,128)(2,1)} %bitcast.16, bf16[2,128,128]{2,1,0:T(8,128)(2,1)} %bitcast.17, ...), custom_call_target="tpu_custom_call" | custom-call | bytes 2097152 | tf_op jit(solution)/shard_map/lend/pallas_call | solution.py:127
  26.9 1.5 %collective-permute-start.10 = (bf16[4,128,128]{2,1,0:T(8,128)(2,1)}, bf16[4,128,128]{2,1,0:T(8,128)(2,1)S(1)}, u32[]{:S(2)}, u32[]{:S(2)}) collective-permute-start(bf16[4,128,128]{2,1,0:T(8,128)(2,1)} %get-tuple-element.71), channel_id=1, source_target_pairs={{0,8},{8,0},{16,24},{24,16},{1,9},{9,1},{17,25},{25,17},{2,10},{10... | collective-permute-start | bytes 393224 | tf_op jit(solution)/shard_map/ppermute | solution.py:371
  28.5 1.5 %collective-permute-start.11 = (bf16[4,128,128]{2,1,0:T(8,128)(2,1)}, bf16[4,128,128]{2,1,0:T(8,128)(2,1)S(1)}, u32[]{:S(2)}, u32[]{:S(2)}) collective-permute-start(bf16[4,128,128]{2,1,0:T(8,128)(2,1)} %get-tuple-element.72), channel_id=1, source_target_pairs={{0,16},{8,24},{16,0},{24,8},{1,17},{9,25},{17,1},{25,9},{2,18},{10... | collective-permute-start | bytes 393224 | tf_op jit(solution)/shard_map/ppermute | solution.py:371
  30.5 0.6 div.46.tau_ref
  31.1 3.9 %all-to-all-done = bf16[8,256,128]{2,1,0:T(8,128)(2,1)S(1)} async-done(((bf16[8,256,128]{2,1,0:T(8,128)(2,1)}), bf16[8,256,128]{2,1,0:T(8,128)(2,1)S(1)}, u32[]{:S(2)}, u32[]{:S(2)}) %all-to-all-start) | async-done | bytes 524320 | tf_op jit(solution)/shard_map/all_to_all | solution.py:406
  35.0 0.8 copy-done.3
  35.8 3.6 %all-to-all-start.1 = ((bf16[8,512,128]{2,1,0:T(8,128)(2,1)}), bf16[8,512,128]{2,1,0:T(8,128)(2,1)S(1)}, u32[]{:S(2)}, u32[]{:S(2)}) async-start(bf16[8,512,128]{2,1,0:T(8,128)(2,1)} %pack.1), calls=%async_computation.1 | async-start | bytes 2097152 | tf_op jit(solution)/shard_map/all_to_all | solution.py:406
  39.4 0.6 copy-done.28
  40.1 18.2 %attend.2 = (bf16[8,128,128]{2,1,0:T(8,128)(2,1)}, f32[16,128,128]{2,1,0:T(8,128)}, bf16[4,128,128]{2,1,0:T(8,128)(2,1)}, bf16[4,128,128]{2,1,0:T(8,128)(2,1)}, bf16[4,128,128]{2,1,0:T(8,128)(2,1)}) custom-call(s32[192]{0:T(256)} %reshape_reshape.3.idx_ref, s32[1]{0:T(128)} %bitcast.h_ref, bf16[8,2,128,128]{3,2,1,0:T(8,128)(2,1)} %get-tuple-element.69.kv_ref, ...), custom_call_target="tpu_custom_call" | custom-call | flops 20132659200 | bytes 6291456 | tf_op jit(solution)/shard_map/attend/pallas_call | solution.py:248
  58.3 1.6 %collective-permute-start.13 = (bf16[4,128,128]{2,1,0:T(8,128)(2,1)}, bf16[4,128,128]{2,1,0:T(8,128)(2,1)S(1)}, u32[]{:S(2)}, u32[]{:S(2)}) collective-permute-start(bf16[4,128,128]{2,1,0:T(8,128)(2,1)} %get-tuple-element.75), channel_id=1, source_target_pairs={{0,8},{8,0},{16,24},{24,16},{1,9},{9,1},{17,25},{25,17},{2,10},{10... | collective-permute-start | bytes 393224 | tf_op jit(solution)/shard_map/ppermute | solution.py:371
  59.9 1.5 %collective-permute-start.14 = (bf16[4,128,128]{2,1,0:T(8,128)(2,1)}, bf16[4,128,128]{2,1,0:T(8,128)(2,1)S(1)}, u32[]{:S(2)}, u32[]{:S(2)}) collective-permute-start(bf16[4,128,128]{2,1,0:T(8,128)(2,1)} %get-tuple-element.76), channel_id=1, source_target_pairs={{0,16},{8,24},{16,0},{24,8},{1,17},{9,25},{17,1},{25,9},{2,18},{10... | collective-permute-start | bytes 393224 | tf_op jit(solution)/shard_map/ppermute | solution.py:371
  61.9 4.0 %all-to-all-done.1 = bf16[8,512,128]{2,1,0:T(8,128)(2,1)S(1)} async-done(((bf16[8,512,128]{2,1,0:T(8,128)(2,1)}), bf16[8,512,128]{2,1,0:T(8,128)(2,1)S(1)}, u32[]{:S(2)}, u32[]{:S(2)}) %all-to-all-start.1) | async-done | bytes 1048608 | tf_op jit(solution)/shard_map/all_to_all | solution.py:406
  65.8 1.0 copy-done
  66.8 2.0 %lend.2 = (bf16[4,128,128]{2,1,0:T(8,128)(2,1)}, bf16[4,128,128]{2,1,0:T(8,128)(2,1)}, bf16[4,128,128]{2,1,0:T(8,128)(2,1)}) custom-call(s32[16]{0:T(128)} %fusion.19.lists_ref, s32[1]{0:T(128)} %bitcast.h_ref, bf16[8,4,128,128]{3,2,1,0:T(8,128)(2,1)} %bitcast.13), custom_call_target="tpu_custom_call" | custom-call | bytes 2097152 | tf_op jit(solution)/shard_map/lend/pallas_call | solution.py:127
  68.9 1.5 %collective-permute-start.2 = (bf16[4,128,128]{2,1,0:T(8,128)(2,1)}, bf16[4,128,128]{2,1,0:T(8,128)(2,1)S(1)}, u32[]{:S(2)}, u32[]{:S(2)}) collective-permute-start(bf16[4,128,128]{2,1,0:T(8,128)(2,1)} %get-tuple-element.58), channel_id=1, source_target_pairs={{0,8},{8,0},{16,24},{24,16},{1,9},{9,1},{17,25},{25,17},{2,10},{10... | collective-permute-start | bytes 393224 | tf_op jit(solution)/shard_map/ppermute | solution.py:371
  70.4 1.5 %collective-permute-start.3 = (bf16[4,128,128]{2,1,0:T(8,128)(2,1)}, bf16[4,128,128]{2,1,0:T(8,128)(2,1)S(1)}, u32[]{:S(2)}, u32[]{:S(2)}) collective-permute-start(bf16[4,128,128]{2,1,0:T(8,128)(2,1)} %get-tuple-element.59), channel_id=1, source_target_pairs={{0,16},{8,24},{16,0},{24,8},{1,17},{9,25},{17,1},{25,9},{2,18},{10... | collective-permute-start | bytes 393224 | tf_op jit(solution)/shard_map/ppermute | solution.py:371
  73.1 2.5 %collect.2 = bf16[8,384,128]{2,1,0:T(8,128)(2,1)} custom-call(s32[16]{0:T(128)} %fusion.19.lists_ref, s32[1]{0:T(128)} %bitcast.h_ref, f32[16,128,128]{2,1,0:T(8,128)} %get-tuple-element.74.own, bf16[4,128,128]{2,1,0:T(8,128)(2,1)} %copy-done.4, bf16[4,128,128]{2,1,0:T(8,128)(2,1)} %copy-done.5, bf16[4,128,128]{2,1,0:T(8,128)(2,1)} %copy-done.7, ...), custom_call_target="tpu_custom_call" | custom-call | bytes 4194304 | tf_op jit(solution)/shard_map/collect/pallas_call | solution.py:299
  75.6 3.5 %all-to-all-start.2 = ((bf16[8,384,128]{2,1,0:T(8,128)(2,1)}), bf16[8,384,128]{2,1,0:T(8,128)(2,1)S(1)}, u32[]{:S(2)}, u32[]{:S(2)}) async-start(bf16[8,384,128]{2,1,0:T(8,128)(2,1)} %collect.2), calls=%async_computation.2 | async-start | bytes 1572864 | tf_op jit(solution)/shard_map/all_to_all | solution.py:406
  79.2 0.6 copy-done.26
  79.9 0.6 copy-done.29
  80.6 18.2 %attend.3 = (bf16[8,128,128]{2,1,0:T(8,128)(2,1)}, f32[16,128,128]{2,1,0:T(8,128)}, bf16[4,128,128]{2,1,0:T(8,128)(2,1)}, bf16[4,128,128]{2,1,0:T(8,128)(2,1)}, bf16[4,128,128]{2,1,0:T(8,128)(2,1)}) custom-call(s32[192]{0:T(256)} %reshape_reshape.3.idx_ref, s32[1]{0:T(128)} %bitcast.h_ref, bf16[8,4,128,128]{3,2,1,0:T(8,128)(2,1)} %bitcast.14, ...), custom_call_target="tpu_custom_call" | custom-call | flops 20132659200 | bytes 6291456 | tf_op jit(solution)/shard_map/attend/pallas_call | solution.py:248
  98.8 1.6 %collective-permute-start.16 = (bf16[4,128,128]{2,1,0:T(8,128)(2,1)}, bf16[4,128,128]{2,1,0:T(8,128)(2,1)S(1)}, u32[]{:S(2)}, u32[]{:S(2)}) collective-permute-start(bf16[4,128,128]{2,1,0:T(8,128)(2,1)} %get-tuple-element.83), channel_id=1, source_target_pairs={{0,8},{8,0},{16,24},{24,16},{1,9},{9,1},{17,25},{25,17},{2,10},{10... | collective-permute-start | bytes 393224 | tf_op jit(solution)/shard_map/ppermute | solution.py:371
  100.4 1.5 %collective-permute-start.17 = (bf16[4,128,128]{2,1,0:T(8,128)(2,1)}, bf16[4,128,128]{2,1,0:T(8,128)(2,1)S(1)}, u32[]{:S(2)}, u32[]{:S(2)}) collective-permute-start(bf16[4,128,128]{2,1,0:T(8,128)(2,1)} %get-tuple-element.84), channel_id=1, source_target_pairs={{0,16},{8,24},{16,0},{24,8},{1,17},{9,25},{17,1},{25,9},{2,18},{10... | collective-permute-start | bytes 393224 | tf_op jit(solution)/shard_map/ppermute | solution.py:371
  102.4 2.9 %collective-permute-done.16.refs_0_ = bf16[4,128,128]{2,1,0:T(8,128)(2,1)S(1)} collective-permute-done((bf16[4,128,128]{2,1,0:T(8,128)(2,1)}, bf16[4,128,128]{2,1,0:T(8,128)(2,1)S(1)}, u32[]{:S(2)}, u32[]{:S(2)}) %collective-permute-start.16) | collective-permute-done | bytes 131104 | tf_op jit(solution)/shard_map/ppermute | solution.py:371
  105.3 3.6 %collective-permute-done.17.refs_1_ = bf16[4,128,128]{2,1,0:T(8,128)(2,1)S(1)} collective-permute-done((bf16[4,128,128]{2,1,0:T(8,128)(2,1)}, bf16[4,128,128]{2,1,0:T(8,128)(2,1)S(1)}, u32[]{:S(2)}, u32[]{:S(2)}) %collective-permute-start.17) | collective-permute-done | bytes 131104 | tf_op jit(solution)/shard_map/ppermute | solution.py:371
  108.9 4.8 %all-to-all-start.3 = ((bf16[8,128,128]{2,1,0:T(8,128)(2,1)}), bf16[8,128,128]{2,1,0:T(8,128)(2,1)S(1)}, u32[]{:S(2)}, u32[]{:S(2)}) async-start(bf16[8,128,128]{2,1,0:T(8,128)(2,1)} %get-tuple-element.87), calls=%async_computation.3 | async-start | bytes 524288 | tf_op jit(solution)/shard_map/all_to_all | solution.py:406
  113.7 2.3 %collect.3 = (bf16[256,128]{1,0:T(8,128)(2,1)}, bf16[256,128]{1,0:T(8,128)(2,1)}, bf16[256,128]{1,0:T(8,128)(2,1)}, bf16[256,128]{1,0:T(8,128)(2,1)}, bf16[256,1...) custom-call(s32[16]{0:T(128)} %fusion.19.lists_ref, ...), custom_call_target="tpu_custom_call" | custom-call | bytes 4194304 | tf_op jit(solution)/shard_map/collect/pallas_call | solution.py:299
  116.0 0.6 collective-permute-start.19
  116.6 1.7 %collective-permute-start.20 = (bf16[256,128]{1,0:T(8,128)(2,1)}, bf16[256,128]{1,0:T(8,128)(2,1)S(1)}, u32[]{:S(2)}, u32[]{:S(2)}) collective-permute-start(bf16[256,128]{1,0:T(8,128)(2,1)} %get-tuple-element.95), channel_id=1, source_target_pairs={{0,2},{1,3},{2,0},{3,1},{4,6},{5,7},{6,4},{7,5},{8,10},{9,11},{10,... | collective-permute-start | bytes 196616 | tf_op jit(solution)/shard_map/ppermute | solution.py:371
  118.2 2.6 %collective-permute-start.22 = (bf16[256,128]{1,0:T(8,128)(2,1)}, bf16[256,128]{1,0:T(8,128)(2,1)S(1)}, u32[]{:S(2)}, u32[]{:S(2)}) collective-permute-start(bf16[256,128]{1,0:T(8,128)(2,1)} %get-tuple-element.97), channel_id=1, source_target_pairs={{0,4},{1,5},{2,6},{3,7},{4,0},{5,1},{6,2},{7,3},{8,12},{9,13},{10,... | collective-permute-start | bytes 196616 | tf_op jit(solution)/shard_map/ppermute | solution.py:371
  121.0 3.5 %collective-permute-start.24 = (bf16[256,128]{1,0:T(8,128)(2,1)}, bf16[256,128]{1,0:T(8,128)(2,1)S(1)}, u32[]{:S(2)}, u32[]{:S(2)}) collective-permute-start(bf16[256,128]{1,0:T(8,128)(2,1)} %get-tuple-element.99), channel_id=1, source_target_pairs={{0,6},{1,7},{2,4},{3,5},{4,2},{5,3},{6,0},{7,1},{8,14},{9,15},{10,... | collective-permute-start | bytes 196616 | tf_op jit(solution)/shard_map/ppermute | solution.py:371
  124.4 1.3 collective-permute-done.20.refs_2_
  125.8 0.7 copy-done.2
  126.5 2.6 %unpack_early.1 = (bf16[256,1024]{1,0:T(8,128)(2,1)}, bf16[256,1024]{1,0:T(8,128)(2,1)}, bf16[256,1024]{1,0:T(8,128)(2,1)}) custom-call(bf16[8,384,128]{2,1,0:T(8,128)(2,1)} %copy-done.1, bf16[8,128,128]{2,1,0:T(8,128)(2,1)} %copy-done.2), custom_call_target="tpu_custom_call" | custom-call | bytes 8388608 | tf_op jit(solution)/shard_map/unpack_early/pallas_call | solution.py:346
  129.1 2.5 %collective-permute-done.23.refs_5_ = bf16[256,128]{1,0:T(8,128)(2,1)S(1)} collective-permute-done((bf16[256,128]{1,0:T(8,128)(2,1)}, bf16[256,128]{1,0:T(8,128)(2,1)S(1)}, u32[]{:S(2)}, u32[]{:S(2)}) %collective-permute-start.23) | collective-permute-done | bytes 65568 | tf_op jit(solution)/shard_map/ppermute | solution.py:371
  131.7 0.6 copy-done.14
  132.3 2.0 %unpack_last.1 = (bf16[256,1024]{1,0:T(8,128)(2,1)}, bf16[256,1024]{1,0:T(8,128)(2,1)}) custom-call(s32[1]{0:T(128)} %bitcast.h_ref, bf16[256,128]{1,0:T(8,128)(2,1)} %get-tuple-element.93.refs_0_, bf16[256,128]{1,0:T(8,128)(2,1)} %copy-done.10, bf16[256,128]{1,0:T(8,128)(2,1)} %copy-done.11, ...), custom_call_target="tpu_custom_call", output_to_operand_aliasing={{0}: (9, {}), {1}: (10, {})} | custom-call | bytes 2097152 | tf_op jit(solution)/shard_map/unpack_last/pallas_call | solution.py:356
  (107 shorter events, 5.1 us)
Async XLA Ops:
  2.8 9.5 %collective-permute-start = (bf16[256,128]{1,0:T(8,128)(2,1)}, bf16[256,128]{1,0:T(8,128)(2,1)S(1)}, u32[]{:S(2)}, u32[]{:S(2)}) collective-permute-start(bf16[256,128]{1,0:T(8,128)(2,1)} %get-tuple-element.54), channel_id=1, source_target_pairs={{0,1},{1,0},{2,3},{3,2},{4,5},{5,4},{6,7},{7,6},{8,9},{9,8},{10,11... | collective-permute-start | bytes 196616 | tf_op jit(solution)/shard_map/ppermute | solution.py:371
  3.2 12.4 %collective-permute-start.1 = (bf16[256,128]{1,0:T(8,128)(2,1)}, bf16[256,128]{1,0:T(8,128)(2,1)S(1)}, u32[]{:S(2)}, u32[]{:S(2)}) collective-permute-start(bf16[256,128]{1,0:T(8,128)(2,1)} %get-tuple-element.55), channel_id=1, source_target_pairs={{0,2},{1,3},{2,0},{3,1},{4,6},{5,7},{6,4},{7,5},{8,10},{9,11},{10,... | collective-permute-start | bytes 196616 | tf_op jit(solution)/shard_map/ppermute | solution.py:371
  5.8 18.4 %collective-permute-start.8 = (bf16[256,128]{1,0:T(8,128)(2,1)}, bf16[256,128]{1,0:T(8,128)(2,1)S(1)}, u32[]{:S(2)}, u32[]{:S(2)}) collective-permute-start(bf16[256,128]{1,0:T(8,128)(2,1)} %get-tuple-element.67), channel_id=1, source_target_pairs={{0,6},{1,7},{2,4},{3,5},{4,2},{5,3},{6,0},{7,1},{8,14},{9,15},{10,... | collective-permute-start | bytes 196616 | tf_op jit(solution)/shard_map/ppermute | solution.py:371
  8.3 0.9 copy-start.24
  8.3 15.9 %collective-permute-start.9 = (bf16[256,128]{1,0:T(8,128)(2,1)}, bf16[256,128]{1,0:T(8,128)(2,1)S(1)}, u32[]{:S(2)}, u32[]{:S(2)}) collective-permute-start(bf16[256,128]{1,0:T(8,128)(2,1)} %get-tuple-element.68), channel_id=1, source_target_pairs={{0,7},{1,6},{2,5},{3,4},{4,3},{5,2},{6,1},{7,0},{8,15},{9,14},{10,... | collective-permute-start | bytes 196616 | tf_op jit(solution)/shard_map/ppermute | solution.py:371
  9.2 15.1 %collective-permute-start.5 = (bf16[256,128]{1,0:T(8,128)(2,1)}, bf16[256,128]{1,0:T(8,128)(2,1)S(1)}, u32[]{:S(2)}, u32[]{:S(2)}) collective-permute-start(bf16[256,128]{1,0:T(8,128)(2,1)} %get-tuple-element.64), channel_id=1, source_target_pairs={{0,3},{1,2},{2,1},{3,0},{4,7},{5,6},{6,5},{7,4},{8,11},{9,10},{10,... | collective-permute-start | bytes 196616 | tf_op jit(solution)/shard_map/ppermute | solution.py:371
  9.2 3.0 %copy-start.33 = (bf16[256,128]{1,0:T(8,128)(2,1)S(1)}, bf16[256,128]{1,0:T(8,128)(2,1)}, u32[]{:S(2)}) copy-start(bf16[256,128]{1,0:T(8,128)(2,1)} %get-tuple-element.65) | copy-start | bytes 196612
  9.2 6.3 %copy-start.32 = (bf16[256,128]{1,0:T(8,128)(2,1)S(1)}, bf16[256,128]{1,0:T(8,128)(2,1)}, u32[]{:S(2)}) copy-start(bf16[256,128]{1,0:T(8,128)(2,1)} %get-tuple-element.66) | copy-start | bytes 196612
  12.2 3.4 %copy-start.17 = (bf16[256,128]{1,0:T(8,128)(2,1)}, bf16[256,128]{1,0:T(8,128)(2,1)S(1)}, u32[]{:S(2)}) copy-start(bf16[256,128]{1,0:T(8,128)(2,1)S(1)} %collective-permute-done) | copy-start | bytes 196612
  12.3 12.0 %collective-permute-start.6 = (bf16[256,128]{1,0:T(8,128)(2,1)S(1)}, bf16[256,128]{1,0:T(8,128)(2,1)S(1)}, u32[]{:S(2)}, u32[]{:S(2)}) collective-permute-start(bf16[256,128]{1,0:T(8,128)(2,1)S(1)} %copy-done.33), channel_id=1, source_target_pairs={{0,4},{1,5},{2,6},{3,7},{4,0},{5,1},{6,2},{7,3},{8,12},{9,13},{10,... | collective-permute-start | bytes 196616 | tf_op jit(solution)/shard_map/ppermute | solution.py:371
  15.6 8.7 %collective-permute-start.7 = (bf16[256,128]{1,0:T(8,128)(2,1)S(1)}, bf16[256,128]{1,0:T(8,128)(2,1)S(1)}, u32[]{:S(2)}, u32[]{:S(2)}) collective-permute-start(bf16[256,128]{1,0:T(8,128)(2,1)S(1)} %copy-done.32), channel_id=1, source_target_pairs={{0,5},{1,4},{2,7},{3,6},{4,1},{5,0},{6,3},{7,2},{8,13},{9,12},{10,... | collective-permute-start | bytes 196616 | tf_op jit(solution)/shard_map/ppermute | solution.py:371
  16.2 18.8 %all-to-all-start = ((bf16[8,256,128]{2,1,0:T(8,128)(2,1)}), bf16[8,256,128]{2,1,0:T(8,128)(2,1)S(1)}, u32[]{:S(2)}, u32[]{:S(2)}) async-start(bf16[8,256,128]{2,1,0:T(8,128)(2,1)} %pack_one.1), calls=%async_computation | async-start | bytes 1048576 | tf_op jit(solution)/shard_map/all_to_all | solution.py:406
  22.7 0.8 copy-start.25
  26.9 12.4 %collective-permute-start.10 = (bf16[4,128,128]{2,1,0:T(8,128)(2,1)}, bf16[4,128,128]{2,1,0:T(8,128)(2,1)S(1)}, u32[]{:S(2)}, u32[]{:S(2)}) collective-permute-start(bf16[4,128,128]{2,1,0:T(8,128)(2,1)} %get-tuple-element.71), channel_id=1, source_target_pairs={{0,8},{8,0},{16,24},{24,16},{1,9},{9,1},{17,25},{25,17},{2,10},{10... | collective-permute-start | bytes 393224 | tf_op jit(solution)/shard_map/ppermute | solution.py:371
  28.5 10.9 %collective-permute-start.11 = (bf16[4,128,128]{2,1,0:T(8,128)(2,1)}, bf16[4,128,128]{2,1,0:T(8,128)(2,1)S(1)}, u32[]{:S(2)}, u32[]{:S(2)}) collective-permute-start(bf16[4,128,128]{2,1,0:T(8,128)(2,1)} %get-tuple-element.72), channel_id=1, source_target_pairs={{0,16},{8,24},{16,0},{24,8},{1,17},{9,25},{17,1},{25,9},{2,18},{10... | collective-permute-start | bytes 393224 | tf_op jit(solution)/shard_map/ppermute | solution.py:371
  30.0 9.4 %collective-permute-start.12 = (bf16[4,128,128]{2,1,0:T(8,128)(2,1)}, bf16[4,128,128]{2,1,0:T(8,128)(2,1)S(1)}, u32[]{:S(2)}, u32[]{:S(2)}) collective-permute-start(bf16[4,128,128]{2,1,0:T(8,128)(2,1)} %get-tuple-element.73), channel_id=1, source_target_pairs={{0,24},{8,16},{16,8},{24,0},{1,25},{9,17},{17,9},{25,1},{2,26},{10... | collective-permute-start | bytes 393224 | tf_op jit(solution)/shard_map/ppermute | solution.py:371
  35.0 0.8 copy-start.3
  35.8 30.1 %all-to-all-start.1 = ((bf16[8,512,128]{2,1,0:T(8,128)(2,1)}), bf16[8,512,128]{2,1,0:T(8,128)(2,1)S(1)}, u32[]{:S(2)}, u32[]{:S(2)}) async-start(bf16[8,512,128]{2,1,0:T(8,128)(2,1)} %pack.1), calls=%async_computation.1 | async-start | bytes 2097152 | tf_op jit(solution)/shard_map/all_to_all | solution.py:406
  39.3 0.7 copy-start.30
  39.4 0.7 copy-start.31
  58.3 13.6 %collective-permute-start.13 = (bf16[4,128,128]{2,1,0:T(8,128)(2,1)}, bf16[4,128,128]{2,1,0:T(8,128)(2,1)S(1)}, u32[]{:S(2)}, u32[]{:S(2)}) collective-permute-start(bf16[4,128,128]{2,1,0:T(8,128)(2,1)} %get-tuple-element.75), channel_id=1, source_target_pairs={{0,8},{8,0},{16,24},{24,16},{1,9},{9,1},{17,25},{25,17},{2,10},{10... | collective-permute-start | bytes 393224 | tf_op jit(solution)/shard_map/ppermute | solution.py:371
  59.9 12.5 %collective-permute-start.14 = (bf16[4,128,128]{2,1,0:T(8,128)(2,1)}, bf16[4,128,128]{2,1,0:T(8,128)(2,1)S(1)}, u32[]{:S(2)}, u32[]{:S(2)}) collective-permute-start(bf16[4,128,128]{2,1,0:T(8,128)(2,1)} %get-tuple-element.76), channel_id=1, source_target_pairs={{0,16},{8,24},{16,0},{24,8},{1,17},{9,25},{17,1},{25,9},{2,18},{10... | collective-permute-start | bytes 393224 | tf_op jit(solution)/shard_map/ppermute | solution.py:371
  61.4 11.0 %collective-permute-start.15 = (bf16[4,128,128]{2,1,0:T(8,128)(2,1)}, bf16[4,128,128]{2,1,0:T(8,128)(2,1)S(1)}, u32[]{:S(2)}, u32[]{:S(2)}) collective-permute-start(bf16[4,128,128]{2,1,0:T(8,128)(2,1)} %get-tuple-element.77), channel_id=1, source_target_pairs={{0,24},{8,16},{16,8},{24,0},{1,25},{9,17},{17,9},{25,1},{2,26},{10... | collective-permute-start | bytes 393224 | tf_op jit(solution)/shard_map/ppermute | solution.py:371
  65.8 1.0 copy-start
  68.9 10.3 %collective-permute-start.2 = (bf16[4,128,128]{2,1,0:T(8,128)(2,1)}, bf16[4,128,128]{2,1,0:T(8,128)(2,1)S(1)}, u32[]{:S(2)}, u32[]{:S(2)}) collective-permute-start(bf16[4,128,128]{2,1,0:T(8,128)(2,1)} %get-tuple-element.58), channel_id=1, source_target_pairs={{0,8},{8,0},{16,24},{24,16},{1,9},{9,1},{17,25},{25,17},{2,10},{10... | collective-permute-start | bytes 393224 | tf_op jit(solution)/shard_map/ppermute | solution.py:371
  70.4 8.8 %collective-permute-start.3 = (bf16[4,128,128]{2,1,0:T(8,128)(2,1)}, bf16[4,128,128]{2,1,0:T(8,128)(2,1)S(1)}, u32[]{:S(2)}, u32[]{:S(2)}) collective-permute-start(bf16[4,128,128]{2,1,0:T(8,128)(2,1)} %get-tuple-element.59), channel_id=1, source_target_pairs={{0,16},{8,24},{16,0},{24,8},{1,17},{9,25},{17,1},{25,9},{2,18},{10... | collective-permute-start | bytes 393224 | tf_op jit(solution)/shard_map/ppermute | solution.py:371
  71.9 7.3 %collective-permute-start.4 = (bf16[4,128,128]{2,1,0:T(8,128)(2,1)}, bf16[4,128,128]{2,1,0:T(8,128)(2,1)S(1)}, u32[]{:S(2)}, u32[]{:S(2)}) collective-permute-start(bf16[4,128,128]{2,1,0:T(8,128)(2,1)} %get-tuple-element.60), channel_id=1, source_target_pairs={{0,24},{8,16},{16,8},{24,0},{1,25},{9,17},{17,9},{25,1},{2,26},{10... | collective-permute-start | bytes 393224 | tf_op jit(solution)/shard_map/ppermute | solution.py:371
  75.6 26.7 %all-to-all-start.2 = ((bf16[8,384,128]{2,1,0:T(8,128)(2,1)}), bf16[8,384,128]{2,1,0:T(8,128)(2,1)S(1)}, u32[]{:S(2)}, u32[]{:S(2)}) async-start(bf16[8,384,128]{2,1,0:T(8,128)(2,1)} %collect.2), calls=%async_computation.2 | async-start | bytes 1572864 | tf_op jit(solution)/shard_map/all_to_all | solution.py:406
  98.8 6.5 %collective-permute-start.16 = (bf16[4,128,128]{2,1,0:T(8,128)(2,1)}, bf16[4,128,128]{2,1,0:T(8,128)(2,1)S(1)}, u32[]{:S(2)}, u32[]{:S(2)}) collective-permute-start(bf16[4,128,128]{2,1,0:T(8,128)(2,1)} %get-tuple-element.83), channel_id=1, source_target_pairs={{0,8},{8,0},{16,24},{24,16},{1,9},{9,1},{17,25},{25,17},{2,10},{10... | collective-permute-start | bytes 393224 | tf_op jit(solution)/shard_map/ppermute | solution.py:371
  100.4 8.5 %collective-permute-start.17 = (bf16[4,128,128]{2,1,0:T(8,128)(2,1)}, bf16[4,128,128]{2,1,0:T(8,128)(2,1)S(1)}, u32[]{:S(2)}, u32[]{:S(2)}) collective-permute-start(bf16[4,128,128]{2,1,0:T(8,128)(2,1)} %get-tuple-element.84), channel_id=1, source_target_pairs={{0,16},{8,24},{16,0},{24,8},{1,17},{9,25},{17,1},{25,9},{2,18},{10... | collective-permute-start | bytes 393224 | tf_op jit(solution)/shard_map/ppermute | solution.py:371
  101.9 7.0 %collective-permute-start.18 = (bf16[4,128,128]{2,1,0:T(8,128)(2,1)}, bf16[4,128,128]{2,1,0:T(8,128)(2,1)S(1)}, u32[]{:S(2)}, u32[]{:S(2)}) collective-permute-start(bf16[4,128,128]{2,1,0:T(8,128)(2,1)} %get-tuple-element.85), channel_id=1, source_target_pairs={{0,24},{8,16},{16,8},{24,0},{1,25},{9,17},{17,9},{25,1},{2,26},{10... | collective-permute-start | bytes 393224 | tf_op jit(solution)/shard_map/ppermute | solution.py:371
  102.4 13.6 %copy-start.1 = (bf16[8,384,128]{2,1,0:T(8,128)(2,1)}, bf16[8,384,128]{2,1,0:T(8,128)(2,1)S(1)}, u32[]{:S(2)}) copy-start(bf16[8,384,128]{2,1,0:T(8,128)(2,1)S(1)} %all-to-all-done.2.refs_0_) | copy-start | bytes 2359300
  105.3 8.4 %copy-start.6 = (bf16[4,128,128]{2,1,0:T(8,128)(2,1)}, bf16[4,128,128]{2,1,0:T(8,128)(2,1)S(1)}, u32[]{:S(2)}) copy-start(bf16[4,128,128]{2,1,0:T(8,128)(2,1)S(1)} %collective-permute-done.16.refs_0_) | copy-start | bytes 393220
  108.9 4.8 %copy-start.8 = (bf16[4,128,128]{2,1,0:T(8,128)(2,1)}, bf16[4,128,128]{2,1,0:T(8,128)(2,1)S(1)}, u32[]{:S(2)}) copy-start(bf16[4,128,128]{2,1,0:T(8,128)(2,1)S(1)} %collective-permute-done.17.refs_1_) | copy-start | bytes 393220
  108.9 4.8 %copy-start.9 = (bf16[4,128,128]{2,1,0:T(8,128)(2,1)}, bf16[4,128,128]{2,1,0:T(8,128)(2,1)S(1)}, u32[]{:S(2)}) copy-start(bf16[4,128,128]{2,1,0:T(8,128)(2,1)S(1)} %collective-permute-done.18.refs_2_) | copy-start | bytes 393220
  108.9 16.8 %all-to-all-start.3 = ((bf16[8,128,128]{2,1,0:T(8,128)(2,1)}), bf16[8,128,128]{2,1,0:T(8,128)(2,1)S(1)}, u32[]{:S(2)}, u32[]{:S(2)}) async-start(bf16[8,128,128]{2,1,0:T(8,128)(2,1)} %get-tuple-element.87), calls=%async_computation.3 | async-start | bytes 524288 | tf_op jit(solution)/shard_map/all_to_all | solution.py:406
  116.0 4.9 %collective-permute-start.19 = (bf16[256,128]{1,0:T(8,128)(2,1)}, bf16[256,128]{1,0:T(8,128)(2,1)S(1)}, u32[]{:S(2)}, u32[]{:S(2)}) collective-permute-start(bf16[256,128]{1,0:T(8,128)(2,1)} %get-tuple-element.94), channel_id=1, source_target_pairs={{0,1},{1,0},{2,3},{3,2},{4,5},{5,4},{6,7},{7,6},{8,9},{9,8},{10,11... | collective-permute-start | bytes 196616 | tf_op jit(solution)/shard_map/ppermute | solution.py:371
  116.6 9.2 %collective-permute-start.20 = (bf16[256,128]{1,0:T(8,128)(2,1)}, bf16[256,128]{1,0:T(8,128)(2,1)S(1)}, u32[]{:S(2)}, u32[]{:S(2)}) collective-permute-start(bf16[256,128]{1,0:T(8,128)(2,1)} %get-tuple-element.95), channel_id=1, source_target_pairs={{0,2},{1,3},{2,0},{3,1},{4,6},{5,7},{6,4},{7,5},{8,10},{9,11},{10,... | collective-permute-start | bytes 196616 | tf_op jit(solution)/shard_map/ppermute | solution.py:371
  118.2 10.9 %collective-permute-start.21 = (bf16[256,128]{1,0:T(8,128)(2,1)}, bf16[256,128]{1,0:T(8,128)(2,1)S(1)}, u32[]{:S(2)}, u32[]{:S(2)}) collective-permute-start(bf16[256,128]{1,0:T(8,128)(2,1)} %get-tuple-element.96), channel_id=1, source_target_pairs={{0,3},{1,2},{2,1},{3,0},{4,7},{5,6},{6,5},{7,4},{8,11},{9,10},{10,... | collective-permute-start | bytes 196616 | tf_op jit(solution)/shard_map/ppermute | solution.py:371
  118.2 10.9 %collective-permute-start.22 = (bf16[256,128]{1,0:T(8,128)(2,1)}, bf16[256,128]{1,0:T(8,128)(2,1)S(1)}, u32[]{:S(2)}, u32[]{:S(2)}) collective-permute-start(bf16[256,128]{1,0:T(8,128)(2,1)} %get-tuple-element.97), channel_id=1, source_target_pairs={{0,4},{1,5},{2,6},{3,7},{4,0},{5,1},{6,2},{7,3},{8,12},{9,13},{10,... | collective-permute-start | bytes 196616 | tf_op jit(solution)/shard_map/ppermute | solution.py:371
  120.8 10.8 %collective-permute-start.23 = (bf16[256,128]{1,0:T(8,128)(2,1)}, bf16[256,128]{1,0:T(8,128)(2,1)S(1)}, u32[]{:S(2)}, u32[]{:S(2)}) collective-permute-start(bf16[256,128]{1,0:T(8,128)(2,1)} %get-tuple-element.98), channel_id=1, source_target_pairs={{0,5},{1,4},{2,7},{3,6},{4,1},{5,0},{6,3},{7,2},{8,13},{9,12},{10,... | collective-permute-start | bytes 196616 | tf_op jit(solution)/shard_map/ppermute | solution.py:371
  121.0 8.1 %copy-start.10 = (bf16[256,128]{1,0:T(8,128)(2,1)}, bf16[256,128]{1,0:T(8,128)(2,1)S(1)}, u32[]{:S(2)}) copy-start(bf16[256,128]{1,0:T(8,128)(2,1)S(1)} %collective-permute-done.19.refs_1_) | copy-start | bytes 196612
  121.0 10.7 %collective-permute-start.24 = (bf16[256,128]{1,0:T(8,128)(2,1)}, bf16[256,128]{1,0:T(8,128)(2,1)S(1)}, u32[]{:S(2)}, u32[]{:S(2)}) collective-permute-start(bf16[256,128]{1,0:T(8,128)(2,1)} %get-tuple-element.99), channel_id=1, source_target_pairs={{0,6},{1,7},{2,4},{3,5},{4,2},{5,3},{6,0},{7,1},{8,14},{9,15},{10,... | collective-permute-start | bytes 196616 | tf_op jit(solution)/shard_map/ppermute | solution.py:371
  125.7 3.3 %copy-start.11 = (bf16[256,128]{1,0:T(8,128)(2,1)}, bf16[256,128]{1,0:T(8,128)(2,1)S(1)}, u32[]{:S(2)}) copy-start(bf16[256,128]{1,0:T(8,128)(2,1)S(1)} %collective-permute-done.20.refs_2_) | copy-start | bytes 196612
  125.8 5.9 %collective-permute-start.25 = (bf16[256,128]{1,0:T(8,128)(2,1)}, bf16[256,128]{1,0:T(8,128)(2,1)S(1)}, u32[]{:S(2)}, u32[]{:S(2)}) collective-permute-start(bf16[256,128]{1,0:T(8,128)(2,1)} %get-tuple-element.100), channel_id=1, source_target_pairs={{0,7},{1,6},{2,5},{3,4},{4,3},{5,2},{6,1},{7,0},{8,15},{9,14},{10,... | collective-permute-start | bytes 196616 | tf_op jit(solution)/shard_map/ppermute | solution.py:371
  125.8 0.7 copy-start.2
  129.1 2.5 %copy-start.12 = (bf16[256,128]{1,0:T(8,128)(2,1)}, bf16[256,128]{1,0:T(8,128)(2,1)S(1)}, u32[]{:S(2)}) copy-start(bf16[256,128]{1,0:T(8,128)(2,1)S(1)} %collective-permute-done.21.refs_3_) | copy-start | bytes 196612
  129.1 2.5 %copy-start.13 = (bf16[256,128]{1,0:T(8,128)(2,1)}, bf16[256,128]{1,0:T(8,128)(2,1)S(1)}, u32[]{:S(2)}) copy-start(bf16[256,128]{1,0:T(8,128)(2,1)S(1)} %collective-permute-done.22.refs_4_) | copy-start | bytes 196612
  (16 other events, 10.3 us)

commit v5 on v4

--- a/solution.py
+++ b/solution.py
@@ -141,30 +141,21 @@
     borrowed, refs = refs[: parts - 1], refs[parts - 1 :]
     dq_out, own_ref, refs = refs[0], refs[1], refs[2:]
     back = refs[: parts - 1]
-    tab, qg_tab, kt_tab, acc, s_buf, dp_buf, sem = refs[parts - 1 :]
+    tab, kt_tab, acc, s_buf, dp_buf = refs[parts - 1 :]
     nblk = n * bpd
     slots = (parts - 1) * cap
-    copies = []
+
+    def enter(t, block):
+        tab[t] = block
+        kt_tab[t] = block.astype(f32).T[:HD].astype(bf16)
+
+    acc[...] = jnp.zeros_like(acc)
     for k in range(n):
-        j = k if paired else k ^ h
-        src = qg.at[k ^ h] if paired else kv_ref.at[j, pl.ds(bpd, bpd)]
-        copies.append(pltpu.make_async_copy(kv_ref.at[j, pl.ds(0, bpd)], tab.at[pl.ds(k * bpd, bpd)], sem.at[k]))
-        copies.append(pltpu.make_async_copy(src, qg_tab.at[pl.ds(k * bpd, bpd)], sem.at[n + parts + k]))
+        for b in range(bpd):
+            enter(k * bpd + b, kv_ref[k if paired else k ^ h, b])
     for k in range(1, parts):
-        copies.append(
-            pltpu.make_async_copy(borrowed[k - 1], tab.at[pl.ds(nblk + (k - 1) * cap, cap)], sem.at[n + k])
-        )
-    for c in copies:
-        c.start()
-    acc[...] = jnp.zeros_like(acc)
-    for c in copies:
-        c.wait()
-
-    def flip(t, _):
-        kt_tab[t] = tab[t].astype(f32).T[:HD].astype(bf16)
-        return 0
-
-    lax.fori_loop(0, nblk + slots, flip, 0, unroll=4)
+        for b in range(cap):
+            enter(nblk + (k - 1) * cap + b, borrowed[k - 1][b])
     lane = lax.broadcasted_iota(jnp.int32, (BS, 2 * HD), 1)
     low = lane < HD
     zero = jnp.zeros((BS, 2 * HD), bf16)
@@ -173,8 +164,9 @@
         return op(x.reshape(BS // 8, 8, BS), axis=0)
 
     def load(r):
-        qg = qg_tab[r]
-        both = jnp.concatenate([jnp.where(low, qg, zero), jnp.where(low, zero, qg)], 0)
+        at, row = lax.div(r, bpd) ^ h, lax.rem(r, bpd)
+        block = qg[at, row] if paired else kv_ref[at, bpd + row]
+        both = jnp.concatenate([jnp.where(low, block, zero), jnp.where(low, zero, block)], 0)
         return both, [idx_ref[r * NBR + i] for i in range(NBR)]
 
     def step1(slot, both, where, i, top):
@@ -256,12 +248,10 @@
         out_specs=[VMEM] * (1 + parts),
         scratch_shapes=[
             pltpu.VMEM((nblk + slots, BS, width), bf16),
-            pltpu.VMEM((nblk, BS, width), bf16),
             pltpu.VMEM((nblk + slots, HD, BS), bf16),
             pltpu.VMEM((nblk + slots, BS, width), f32),
             pltpu.VMEM((bpd, NBR, BS, BS), f32),
             pltpu.VMEM((bpd, NBR, BS, BS), f32),
-            pltpu.SemaphoreType.DMA((2 * n + parts,)),
         ],
         compiler_params=params(),
         cost_estimate=cost(nblk * NBR * BS * BS * HD * 100, 6 << 20),

time: 136 us -> 133 us (0.978)
  Pallas kernels: 57.3 us -> 52.2 us
  waiting for transfers between devices: 18.3 us -> 20.8 us
    pallas_call x2, Pallas kernels: 36.5 us -> 31.5 us  [attend(): pl.pallas_call(functools.partial(attend_kernel, bool(qg), parts, cap, n,...]
    all_to_all x4, waiting for transfers between devices: 7.86 us -> 10.7 us  [spread(): return lax.all_to_all(x, 'head', split_axis=0, concat_axis=0, tiled=True)]
  transfers between devices with their start and end apart: 30 -> 30, of which waited for: 6 -> 7; matrix products, arithmetic and copies ran while one was open for 2% -> 2% of each run, Pallas kernels for 40% -> 37%
where the time goes in v5:
time: 133 us; the launch traced here: 132 us
  Pallas kernels  52.2 us (39%)
  starting transfers between devices  47.6 us (36%)
  waiting for transfers between devices  20.8 us (16%)
  local copies, waits for them, and re-layouts  8.48 us (6%)
  other arithmetic  1.6 us (1%)
    ppermute x26, starting transfers between devices, swap(): return lax.ppermute(x, axis, [(i, i ^ k) for i in range(size)])  32.2 us
    pallas_call x2, Pallas kernels, attend(): pl.pallas_call(functools.partial(attend_kernel, bool(qg), parts, cap, n,...  31.5 us
    all_to_all x4, starting transfers between devices, spread(): return lax.all_to_all(x, 'head', split_axis=0, concat_axis=0, tiled=True)  15.4 us
    all_to_all x4, waiting for transfers between devices, spread(): return lax.all_to_all(x, 'head', split_axis=0, concat_axis=0, tiled=True)  10.7 us
    ppermute x26, waiting for transfers between devices, swap(): return lax.ppermute(x, axis, [(i, i ^ k) for i in range(size)])  10.1 us
    unnamed x68, local copies, waits for them, and re-layouts  7.07 us
    pallas_call x2, Pallas kernels, collect(): pl.pallas_call(functools.partial(collect_kernel, last, parts, cap, n, bpd...  4.82 us
    pallas_call x2, Pallas kernels, lend(): pl.pallas_call(functools.partial(lend_kernel, parts, cap, bpd), out_shape...  4.07 us
  transfers between devices with their start and end apart: 30, of which 7 were waited for; matrix products, arithmetic and copies ran while one was open for 2% of the time, Pallas kernels for 37%

profile of v5, /device:TPU:0, one launch (start us, length us, event | category | flops | bytes accessed | tf_op | source)
XLA Modules:
  0.0 131.7 jit_solution(14295255404808292090)
XLA Ops:
  0.6 2.1 %pieces.1 = (bf16[256,128]{1,0:T(8,128)(2,1)}, bf16[256,128]{1,0:T(8,128)(2,1)}, bf16[256,128]{1,0:T(8,128)(2,1)}, bf16[256,128]{1,0:T(8,128)(2,1)}, bf16[256,12...) custom-call(s32[1]{0:T(128)} %bitcast.h_ref, ...), custom_call_target="tpu_custom_call" | custom-call | bytes 2097152 | tf_op jit(solution)/shard_map/pieces/pallas_call | solution.py:98
  3.2 2.6 %collective-permute-start.1 = (bf16[256,128]{1,0:T(8,128)(2,1)}, bf16[256,128]{1,0:T(8,128)(2,1)S(1)}, u32[]{:S(2)}, u32[]{:S(2)}) collective-permute-start(bf16[256,128]{1,0:T(8,128)(2,1)} %get-tuple-element.55), channel_id=1, source_target_pairs={{0,2},{1,3},{2,0},{3,1},{4,6},{5,7},{6,4},{7,5},{8,10},{9,11},{10,... | collective-permute-start | bytes 196616 | tf_op jit(solution)/shard_map/ppermute | solution.py:361
  5.8 2.5 %collective-permute-start.8 = (bf16[256,128]{1,0:T(8,128)(2,1)}, bf16[256,128]{1,0:T(8,128)(2,1)S(1)}, u32[]{:S(2)}, u32[]{:S(2)}) collective-permute-start(bf16[256,128]{1,0:T(8,128)(2,1)} %get-tuple-element.67), channel_id=1, source_target_pairs={{0,6},{1,7},{2,4},{3,5},{4,2},{5,3},{6,0},{7,1},{8,14},{9,15},{10,... | collective-permute-start | bytes 196616 | tf_op jit(solution)/shard_map/ppermute | solution.py:361
  8.3 0.9 collective-permute-start.9
  9.2 2.2 %pack_one.1 = bf16[8,256,128]{2,1,0:T(8,128)(2,1)} custom-call(bf16[256,1024]{1,0:T(8,128)(2,1)} %x_ref.2, bf16[256,1024]{1,0:T(8,128)(2,1)} %y_ref.2), custom_call_target="tpu_custom_call" | custom-call | bytes 2097152 | tf_op jit(solution)/shard_map/pack_one/pallas_call | solution.py:72
  11.5 0.7 maximum_bitcast_fusion
  12.3 3.3 %collective-permute-start.6 = (bf16[256,128]{1,0:T(8,128)(2,1)S(1)}, bf16[256,128]{1,0:T(8,128)(2,1)S(1)}, u32[]{:S(2)}, u32[]{:S(2)}) collective-permute-start(bf16[256,128]{1,0:T(8,128)(2,1)S(1)} %copy-done.33), channel_id=1, source_target_pairs={{0,4},{1,5},{2,6},{3,7},{4,0},{5,1},{6,2},{7,3},{8,12},{9,13},{10,... | collective-permute-start | bytes 196616 | tf_op jit(solution)/shard_map/ppermute | solution.py:361
  16.2 3.5 %all-to-all-start = ((bf16[8,256,128]{2,1,0:T(8,128)(2,1)}), bf16[8,256,128]{2,1,0:T(8,128)(2,1)S(1)}, u32[]{:S(2)}, u32[]{:S(2)}) async-start(bf16[8,256,128]{2,1,0:T(8,128)(2,1)} %pack_one.1), calls=%async_computation | async-start | bytes 1048576 | tf_op jit(solution)/shard_map/all_to_all | solution.py:396
  19.7 2.9 %pack.1 = bf16[8,512,128]{2,1,0:T(8,128)(2,1)} custom-call(bf16[256,1024]{1,0:T(8,128)(2,1)} %x_ref.2, bf16[256,1024]{1,0:T(8,128)(2,1)} %x_ref.3, bf16[256,1024]{1,0:T(8,128)(2,1)} %y_ref.3, bf16[256,1024]{1,0:T(8,128)(2,1)} %y_ref.2), custom_call_target="tpu_custom_call" | custom-call | bytes 2097152 | tf_op jit(solution)/shard_map/pack/pallas_call | solution.py:47
  22.8 0.7 reshape_reshape.3.idx_ref
  23.5 0.6 fusion.19.lists_ref
  24.9 2.0 %lend.3 = (bf16[8,2,128,128]{3,2,1,0:T(8,128)(2,1)}, bf16[4,128,128]{2,1,0:T(8,128)(2,1)}, bf16[4,128,128]{2,1,0:T(8,128)(2,1)}, bf16[4,128,128]{2,1,0:T(8,128)(2,1)}) custom-call(s32[16]{0:T(128)} %fusion.19.lists_ref, s32[1]{0:T(128)} %bitcast.h_ref, bf16[2,128,128]{2,1,0:T(8,128)(2,1)} %bitcast.16, bf16[2,128,128]{2,1,0:T(8,128)(2,1)} %bitcast.17, ...), custom_call_target="tpu_custom_call" | custom-call | bytes 2097152 | tf_op jit(solution)/shard_map/lend/pallas_call | solution.py:127
  26.9 1.5 %collective-permute-start.10 = (bf16[4,128,128]{2,1,0:T(8,128)(2,1)}, bf16[4,128,128]{2,1,0:T(8,128)(2,1)S(1)}, u32[]{:S(2)}, u32[]{:S(2)}) collective-permute-start(bf16[4,128,128]{2,1,0:T(8,128)(2,1)} %get-tuple-element.71), channel_id=1, source_target_pairs={{0,8},{8,0},{16,24},{24,16},{1,9},{9,1},{17,25},{25,17},{2,10},{10... | collective-permute-start | bytes 393224 | tf_op jit(solution)/shard_map/ppermute | solution.py:361
  28.5 1.5 %collective-permute-start.11 = (bf16[4,128,128]{2,1,0:T(8,128)(2,1)}, bf16[4,128,128]{2,1,0:T(8,128)(2,1)S(1)}, u32[]{:S(2)}, u32[]{:S(2)}) collective-permute-start(bf16[4,128,128]{2,1,0:T(8,128)(2,1)} %get-tuple-element.72), channel_id=1, source_target_pairs={{0,16},{8,24},{16,0},{24,8},{1,17},{9,25},{17,1},{25,9},{2,18},{10... | collective-permute-start | bytes 393224 | tf_op jit(solution)/shard_map/ppermute | solution.py:361
  30.5 0.6 div.46.tau_ref
  31.1 3.9 %all-to-all-done = bf16[8,256,128]{2,1,0:T(8,128)(2,1)S(1)} async-done(((bf16[8,256,128]{2,1,0:T(8,128)(2,1)}), bf16[8,256,128]{2,1,0:T(8,128)(2,1)S(1)}, u32[]{:S(2)}, u32[]{:S(2)}) %all-to-all-start) | async-done | bytes 524320 | tf_op jit(solution)/shard_map/all_to_all | solution.py:396
  35.0 0.8 copy-done.3
  35.8 3.6 %all-to-all-start.1 = ((bf16[8,512,128]{2,1,0:T(8,128)(2,1)}), bf16[8,512,128]{2,1,0:T(8,128)(2,1)S(1)}, u32[]{:S(2)}, u32[]{:S(2)}) async-start(bf16[8,512,128]{2,1,0:T(8,128)(2,1)} %pack.1), calls=%async_computation.1 | async-start | bytes 2097152 | tf_op jit(solution)/shard_map/all_to_all | solution.py:396
  39.4 0.6 copy-done.28
  40.1 15.7 %attend.2 = (bf16[8,128,128]{2,1,0:T(8,128)(2,1)}, f32[16,128,128]{2,1,0:T(8,128)}, bf16[4,128,128]{2,1,0:T(8,128)(2,1)}, bf16[4,128,128]{2,1,0:T(8,128)(2,1)}, bf16[4,128,128]{2,1,0:T(8,128)(2,1)}) custom-call(s32[192]{0:T(256)} %reshape_reshape.3.idx_ref, s32[1]{0:T(128)} %bitcast.h_ref, bf16[8,2,128,128]{3,2,1,0:T(8,128)(2,1)} %get-tuple-element.69.kv_ref, ...), custom_call_target="tpu_custom_call" | custom-call | flops 20132659200 | bytes 6291456 | tf_op jit(solution)/shard_map/attend/pallas_call | solution.py:240
  55.8 1.5 %collective-permute-start.13 = (bf16[4,128,128]{2,1,0:T(8,128)(2,1)}, bf16[4,128,128]{2,1,0:T(8,128)(2,1)S(1)}, u32[]{:S(2)}, u32[]{:S(2)}) collective-permute-start(bf16[4,128,128]{2,1,0:T(8,128)(2,1)} %get-tuple-element.75), channel_id=1, source_target_pairs={{0,8},{8,0},{16,24},{24,16},{1,9},{9,1},{17,25},{25,17},{2,10},{10... | collective-permute-start | bytes 393224 | tf_op jit(solution)/shard_map/ppermute | solution.py:361
  57.3 1.5 %collective-permute-start.14 = (bf16[4,128,128]{2,1,0:T(8,128)(2,1)}, bf16[4,128,128]{2,1,0:T(8,128)(2,1)S(1)}, u32[]{:S(2)}, u32[]{:S(2)}) collective-permute-start(bf16[4,128,128]{2,1,0:T(8,128)(2,1)} %get-tuple-element.76), channel_id=1, source_target_pairs={{0,16},{8,24},{16,0},{24,8},{1,17},{9,25},{17,1},{25,9},{2,18},{10... | collective-permute-start | bytes 393224 | tf_op jit(solution)/shard_map/ppermute | solution.py:361
  59.3 6.5 %all-to-all-done.1 = bf16[8,512,128]{2,1,0:T(8,128)(2,1)S(1)} async-done(((bf16[8,512,128]{2,1,0:T(8,128)(2,1)}), bf16[8,512,128]{2,1,0:T(8,128)(2,1)S(1)}, u32[]{:S(2)}, u32[]{:S(2)}) %all-to-all-start.1) | async-done | bytes 1048608 | tf_op jit(solution)/shard_map/all_to_all | solution.py:396
  65.8 1.0 copy-done
  66.8 2.0 %lend.2 = (bf16[4,128,128]{2,1,0:T(8,128)(2,1)}, bf16[4,128,128]{2,1,0:T(8,128)(2,1)}, bf16[4,128,128]{2,1,0:T(8,128)(2,1)}) custom-call(s32[16]{0:T(128)} %fusion.19.lists_ref, s32[1]{0:T(128)} %bitcast.h_ref, bf16[8,4,128,128]{3,2,1,0:T(8,128)(2,1)} %bitcast.13), custom_call_target="tpu_custom_call" | custom-call | bytes 2097152 | tf_op jit(solution)/shard_map/lend/pallas_call | solution.py:127
  68.9 1.5 %collective-permute-start.2 = (bf16[4,128,128]{2,1,0:T(8,128)(2,1)}, bf16[4,128,128]{2,1,0:T(8,128)(2,1)S(1)}, u32[]{:S(2)}, u32[]{:S(2)}) collective-permute-start(bf16[4,128,128]{2,1,0:T(8,128)(2,1)} %get-tuple-element.58), channel_id=1, source_target_pairs={{0,8},{8,0},{16,24},{24,16},{1,9},{9,1},{17,25},{25,17},{2,10},{10... | collective-permute-start | bytes 393224 | tf_op jit(solution)/shard_map/ppermute | solution.py:361
  70.4 1.5 %collective-permute-start.3 = (bf16[4,128,128]{2,1,0:T(8,128)(2,1)}, bf16[4,128,128]{2,1,0:T(8,128)(2,1)S(1)}, u32[]{:S(2)}, u32[]{:S(2)}) collective-permute-start(bf16[4,128,128]{2,1,0:T(8,128)(2,1)} %get-tuple-element.59), channel_id=1, source_target_pairs={{0,16},{8,24},{16,0},{24,8},{1,17},{9,25},{17,1},{25,9},{2,18},{10... | collective-permute-start | bytes 393224 | tf_op jit(solution)/shard_map/ppermute | solution.py:361
  73.1 2.5 %collect.2 = bf16[8,384,128]{2,1,0:T(8,128)(2,1)} custom-call(s32[16]{0:T(128)} %fusion.19.lists_ref, s32[1]{0:T(128)} %bitcast.h_ref, f32[16,128,128]{2,1,0:T(8,128)} %get-tuple-element.74.own, bf16[4,128,128]{2,1,0:T(8,128)(2,1)} %copy-done.4, bf16[4,128,128]{2,1,0:T(8,128)(2,1)} %copy-done.5, bf16[4,128,128]{2,1,0:T(8,128)(2,1)} %copy-done.7, ...), custom_call_target="tpu_custom_call" | custom-call | bytes 4194304 | tf_op jit(solution)/shard_map/collect/pallas_call | solution.py:289
  75.6 3.5 %all-to-all-start.2 = ((bf16[8,384,128]{2,1,0:T(8,128)(2,1)}), bf16[8,384,128]{2,1,0:T(8,128)(2,1)S(1)}, u32[]{:S(2)}, u32[]{:S(2)}) async-start(bf16[8,384,128]{2,1,0:T(8,128)(2,1)} %collect.2), calls=%async_computation.2 | async-start | bytes 1572864 | tf_op jit(solution)/shard_map/all_to_all | solution.py:396
  79.2 0.6 copy-done.26
  79.9 0.6 copy-done.29
  80.5 15.7 %attend.3 = (bf16[8,128,128]{2,1,0:T(8,128)(2,1)}, f32[16,128,128]{2,1,0:T(8,128)}, bf16[4,128,128]{2,1,0:T(8,128)(2,1)}, bf16[4,128,128]{2,1,0:T(8,128)(2,1)}, bf16[4,128,128]{2,1,0:T(8,128)(2,1)}) custom-call(s32[192]{0:T(256)} %reshape_reshape.3.idx_ref, s32[1]{0:T(128)} %bitcast.h_ref, bf16[8,4,128,128]{3,2,1,0:T(8,128)(2,1)} %bitcast.14, ...), custom_call_target="tpu_custom_call" | custom-call | flops 20132659200 | bytes 6291456 | tf_op jit(solution)/shard_map/attend/pallas_call | solution.py:240
  96.3 1.5 %collective-permute-start.16 = (bf16[4,128,128]{2,1,0:T(8,128)(2,1)}, bf16[4,128,128]{2,1,0:T(8,128)(2,1)S(1)}, u32[]{:S(2)}, u32[]{:S(2)}) collective-permute-start(bf16[4,128,128]{2,1,0:T(8,128)(2,1)} %get-tuple-element.83), channel_id=1, source_target_pairs={{0,8},{8,0},{16,24},{24,16},{1,9},{9,1},{17,25},{25,17},{2,10},{10... | collective-permute-start | bytes 393224 | tf_op jit(solution)/shard_map/ppermute | solution.py:361
  97.8 1.5 %collective-permute-start.17 = (bf16[4,128,128]{2,1,0:T(8,128)(2,1)}, bf16[4,128,128]{2,1,0:T(8,128)(2,1)S(1)}, u32[]{:S(2)}, u32[]{:S(2)}) collective-permute-start(bf16[4,128,128]{2,1,0:T(8,128)(2,1)} %get-tuple-element.84), channel_id=1, source_target_pairs={{0,16},{8,24},{16,0},{24,8},{1,17},{9,25},{17,1},{25,9},{2,18},{10... | collective-permute-start | bytes 393224 | tf_op jit(solution)/shard_map/ppermute | solution.py:361
  100.1 2.6 %collective-permute-done.16.refs_0_ = bf16[4,128,128]{2,1,0:T(8,128)(2,1)S(1)} collective-permute-done((bf16[4,128,128]{2,1,0:T(8,128)(2,1)}, bf16[4,128,128]{2,1,0:T(8,128)(2,1)S(1)}, u32[]{:S(2)}, u32[]{:S(2)}) %collective-permute-start.16) | collective-permute-done | bytes 131104 | tf_op jit(solution)/shard_map/ppermute | solution.py:361
  102.7 3.6 %collective-permute-done.17.refs_1_ = bf16[4,128,128]{2,1,0:T(8,128)(2,1)S(1)} collective-permute-done((bf16[4,128,128]{2,1,0:T(8,128)(2,1)}, bf16[4,128,128]{2,1,0:T(8,128)(2,1)S(1)}, u32[]{:S(2)}, u32[]{:S(2)}) %collective-permute-start.17) | collective-permute-done | bytes 131104 | tf_op jit(solution)/shard_map/ppermute | solution.py:361
  106.3 4.8 %all-to-all-start.3 = ((bf16[8,128,128]{2,1,0:T(8,128)(2,1)}), bf16[8,128,128]{2,1,0:T(8,128)(2,1)S(1)}, u32[]{:S(2)}, u32[]{:S(2)}) async-start(bf16[8,128,128]{2,1,0:T(8,128)(2,1)} %get-tuple-element.87), calls=%async_computation.3 | async-start | bytes 524288 | tf_op jit(solution)/shard_map/all_to_all | solution.py:396
  111.1 2.3 %collect.3 = (bf16[256,128]{1,0:T(8,128)(2,1)}, bf16[256,128]{1,0:T(8,128)(2,1)}, bf16[256,128]{1,0:T(8,128)(2,1)}, bf16[256,128]{1,0:T(8,128)(2,1)}, bf16[256,1...) custom-call(s32[16]{0:T(128)} %fusion.19.lists_ref, ...), custom_call_target="tpu_custom_call" | custom-call | bytes 4194304 | tf_op jit(solution)/shard_map/collect/pallas_call | solution.py:289
  113.4 0.5 collective-permute-start.19
  114.0 1.7 %collective-permute-start.20 = (bf16[256,128]{1,0:T(8,128)(2,1)}, bf16[256,128]{1,0:T(8,128)(2,1)S(1)}, u32[]{:S(2)}, u32[]{:S(2)}) collective-permute-start(bf16[256,128]{1,0:T(8,128)(2,1)} %get-tuple-element.95), channel_id=1, source_target_pairs={{0,2},{1,3},{2,0},{3,1},{4,6},{5,7},{6,4},{7,5},{8,10},{9,11},{10,... | collective-permute-start | bytes 196616 | tf_op jit(solution)/shard_map/ppermute | solution.py:361
  115.7 2.6 %collective-permute-start.22 = (bf16[256,128]{1,0:T(8,128)(2,1)}, bf16[256,128]{1,0:T(8,128)(2,1)S(1)}, u32[]{:S(2)}, u32[]{:S(2)}) collective-permute-start(bf16[256,128]{1,0:T(8,128)(2,1)} %get-tuple-element.97), channel_id=1, source_target_pairs={{0,4},{1,5},{2,6},{3,7},{4,0},{5,1},{6,2},{7,3},{8,12},{9,13},{10,... | collective-permute-start | bytes 196616 | tf_op jit(solution)/shard_map/ppermute | solution.py:361
  118.4 3.5 %collective-permute-start.24 = (bf16[256,128]{1,0:T(8,128)(2,1)}, bf16[256,128]{1,0:T(8,128)(2,1)S(1)}, u32[]{:S(2)}, u32[]{:S(2)}) collective-permute-start(bf16[256,128]{1,0:T(8,128)(2,1)} %get-tuple-element.99), channel_id=1, source_target_pairs={{0,6},{1,7},{2,4},{3,5},{4,2},{5,3},{6,0},{7,1},{8,14},{9,15},{10,... | collective-permute-start | bytes 196616 | tf_op jit(solution)/shard_map/ppermute | solution.py:361
  121.8 1.3 %collective-permute-done.20.refs_2_ = bf16[256,128]{1,0:T(8,128)(2,1)S(1)} collective-permute-done((bf16[256,128]{1,0:T(8,128)(2,1)}, bf16[256,128]{1,0:T(8,128)(2,1)S(1)}, u32[]{:S(2)}, u32[]{:S(2)}) %collective-permute-start.20) | collective-permute-done | bytes 65568 | tf_op jit(solution)/shard_map/ppermute | solution.py:361
  123.2 0.7 copy-done.2
  123.9 2.6 %unpack_early.1 = (bf16[256,1024]{1,0:T(8,128)(2,1)}, bf16[256,1024]{1,0:T(8,128)(2,1)}, bf16[256,1024]{1,0:T(8,128)(2,1)}) custom-call(bf16[8,384,128]{2,1,0:T(8,128)(2,1)} %copy-done.1, bf16[8,128,128]{2,1,0:T(8,128)(2,1)} %copy-done.2), custom_call_target="tpu_custom_call" | custom-call | bytes 8388608 | tf_op jit(solution)/shard_map/unpack_early/pallas_call | solution.py:336
  126.6 2.5 %collective-permute-done.23.refs_5_ = bf16[256,128]{1,0:T(8,128)(2,1)S(1)} collective-permute-done((bf16[256,128]{1,0:T(8,128)(2,1)}, bf16[256,128]{1,0:T(8,128)(2,1)S(1)}, u32[]{:S(2)}, u32[]{:S(2)}) %collective-permute-start.23) | collective-permute-done | bytes 65568 | tf_op jit(solution)/shard_map/ppermute | solution.py:361
  129.1 0.6 copy-done.14
  129.7 2.0 %unpack_last.1 = (bf16[256,1024]{1,0:T(8,128)(2,1)}, bf16[256,1024]{1,0:T(8,128)(2,1)}) custom-call(s32[1]{0:T(128)} %bitcast.h_ref, bf16[256,128]{1,0:T(8,128)(2,1)} %get-tuple-element.93.refs_0_, bf16[256,128]{1,0:T(8,128)(2,1)} %copy-done.10, bf16[256,128]{1,0:T(8,128)(2,1)} %copy-done.11, ...), custom_call_target="tpu_custom_call", output_to_operand_aliasing={{0}: (9, {}), {1}: (10, {})} | custom-call | bytes 2097152 | tf_op jit(solution)/shard_map/unpack_last/pallas_call | solution.py:346
  (107 shorter events, 5.5 us)
Async XLA Ops:
  2.8 9.5 %collective-permute-start = (bf16[256,128]{1,0:T(8,128)(2,1)}, bf16[256,128]{1,0:T(8,128)(2,1)S(1)}, u32[]{:S(2)}, u32[]{:S(2)}) collective-permute-start(bf16[256,128]{1,0:T(8,128)(2,1)} %get-tuple-element.54), channel_id=1, source_target_pairs={{0,1},{1,0},{2,3},{3,2},{4,5},{5,4},{6,7},{7,6},{8,9},{9,8},{10,11... | collective-permute-start | bytes 196616 | tf_op jit(solution)/shard_map/ppermute | solution.py:361
  3.2 12.4 %collective-permute-start.1 = (bf16[256,128]{1,0:T(8,128)(2,1)}, bf16[256,128]{1,0:T(8,128)(2,1)S(1)}, u32[]{:S(2)}, u32[]{:S(2)}) collective-permute-start(bf16[256,128]{1,0:T(8,128)(2,1)} %get-tuple-element.55), channel_id=1, source_target_pairs={{0,2},{1,3},{2,0},{3,1},{4,6},{5,7},{6,4},{7,5},{8,10},{9,11},{10,... | collective-permute-start | bytes 196616 | tf_op jit(solution)/shard_map/ppermute | solution.py:361
  5.8 18.4 %collective-permute-start.8 = (bf16[256,128]{1,0:T(8,128)(2,1)}, bf16[256,128]{1,0:T(8,128)(2,1)S(1)}, u32[]{:S(2)}, u32[]{:S(2)}) collective-permute-start(bf16[256,128]{1,0:T(8,128)(2,1)} %get-tuple-element.67), channel_id=1, source_target_pairs={{0,6},{1,7},{2,4},{3,5},{4,2},{5,3},{6,0},{7,1},{8,14},{9,15},{10,... | collective-permute-start | bytes 196616 | tf_op jit(solution)/shard_map/ppermute | solution.py:361
  8.3 0.9 copy-start.24
  8.3 15.9 %collective-permute-start.9 = (bf16[256,128]{1,0:T(8,128)(2,1)}, bf16[256,128]{1,0:T(8,128)(2,1)S(1)}, u32[]{:S(2)}, u32[]{:S(2)}) collective-permute-start(bf16[256,128]{1,0:T(8,128)(2,1)} %get-tuple-element.68), channel_id=1, source_target_pairs={{0,7},{1,6},{2,5},{3,4},{4,3},{5,2},{6,1},{7,0},{8,15},{9,14},{10,... | collective-permute-start | bytes 196616 | tf_op jit(solution)/shard_map/ppermute | solution.py:361
  9.2 15.1 %collective-permute-start.5 = (bf16[256,128]{1,0:T(8,128)(2,1)}, bf16[256,128]{1,0:T(8,128)(2,1)S(1)}, u32[]{:S(2)}, u32[]{:S(2)}) collective-permute-start(bf16[256,128]{1,0:T(8,128)(2,1)} %get-tuple-element.64), channel_id=1, source_target_pairs={{0,3},{1,2},{2,1},{3,0},{4,7},{5,6},{6,5},{7,4},{8,11},{9,10},{10,... | collective-permute-start | bytes 196616 | tf_op jit(solution)/shard_map/ppermute | solution.py:361
  9.2 3.0 %copy-start.33 = (bf16[256,128]{1,0:T(8,128)(2,1)S(1)}, bf16[256,128]{1,0:T(8,128)(2,1)}, u32[]{:S(2)}) copy-start(bf16[256,128]{1,0:T(8,128)(2,1)} %get-tuple-element.65) | copy-start | bytes 196612
  9.2 6.3 %copy-start.32 = (bf16[256,128]{1,0:T(8,128)(2,1)S(1)}, bf16[256,128]{1,0:T(8,128)(2,1)}, u32[]{:S(2)}) copy-start(bf16[256,128]{1,0:T(8,128)(2,1)} %get-tuple-element.66) | copy-start | bytes 196612
  12.2 3.4 %copy-start.17 = (bf16[256,128]{1,0:T(8,128)(2,1)}, bf16[256,128]{1,0:T(8,128)(2,1)S(1)}, u32[]{:S(2)}) copy-start(bf16[256,128]{1,0:T(8,128)(2,1)S(1)} %collective-permute-done) | copy-start | bytes 196612
  12.3 12.0 %collective-permute-start.6 = (bf16[256,128]{1,0:T(8,128)(2,1)S(1)}, bf16[256,128]{1,0:T(8,128)(2,1)S(1)}, u32[]{:S(2)}, u32[]{:S(2)}) collective-permute-start(bf16[256,128]{1,0:T(8,128)(2,1)S(1)} %copy-done.33), channel_id=1, source_target_pairs={{0,4},{1,5},{2,6},{3,7},{4,0},{5,1},{6,2},{7,3},{8,12},{9,13},{10,... | collective-permute-start | bytes 196616 | tf_op jit(solution)/shard_map/ppermute | solution.py:361
  15.6 8.7 %collective-permute-start.7 = (bf16[256,128]{1,0:T(8,128)(2,1)S(1)}, bf16[256,128]{1,0:T(8,128)(2,1)S(1)}, u32[]{:S(2)}, u32[]{:S(2)}) collective-permute-start(bf16[256,128]{1,0:T(8,128)(2,1)S(1)} %copy-done.32), channel_id=1, source_target_pairs={{0,5},{1,4},{2,7},{3,6},{4,1},{5,0},{6,3},{7,2},{8,13},{9,12},{10,... | collective-permute-start | bytes 196616 | tf_op jit(solution)/shard_map/ppermute | solution.py:361
  16.2 18.8 %all-to-all-start = ((bf16[8,256,128]{2,1,0:T(8,128)(2,1)}), bf16[8,256,128]{2,1,0:T(8,128)(2,1)S(1)}, u32[]{:S(2)}, u32[]{:S(2)}) async-start(bf16[8,256,128]{2,1,0:T(8,128)(2,1)} %pack_one.1), calls=%async_computation | async-start | bytes 1048576 | tf_op jit(solution)/shard_map/all_to_all | solution.py:396
  22.7 0.8 copy-start.25
  26.9 12.4 %collective-permute-start.10 = (bf16[4,128,128]{2,1,0:T(8,128)(2,1)}, bf16[4,128,128]{2,1,0:T(8,128)(2,1)S(1)}, u32[]{:S(2)}, u32[]{:S(2)}) collective-permute-start(bf16[4,128,128]{2,1,0:T(8,128)(2,1)} %get-tuple-element.71), channel_id=1, source_target_pairs={{0,8},{8,0},{16,24},{24,16},{1,9},{9,1},{17,25},{25,17},{2,10},{10... | collective-permute-start | bytes 393224 | tf_op jit(solution)/shard_map/ppermute | solution.py:361
  28.5 10.9 %collective-permute-start.11 = (bf16[4,128,128]{2,1,0:T(8,128)(2,1)}, bf16[4,128,128]{2,1,0:T(8,128)(2,1)S(1)}, u32[]{:S(2)}, u32[]{:S(2)}) collective-permute-start(bf16[4,128,128]{2,1,0:T(8,128)(2,1)} %get-tuple-element.72), channel_id=1, source_target_pairs={{0,16},{8,24},{16,0},{24,8},{1,17},{9,25},{17,1},{25,9},{2,18},{10... | collective-permute-start | bytes 393224 | tf_op jit(solution)/shard_map/ppermute | solution.py:361
  30.0 9.4 %collective-permute-start.12 = (bf16[4,128,128]{2,1,0:T(8,128)(2,1)}, bf16[4,128,128]{2,1,0:T(8,128)(2,1)S(1)}, u32[]{:S(2)}, u32[]{:S(2)}) collective-permute-start(bf16[4,128,128]{2,1,0:T(8,128)(2,1)} %get-tuple-element.73), channel_id=1, source_target_pairs={{0,24},{8,16},{16,8},{24,0},{1,25},{9,17},{17,9},{25,1},{2,26},{10... | collective-permute-start | bytes 393224 | tf_op jit(solution)/shard_map/ppermute | solution.py:361
  35.0 0.8 copy-start.3
  35.8 30.1 %all-to-all-start.1 = ((bf16[8,512,128]{2,1,0:T(8,128)(2,1)}), bf16[8,512,128]{2,1,0:T(8,128)(2,1)S(1)}, u32[]{:S(2)}, u32[]{:S(2)}) async-start(bf16[8,512,128]{2,1,0:T(8,128)(2,1)} %pack.1), calls=%async_computation.1 | async-start | bytes 2097152 | tf_op jit(solution)/shard_map/all_to_all | solution.py:396
  39.3 0.7 copy-start.30
  39.4 0.7 copy-start.31
  55.8 16.1 %collective-permute-start.13 = (bf16[4,128,128]{2,1,0:T(8,128)(2,1)}, bf16[4,128,128]{2,1,0:T(8,128)(2,1)S(1)}, u32[]{:S(2)}, u32[]{:S(2)}) collective-permute-start(bf16[4,128,128]{2,1,0:T(8,128)(2,1)} %get-tuple-element.75), channel_id=1, source_target_pairs={{0,8},{8,0},{16,24},{24,16},{1,9},{9,1},{17,25},{25,17},{2,10},{10... | collective-permute-start | bytes 393224 | tf_op jit(solution)/shard_map/ppermute | solution.py:361
  57.3 15.1 %collective-permute-start.14 = (bf16[4,128,128]{2,1,0:T(8,128)(2,1)}, bf16[4,128,128]{2,1,0:T(8,128)(2,1)S(1)}, u32[]{:S(2)}, u32[]{:S(2)}) collective-permute-start(bf16[4,128,128]{2,1,0:T(8,128)(2,1)} %get-tuple-element.76), channel_id=1, source_target_pairs={{0,16},{8,24},{16,0},{24,8},{1,17},{9,25},{17,1},{25,9},{2,18},{10... | collective-permute-start | bytes 393224 | tf_op jit(solution)/shard_map/ppermute | solution.py:361
  58.8 13.6 %collective-permute-start.15 = (bf16[4,128,128]{2,1,0:T(8,128)(2,1)}, bf16[4,128,128]{2,1,0:T(8,128)(2,1)S(1)}, u32[]{:S(2)}, u32[]{:S(2)}) collective-permute-start(bf16[4,128,128]{2,1,0:T(8,128)(2,1)} %get-tuple-element.77), channel_id=1, source_target_pairs={{0,24},{8,16},{16,8},{24,0},{1,25},{9,17},{17,9},{25,1},{2,26},{10... | collective-permute-start | bytes 393224 | tf_op jit(solution)/shard_map/ppermute | solution.py:361
  65.8 1.0 copy-start
  68.9 10.3 %collective-permute-start.2 = (bf16[4,128,128]{2,1,0:T(8,128)(2,1)}, bf16[4,128,128]{2,1,0:T(8,128)(2,1)S(1)}, u32[]{:S(2)}, u32[]{:S(2)}) collective-permute-start(bf16[4,128,128]{2,1,0:T(8,128)(2,1)} %get-tuple-element.58), channel_id=1, source_target_pairs={{0,8},{8,0},{16,24},{24,16},{1,9},{9,1},{17,25},{25,17},{2,10},{10... | collective-permute-start | bytes 393224 | tf_op jit(solution)/shard_map/ppermute | solution.py:361
  70.4 8.8 %collective-permute-start.3 = (bf16[4,128,128]{2,1,0:T(8,128)(2,1)}, bf16[4,128,128]{2,1,0:T(8,128)(2,1)S(1)}, u32[]{:S(2)}, u32[]{:S(2)}) collective-permute-start(bf16[4,128,128]{2,1,0:T(8,128)(2,1)} %get-tuple-element.59), channel_id=1, source_target_pairs={{0,16},{8,24},{16,0},{24,8},{1,17},{9,25},{17,1},{25,9},{2,18},{10... | collective-permute-start | bytes 393224 | tf_op jit(solution)/shard_map/ppermute | solution.py:361
  71.9 7.3 %collective-permute-start.4 = (bf16[4,128,128]{2,1,0:T(8,128)(2,1)}, bf16[4,128,128]{2,1,0:T(8,128)(2,1)S(1)}, u32[]{:S(2)}, u32[]{:S(2)}) collective-permute-start(bf16[4,128,128]{2,1,0:T(8,128)(2,1)} %get-tuple-element.60), channel_id=1, source_target_pairs={{0,24},{8,16},{16,8},{24,0},{1,25},{9,17},{17,9},{25,1},{2,26},{10... | collective-permute-start | bytes 393224 | tf_op jit(solution)/shard_map/ppermute | solution.py:361
  75.6 24.4 %all-to-all-start.2 = ((bf16[8,384,128]{2,1,0:T(8,128)(2,1)}), bf16[8,384,128]{2,1,0:T(8,128)(2,1)S(1)}, u32[]{:S(2)}, u32[]{:S(2)}) async-start(bf16[8,384,128]{2,1,0:T(8,128)(2,1)} %collect.2), calls=%async_computation.2 | async-start | bytes 1572864 | tf_op jit(solution)/shard_map/all_to_all | solution.py:396
  96.3 6.4 %collective-permute-start.16 = (bf16[4,128,128]{2,1,0:T(8,128)(2,1)}, bf16[4,128,128]{2,1,0:T(8,128)(2,1)S(1)}, u32[]{:S(2)}, u32[]{:S(2)}) collective-permute-start(bf16[4,128,128]{2,1,0:T(8,128)(2,1)} %get-tuple-element.83), channel_id=1, source_target_pairs={{0,8},{8,0},{16,24},{24,16},{1,9},{9,1},{17,25},{25,17},{2,10},{10... | collective-permute-start | bytes 393224 | tf_op jit(solution)/shard_map/ppermute | solution.py:361
  97.8 8.5 %collective-permute-start.17 = (bf16[4,128,128]{2,1,0:T(8,128)(2,1)}, bf16[4,128,128]{2,1,0:T(8,128)(2,1)S(1)}, u32[]{:S(2)}, u32[]{:S(2)}) collective-permute-start(bf16[4,128,128]{2,1,0:T(8,128)(2,1)} %get-tuple-element.84), channel_id=1, source_target_pairs={{0,16},{8,24},{16,0},{24,8},{1,17},{9,25},{17,1},{25,9},{2,18},{10... | collective-permute-start | bytes 393224 | tf_op jit(solution)/shard_map/ppermute | solution.py:361
  99.3 7.0 %collective-permute-start.18 = (bf16[4,128,128]{2,1,0:T(8,128)(2,1)}, bf16[4,128,128]{2,1,0:T(8,128)(2,1)S(1)}, u32[]{:S(2)}, u32[]{:S(2)}) collective-permute-start(bf16[4,128,128]{2,1,0:T(8,128)(2,1)} %get-tuple-element.85), channel_id=1, source_target_pairs={{0,24},{8,16},{16,8},{24,0},{1,25},{9,17},{17,9},{25,1},{2,26},{10... | collective-permute-start | bytes 393224 | tf_op jit(solution)/shard_map/ppermute | solution.py:361
  100.1 13.3 %copy-start.1 = (bf16[8,384,128]{2,1,0:T(8,128)(2,1)}, bf16[8,384,128]{2,1,0:T(8,128)(2,1)S(1)}, u32[]{:S(2)}) copy-start(bf16[8,384,128]{2,1,0:T(8,128)(2,1)S(1)} %all-to-all-done.2.refs_0_) | copy-start | bytes 2359300
  102.7 8.4 %copy-start.6 = (bf16[4,128,128]{2,1,0:T(8,128)(2,1)}, bf16[4,128,128]{2,1,0:T(8,128)(2,1)S(1)}, u32[]{:S(2)}) copy-start(bf16[4,128,128]{2,1,0:T(8,128)(2,1)S(1)} %collective-permute-done.16.refs_0_) | copy-start | bytes 393220
  106.3 4.8 %copy-start.8 = (bf16[4,128,128]{2,1,0:T(8,128)(2,1)}, bf16[4,128,128]{2,1,0:T(8,128)(2,1)S(1)}, u32[]{:S(2)}) copy-start(bf16[4,128,128]{2,1,0:T(8,128)(2,1)S(1)} %collective-permute-done.17.refs_1_) | copy-start | bytes 393220
  106.3 4.8 %copy-start.9 = (bf16[4,128,128]{2,1,0:T(8,128)(2,1)}, bf16[4,128,128]{2,1,0:T(8,128)(2,1)S(1)}, u32[]{:S(2)}) copy-start(bf16[4,128,128]{2,1,0:T(8,128)(2,1)S(1)} %collective-permute-done.18.refs_2_) | copy-start | bytes 393220
  106.3 16.9 %all-to-all-start.3 = ((bf16[8,128,128]{2,1,0:T(8,128)(2,1)}), bf16[8,128,128]{2,1,0:T(8,128)(2,1)S(1)}, u32[]{:S(2)}, u32[]{:S(2)}) async-start(bf16[8,128,128]{2,1,0:T(8,128)(2,1)} %get-tuple-element.87), calls=%async_computation.3 | async-start | bytes 524288 | tf_op jit(solution)/shard_map/all_to_all | solution.py:396
  113.4 4.9 %collective-permute-start.19 = (bf16[256,128]{1,0:T(8,128)(2,1)}, bf16[256,128]{1,0:T(8,128)(2,1)S(1)}, u32[]{:S(2)}, u32[]{:S(2)}) collective-permute-start(bf16[256,128]{1,0:T(8,128)(2,1)} %get-tuple-element.94), channel_id=1, source_target_pairs={{0,1},{1,0},{2,3},{3,2},{4,5},{5,4},{6,7},{7,6},{8,9},{9,8},{10,11... | collective-permute-start | bytes 196616 | tf_op jit(solution)/shard_map/ppermute | solution.py:361
  114.0 9.2 %collective-permute-start.20 = (bf16[256,128]{1,0:T(8,128)(2,1)}, bf16[256,128]{1,0:T(8,128)(2,1)S(1)}, u32[]{:S(2)}, u32[]{:S(2)}) collective-permute-start(bf16[256,128]{1,0:T(8,128)(2,1)} %get-tuple-element.95), channel_id=1, source_target_pairs={{0,2},{1,3},{2,0},{3,1},{4,6},{5,7},{6,4},{7,5},{8,10},{9,11},{10,... | collective-permute-start | bytes 196616 | tf_op jit(solution)/shard_map/ppermute | solution.py:361
  115.7 10.9 %collective-permute-start.21 = (bf16[256,128]{1,0:T(8,128)(2,1)}, bf16[256,128]{1,0:T(8,128)(2,1)S(1)}, u32[]{:S(2)}, u32[]{:S(2)}) collective-permute-start(bf16[256,128]{1,0:T(8,128)(2,1)} %get-tuple-element.96), channel_id=1, source_target_pairs={{0,3},{1,2},{2,1},{3,0},{4,7},{5,6},{6,5},{7,4},{8,11},{9,10},{10,... | collective-permute-start | bytes 196616 | tf_op jit(solution)/shard_map/ppermute | solution.py:361
  115.7 10.9 %collective-permute-start.22 = (bf16[256,128]{1,0:T(8,128)(2,1)}, bf16[256,128]{1,0:T(8,128)(2,1)S(1)}, u32[]{:S(2)}, u32[]{:S(2)}) collective-permute-start(bf16[256,128]{1,0:T(8,128)(2,1)} %get-tuple-element.97), channel_id=1, source_target_pairs={{0,4},{1,5},{2,6},{3,7},{4,0},{5,1},{6,2},{7,3},{8,12},{9,13},{10,... | collective-permute-start | bytes 196616 | tf_op jit(solution)/shard_map/ppermute | solution.py:361
  118.2 10.8 %collective-permute-start.23 = (bf16[256,128]{1,0:T(8,128)(2,1)}, bf16[256,128]{1,0:T(8,128)(2,1)S(1)}, u32[]{:S(2)}, u32[]{:S(2)}) collective-permute-start(bf16[256,128]{1,0:T(8,128)(2,1)} %get-tuple-element.98), channel_id=1, source_target_pairs={{0,5},{1,4},{2,7},{3,6},{4,1},{5,0},{6,3},{7,2},{8,13},{9,12},{10,... | collective-permute-start | bytes 196616 | tf_op jit(solution)/shard_map/ppermute | solution.py:361
  118.4 8.2 %copy-start.10 = (bf16[256,128]{1,0:T(8,128)(2,1)}, bf16[256,128]{1,0:T(8,128)(2,1)S(1)}, u32[]{:S(2)}) copy-start(bf16[256,128]{1,0:T(8,128)(2,1)S(1)} %collective-permute-done.19.refs_1_) | copy-start | bytes 196612
  118.4 10.7 %collective-permute-start.24 = (bf16[256,128]{1,0:T(8,128)(2,1)}, bf16[256,128]{1,0:T(8,128)(2,1)S(1)}, u32[]{:S(2)}, u32[]{:S(2)}) collective-permute-start(bf16[256,128]{1,0:T(8,128)(2,1)} %get-tuple-element.99), channel_id=1, source_target_pairs={{0,6},{1,7},{2,4},{3,5},{4,2},{5,3},{6,0},{7,1},{8,14},{9,15},{10,... | collective-permute-start | bytes 196616 | tf_op jit(solution)/shard_map/ppermute | solution.py:361
  123.2 3.3 %copy-start.11 = (bf16[256,128]{1,0:T(8,128)(2,1)}, bf16[256,128]{1,0:T(8,128)(2,1)S(1)}, u32[]{:S(2)}) copy-start(bf16[256,128]{1,0:T(8,128)(2,1)S(1)} %collective-permute-done.20.refs_2_) | copy-start | bytes 196612
  123.2 5.9 %collective-permute-start.25 = (bf16[256,128]{1,0:T(8,128)(2,1)}, bf16[256,128]{1,0:T(8,128)(2,1)S(1)}, u32[]{:S(2)}, u32[]{:S(2)}) collective-permute-start(bf16[256,128]{1,0:T(8,128)(2,1)} %get-tuple-element.100), channel_id=1, source_target_pairs={{0,7},{1,6},{2,5},{3,4},{4,3},{5,2},{6,1},{7,0},{8,15},{9,14},{10,... | collective-permute-start | bytes 196616 | tf_op jit(solution)/shard_map/ppermute | solution.py:361
  123.2 0.7 copy-start.2
  126.5 2.5 %copy-start.12 = (bf16[256,128]{1,0:T(8,128)(2,1)}, bf16[256,128]{1,0:T(8,128)(2,1)S(1)}, u32[]{:S(2)}) copy-start(bf16[256,128]{1,0:T(8,128)(2,1)S(1)} %collective-permute-done.21.refs_3_) | copy-start | bytes 196612
  126.5 2.5 %copy-start.13 = (bf16[256,128]{1,0:T(8,128)(2,1)}, bf16[256,128]{1,0:T(8,128)(2,1)S(1)}, u32[]{:S(2)}) copy-start(bf16[256,128]{1,0:T(8,128)(2,1)S(1)} %collective-permute-done.22.refs_4_) | copy-start | bytes 196612
  (16 other events, 10.3 us)

commit v6 on v5

--- a/solution.py
+++ b/solution.py
@@ -187,8 +187,9 @@
         total = weighted = None
         nxt = 0
         for i in range(NBR):
-            if i % 2 == 0:
-                top2 = step1(1 - slot, both2, where2, nxt, top2); nxt += 1
+            if i % 4 < 3:
+                top2 = step1(1 - slot, both2, where2, nxt, top2)
+                nxt += 1
             ex = jnp.exp2((s_buf[slot, i] - m) * c)
             s_buf[slot, i] = ex
             l8 = fold8(ex, jnp.sum)
@@ -201,7 +202,9 @@
         dq = None
         for i in range(0, NBR, 2):
             us = []
-            top2 = step1(1 - slot, both2, where2, nxt, top2); nxt += 1
+            if nxt < NBR:
+                top2 = step1(1 - slot, both2, where2, nxt, top2)
+                nxt += 1
             for j in (i, i + 1):
                 p = s_buf[slot, j] * inv
                 u = (p * (dp_buf[slot, j] - delta) * tau).astype(bf16)

time: 133 us -> 133 us (level)
  transfers between devices with their start and end apart: 30 -> 30, of which waited for: 7 -> 7; matrix products, arithmetic and copies ran while one was open for 2% -> 2% of each run, Pallas kernels for 37% -> 36%
where the time goes in v6:
time: 133 us; the launch traced here: 132 us
  Pallas kernels  52.2 us (39%)
  starting transfers between devices  47.6 us (36%)
  waiting for transfers between devices  20.8 us (16%)
  local copies, waits for them, and re-layouts  8.48 us (6%)
  other arithmetic  1.6 us (1%)
    ppermute x26, starting transfers between devices, swap(): return lax.ppermute(x, axis, [(i, i ^ k) for i in range(size)])  32.2 us
    pallas_call x2, Pallas kernels, attend(): pl.pallas_call(functools.partial(attend_kernel, bool(qg), parts, cap, n,...  31.4 us
    all_to_all x4, starting transfers between devices, spread(): return lax.all_to_all(x, 'head', split_axis=0, concat_axis=0, tiled=True)  15.4 us
    all_to_all x4, waiting for transfers between devices, spread(): return lax.all_to_all(x, 'head', split_axis=0, concat_axis=0, tiled=True)  10.8 us
    ppermute x26, waiting for transfers between devices, swap(): return lax.ppermute(x, axis, [(i, i ^ k) for i in range(size)])  10 us
    unnamed x68, local copies, waits for them, and re-layouts  7.07 us
    pallas_call x2, Pallas kernels, collect(): pl.pallas_call(functools.partial(collect_kernel, last, parts, cap, n, bpd...  4.83 us
    pallas_call x2, Pallas kernels, lend(): pl.pallas_call(functools.partial(lend_kernel, parts, cap, bpd), out_shape...  4.07 us
  transfers between devices with their start and end apart: 30, of which 7 were waited for; matrix products, arithmetic and copies ran while one was open for 2% of the time, Pallas kernels for 36%

profile of v6, /device:TPU:0, one launch (start us, length us, event | category | flops | bytes accessed | tf_op | source)
XLA Modules:
  0.0 131.7 jit_solution(4947447767537921853)
XLA Ops:
  0.6 2.1 %pieces.1 = (bf16[256,128]{1,0:T(8,128)(2,1)}, bf16[256,128]{1,0:T(8,128)(2,1)}, bf16[256,128]{1,0:T(8,128)(2,1)}, bf16[256,128]{1,0:T(8,128)(2,1)}, bf16[256,12...) custom-call(s32[1]{0:T(128)} %bitcast.h_ref, ...), custom_call_target="tpu_custom_call" | custom-call | bytes 2097152 | tf_op jit(solution)/shard_map/pieces/pallas_call | solution.py:98
  3.2 2.6 %collective-permute-start.1 = (bf16[256,128]{1,0:T(8,128)(2,1)}, bf16[256,128]{1,0:T(8,128)(2,1)S(1)}, u32[]{:S(2)}, u32[]{:S(2)}) collective-permute-start(bf16[256,128]{1,0:T(8,128)(2,1)} %get-tuple-element.55), channel_id=1, source_target_pairs={{0,2},{1,3},{2,0},{3,1},{4,6},{5,7},{6,4},{7,5},{8,10},{9,11},{10,... | collective-permute-start | bytes 196616 | tf_op jit(solution)/shard_map/ppermute | solution.py:364
  5.8 2.5 %collective-permute-start.8 = (bf16[256,128]{1,0:T(8,128)(2,1)}, bf16[256,128]{1,0:T(8,128)(2,1)S(1)}, u32[]{:S(2)}, u32[]{:S(2)}) collective-permute-start(bf16[256,128]{1,0:T(8,128)(2,1)} %get-tuple-element.67), channel_id=1, source_target_pairs={{0,6},{1,7},{2,4},{3,5},{4,2},{5,3},{6,0},{7,1},{8,14},{9,15},{10,... | collective-permute-start | bytes 196616 | tf_op jit(solution)/shard_map/ppermute | solution.py:364
  8.3 0.9 collective-permute-start.9
  9.2 2.2 %pack_one.1 = bf16[8,256,128]{2,1,0:T(8,128)(2,1)} custom-call(bf16[256,1024]{1,0:T(8,128)(2,1)} %x_ref.2, bf16[256,1024]{1,0:T(8,128)(2,1)} %y_ref.2), custom_call_target="tpu_custom_call" | custom-call | bytes 2097152 | tf_op jit(solution)/shard_map/pack_one/pallas_call | solution.py:72
  11.5 0.7 maximum_bitcast_fusion
  12.3 3.3 %collective-permute-start.6 = (bf16[256,128]{1,0:T(8,128)(2,1)S(1)}, bf16[256,128]{1,0:T(8,128)(2,1)S(1)}, u32[]{:S(2)}, u32[]{:S(2)}) collective-permute-start(bf16[256,128]{1,0:T(8,128)(2,1)S(1)} %copy-done.33), channel_id=1, source_target_pairs={{0,4},{1,5},{2,6},{3,7},{4,0},{5,1},{6,2},{7,3},{8,12},{9,13},{10,... | collective-permute-start | bytes 196616 | tf_op jit(solution)/shard_map/ppermute | solution.py:364
  16.2 3.5 %all-to-all-start = ((bf16[8,256,128]{2,1,0:T(8,128)(2,1)}), bf16[8,256,128]{2,1,0:T(8,128)(2,1)S(1)}, u32[]{:S(2)}, u32[]{:S(2)}) async-start(bf16[8,256,128]{2,1,0:T(8,128)(2,1)} %pack_one.1), calls=%async_computation | async-start | bytes 1048576 | tf_op jit(solution)/shard_map/all_to_all | solution.py:399
  19.7 2.9 %pack.1 = bf16[8,512,128]{2,1,0:T(8,128)(2,1)} custom-call(bf16[256,1024]{1,0:T(8,128)(2,1)} %x_ref.2, bf16[256,1024]{1,0:T(8,128)(2,1)} %x_ref.3, bf16[256,1024]{1,0:T(8,128)(2,1)} %y_ref.3, bf16[256,1024]{1,0:T(8,128)(2,1)} %y_ref.2), custom_call_target="tpu_custom_call" | custom-call | bytes 2097152 | tf_op jit(solution)/shard_map/pack/pallas_call | solution.py:47
  22.8 0.7 reshape_reshape.3.idx_ref
  23.5 0.6 fusion.19.lists_ref
  24.9 2.0 %lend.3 = (bf16[8,2,128,128]{3,2,1,0:T(8,128)(2,1)}, bf16[4,128,128]{2,1,0:T(8,128)(2,1)}, bf16[4,128,128]{2,1,0:T(8,128)(2,1)}, bf16[4,128,128]{2,1,0:T(8,128)(2,1)}) custom-call(s32[16]{0:T(128)} %fusion.19.lists_ref, s32[1]{0:T(128)} %bitcast.h_ref, bf16[2,128,128]{2,1,0:T(8,128)(2,1)} %bitcast.16, bf16[2,128,128]{2,1,0:T(8,128)(2,1)} %bitcast.17, ...), custom_call_target="tpu_custom_call" | custom-call | bytes 2097152 | tf_op jit(solution)/shard_map/lend/pallas_call | solution.py:127
  26.9 1.5 %collective-permute-start.10 = (bf16[4,128,128]{2,1,0:T(8,128)(2,1)}, bf16[4,128,128]{2,1,0:T(8,128)(2,1)S(1)}, u32[]{:S(2)}, u32[]{:S(2)}) collective-permute-start(bf16[4,128,128]{2,1,0:T(8,128)(2,1)} %get-tuple-element.71), channel_id=1, source_target_pairs={{0,8},{8,0},{16,24},{24,16},{1,9},{9,1},{17,25},{25,17},{2,10},{10... | collective-permute-start | bytes 393224 | tf_op jit(solution)/shard_map/ppermute | solution.py:364
  28.5 1.5 %collective-permute-start.11 = (bf16[4,128,128]{2,1,0:T(8,128)(2,1)}, bf16[4,128,128]{2,1,0:T(8,128)(2,1)S(1)}, u32[]{:S(2)}, u32[]{:S(2)}) collective-permute-start(bf16[4,128,128]{2,1,0:T(8,128)(2,1)} %get-tuple-element.72), channel_id=1, source_target_pairs={{0,16},{8,24},{16,0},{24,8},{1,17},{9,25},{17,1},{25,9},{2,18},{10... | collective-permute-start | bytes 393224 | tf_op jit(solution)/shard_map/ppermute | solution.py:364
  30.5 0.6 div.46.tau_ref
  31.1 3.9 %all-to-all-done = bf16[8,256,128]{2,1,0:T(8,128)(2,1)S(1)} async-done(((bf16[8,256,128]{2,1,0:T(8,128)(2,1)}), bf16[8,256,128]{2,1,0:T(8,128)(2,1)S(1)}, u32[]{:S(2)}, u32[]{:S(2)}) %all-to-all-start) | async-done | bytes 524320 | tf_op jit(solution)/shard_map/all_to_all | solution.py:399
  35.0 0.8 copy-done.3
  35.8 3.6 %all-to-all-start.1 = ((bf16[8,512,128]{2,1,0:T(8,128)(2,1)}), bf16[8,512,128]{2,1,0:T(8,128)(2,1)S(1)}, u32[]{:S(2)}, u32[]{:S(2)}) async-start(bf16[8,512,128]{2,1,0:T(8,128)(2,1)} %pack.1), calls=%async_computation.1 | async-start | bytes 2097152 | tf_op jit(solution)/shard_map/all_to_all | solution.py:399
  39.4 0.6 copy-done.28
  40.1 15.7 %attend.2 = (bf16[8,128,128]{2,1,0:T(8,128)(2,1)}, f32[16,128,128]{2,1,0:T(8,128)}, bf16[4,128,128]{2,1,0:T(8,128)(2,1)}, bf16[4,128,128]{2,1,0:T(8,128)(2,1)}, bf16[4,128,128]{2,1,0:T(8,128)(2,1)}) custom-call(s32[192]{0:T(256)} %reshape_reshape.3.idx_ref, s32[1]{0:T(128)} %bitcast.h_ref, bf16[8,2,128,128]{3,2,1,0:T(8,128)(2,1)} %get-tuple-element.69.kv_ref, ...), custom_call_target="tpu_custom_call" | custom-call | flops 20132659200 | bytes 6291456 | tf_op jit(solution)/shard_map/attend/pallas_call | solution.py:243
  55.8 1.5 %collective-permute-start.13 = (bf16[4,128,128]{2,1,0:T(8,128)(2,1)}, bf16[4,128,128]{2,1,0:T(8,128)(2,1)S(1)}, u32[]{:S(2)}, u32[]{:S(2)}) collective-permute-start(bf16[4,128,128]{2,1,0:T(8,128)(2,1)} %get-tuple-element.75), channel_id=1, source_target_pairs={{0,8},{8,0},{16,24},{24,16},{1,9},{9,1},{17,25},{25,17},{2,10},{10... | collective-permute-start | bytes 393224 | tf_op jit(solution)/shard_map/ppermute | solution.py:364
  57.3 1.5 %collective-permute-start.14 = (bf16[4,128,128]{2,1,0:T(8,128)(2,1)}, bf16[4,128,128]{2,1,0:T(8,128)(2,1)S(1)}, u32[]{:S(2)}, u32[]{:S(2)}) collective-permute-start(bf16[4,128,128]{2,1,0:T(8,128)(2,1)} %get-tuple-element.76), channel_id=1, source_target_pairs={{0,16},{8,24},{16,0},{24,8},{1,17},{9,25},{17,1},{25,9},{2,18},{10... | collective-permute-start | bytes 393224 | tf_op jit(solution)/shard_map/ppermute | solution.py:364
  59.3 6.5 %all-to-all-done.1 = bf16[8,512,128]{2,1,0:T(8,128)(2,1)S(1)} async-done(((bf16[8,512,128]{2,1,0:T(8,128)(2,1)}), bf16[8,512,128]{2,1,0:T(8,128)(2,1)S(1)}, u32[]{:S(2)}, u32[]{:S(2)}) %all-to-all-start.1) | async-done | bytes 1048608 | tf_op jit(solution)/shard_map/all_to_all | solution.py:399
  65.8 1.0 copy-done
  66.8 2.0 %lend.2 = (bf16[4,128,128]{2,1,0:T(8,128)(2,1)}, bf16[4,128,128]{2,1,0:T(8,128)(2,1)}, bf16[4,128,128]{2,1,0:T(8,128)(2,1)}) custom-call(s32[16]{0:T(128)} %fusion.19.lists_ref, s32[1]{0:T(128)} %bitcast.h_ref, bf16[8,4,128,128]{3,2,1,0:T(8,128)(2,1)} %bitcast.13), custom_call_target="tpu_custom_call" | custom-call | bytes 2097152 | tf_op jit(solution)/shard_map/lend/pallas_call | solution.py:127
  68.9 1.5 %collective-permute-start.2 = (bf16[4,128,128]{2,1,0:T(8,128)(2,1)}, bf16[4,128,128]{2,1,0:T(8,128)(2,1)S(1)}, u32[]{:S(2)}, u32[]{:S(2)}) collective-permute-start(bf16[4,128,128]{2,1,0:T(8,128)(2,1)} %get-tuple-element.58), channel_id=1, source_target_pairs={{0,8},{8,0},{16,24},{24,16},{1,9},{9,1},{17,25},{25,17},{2,10},{10... | collective-permute-start | bytes 393224 | tf_op jit(solution)/shard_map/ppermute | solution.py:364
  70.4 1.5 %collective-permute-start.3 = (bf16[4,128,128]{2,1,0:T(8,128)(2,1)}, bf16[4,128,128]{2,1,0:T(8,128)(2,1)S(1)}, u32[]{:S(2)}, u32[]{:S(2)}) collective-permute-start(bf16[4,128,128]{2,1,0:T(8,128)(2,1)} %get-tuple-element.59), channel_id=1, source_target_pairs={{0,16},{8,24},{16,0},{24,8},{1,17},{9,25},{17,1},{25,9},{2,18},{10... | collective-permute-start | bytes 393224 | tf_op jit(solution)/shard_map/ppermute | solution.py:364
  73.1 2.5 %collect.2 = bf16[8,384,128]{2,1,0:T(8,128)(2,1)} custom-call(s32[16]{0:T(128)} %fusion.19.lists_ref, s32[1]{0:T(128)} %bitcast.h_ref, f32[16,128,128]{2,1,0:T(8,128)} %get-tuple-element.74.own, bf16[4,128,128]{2,1,0:T(8,128)(2,1)} %copy-done.4, bf16[4,128,128]{2,1,0:T(8,128)(2,1)} %copy-done.5, bf16[4,128,128]{2,1,0:T(8,128)(2,1)} %copy-done.7, ...), custom_call_target="tpu_custom_call" | custom-call | bytes 4194304 | tf_op jit(solution)/shard_map/collect/pallas_call | solution.py:292
  75.6 3.5 %all-to-all-start.2 = ((bf16[8,384,128]{2,1,0:T(8,128)(2,1)}), bf16[8,384,128]{2,1,0:T(8,128)(2,1)S(1)}, u32[]{:S(2)}, u32[]{:S(2)}) async-start(bf16[8,384,128]{2,1,0:T(8,128)(2,1)} %collect.2), calls=%async_computation.2 | async-start | bytes 1572864 | tf_op jit(solution)/shard_map/all_to_all | solution.py:399
  79.2 0.6 copy-done.26
  79.9 0.6 copy-done.29
  80.5 15.7 %attend.3 = (bf16[8,128,128]{2,1,0:T(8,128)(2,1)}, f32[16,128,128]{2,1,0:T(8,128)}, bf16[4,128,128]{2,1,0:T(8,128)(2,1)}, bf16[4,128,128]{2,1,0:T(8,128)(2,1)}, bf16[4,128,128]{2,1,0:T(8,128)(2,1)}) custom-call(s32[192]{0:T(256)} %reshape_reshape.3.idx_ref, s32[1]{0:T(128)} %bitcast.h_ref, bf16[8,4,128,128]{3,2,1,0:T(8,128)(2,1)} %bitcast.14, ...), custom_call_target="tpu_custom_call" | custom-call | flops 20132659200 | bytes 6291456 | tf_op jit(solution)/shard_map/attend/pallas_call | solution.py:243
  96.2 1.5 %collective-permute-start.16 = (bf16[4,128,128]{2,1,0:T(8,128)(2,1)}, bf16[4,128,128]{2,1,0:T(8,128)(2,1)S(1)}, u32[]{:S(2)}, u32[]{:S(2)}) collective-permute-start(bf16[4,128,128]{2,1,0:T(8,128)(2,1)} %get-tuple-element.83), channel_id=1, source_target_pairs={{0,8},{8,0},{16,24},{24,16},{1,9},{9,1},{17,25},{25,17},{2,10},{10... | collective-permute-start | bytes 393224 | tf_op jit(solution)/shard_map/ppermute | solution.py:364
  97.7 1.5 %collective-permute-start.17 = (bf16[4,128,128]{2,1,0:T(8,128)(2,1)}, bf16[4,128,128]{2,1,0:T(8,128)(2,1)S(1)}, u32[]{:S(2)}, u32[]{:S(2)}) collective-permute-start(bf16[4,128,128]{2,1,0:T(8,128)(2,1)} %get-tuple-element.84), channel_id=1, source_target_pairs={{0,16},{8,24},{16,0},{24,8},{1,17},{9,25},{17,1},{25,9},{2,18},{10... | collective-permute-start | bytes 393224 | tf_op jit(solution)/shard_map/ppermute | solution.py:364
  100.1 2.5 %collective-permute-done.16.refs_0_ = bf16[4,128,128]{2,1,0:T(8,128)(2,1)S(1)} collective-permute-done((bf16[4,128,128]{2,1,0:T(8,128)(2,1)}, bf16[4,128,128]{2,1,0:T(8,128)(2,1)S(1)}, u32[]{:S(2)}, u32[]{:S(2)}) %collective-permute-start.16) | collective-permute-done | bytes 131104 | tf_op jit(solution)/shard_map/ppermute | solution.py:364
  102.6 3.7 %collective-permute-done.17.refs_1_ = bf16[4,128,128]{2,1,0:T(8,128)(2,1)S(1)} collective-permute-done((bf16[4,128,128]{2,1,0:T(8,128)(2,1)}, bf16[4,128,128]{2,1,0:T(8,128)(2,1)S(1)}, u32[]{:S(2)}, u32[]{:S(2)}) %collective-permute-start.17) | collective-permute-done | bytes 131104 | tf_op jit(solution)/shard_map/ppermute | solution.py:364
  106.3 4.8 %all-to-all-start.3 = ((bf16[8,128,128]{2,1,0:T(8,128)(2,1)}), bf16[8,128,128]{2,1,0:T(8,128)(2,1)S(1)}, u32[]{:S(2)}, u32[]{:S(2)}) async-start(bf16[8,128,128]{2,1,0:T(8,128)(2,1)} %get-tuple-element.87), calls=%async_computation.3 | async-start | bytes 524288 | tf_op jit(solution)/shard_map/all_to_all | solution.py:399
  111.1 2.3 %collect.3 = (bf16[256,128]{1,0:T(8,128)(2,1)}, bf16[256,128]{1,0:T(8,128)(2,1)}, bf16[256,128]{1,0:T(8,128)(2,1)}, bf16[256,128]{1,0:T(8,128)(2,1)}, bf16[256,1...) custom-call(s32[16]{0:T(128)} %fusion.19.lists_ref, ...), custom_call_target="tpu_custom_call" | custom-call | bytes 4194304 | tf_op jit(solution)/shard_map/collect/pallas_call | solution.py:292
  113.4 0.6 collective-permute-start.19
  113.9 1.7 %collective-permute-start.20 = (bf16[256,128]{1,0:T(8,128)(2,1)}, bf16[256,128]{1,0:T(8,128)(2,1)S(1)}, u32[]{:S(2)}, u32[]{:S(2)}) collective-permute-start(bf16[256,128]{1,0:T(8,128)(2,1)} %get-tuple-element.95), channel_id=1, source_target_pairs={{0,2},{1,3},{2,0},{3,1},{4,6},{5,7},{6,4},{7,5},{8,10},{9,11},{10,... | collective-permute-start | bytes 196616 | tf_op jit(solution)/shard_map/ppermute | solution.py:364
  115.6 2.6 %collective-permute-start.22 = (bf16[256,128]{1,0:T(8,128)(2,1)}, bf16[256,128]{1,0:T(8,128)(2,1)S(1)}, u32[]{:S(2)}, u32[]{:S(2)}) collective-permute-start(bf16[256,128]{1,0:T(8,128)(2,1)} %get-tuple-element.97), channel_id=1, source_target_pairs={{0,4},{1,5},{2,6},{3,7},{4,0},{5,1},{6,2},{7,3},{8,12},{9,13},{10,... | collective-permute-start | bytes 196616 | tf_op jit(solution)/shard_map/ppermute | solution.py:364
  118.3 3.5 %collective-permute-start.24 = (bf16[256,128]{1,0:T(8,128)(2,1)}, bf16[256,128]{1,0:T(8,128)(2,1)S(1)}, u32[]{:S(2)}, u32[]{:S(2)}) collective-permute-start(bf16[256,128]{1,0:T(8,128)(2,1)} %get-tuple-element.99), channel_id=1, source_target_pairs={{0,6},{1,7},{2,4},{3,5},{4,2},{5,3},{6,0},{7,1},{8,14},{9,15},{10,... | collective-permute-start | bytes 196616 | tf_op jit(solution)/shard_map/ppermute | solution.py:364
  121.8 1.3 %collective-permute-done.20.refs_2_ = bf16[256,128]{1,0:T(8,128)(2,1)S(1)} collective-permute-done((bf16[256,128]{1,0:T(8,128)(2,1)}, bf16[256,128]{1,0:T(8,128)(2,1)S(1)}, u32[]{:S(2)}, u32[]{:S(2)}) %collective-permute-start.20) | collective-permute-done | bytes 65568 | tf_op jit(solution)/shard_map/ppermute | solution.py:364
  123.1 0.7 copy-done.2
  123.8 2.6 %unpack_early.1 = (bf16[256,1024]{1,0:T(8,128)(2,1)}, bf16[256,1024]{1,0:T(8,128)(2,1)}, bf16[256,1024]{1,0:T(8,128)(2,1)}) custom-call(bf16[8,384,128]{2,1,0:T(8,128)(2,1)} %copy-done.1, bf16[8,128,128]{2,1,0:T(8,128)(2,1)} %copy-done.2), custom_call_target="tpu_custom_call" | custom-call | bytes 8388608 | tf_op jit(solution)/shard_map/unpack_early/pallas_call | solution.py:339
  126.5 2.5 %collective-permute-done.23.refs_5_ = bf16[256,128]{1,0:T(8,128)(2,1)S(1)} collective-permute-done((bf16[256,128]{1,0:T(8,128)(2,1)}, bf16[256,128]{1,0:T(8,128)(2,1)S(1)}, u32[]{:S(2)}, u32[]{:S(2)}) %collective-permute-start.23) | collective-permute-done | bytes 65568 | tf_op jit(solution)/shard_map/ppermute | solution.py:364
  129.0 0.6 copy-done.14
  129.6 2.0 %unpack_last.1 = (bf16[256,1024]{1,0:T(8,128)(2,1)}, bf16[256,1024]{1,0:T(8,128)(2,1)}) custom-call(s32[1]{0:T(128)} %bitcast.h_ref, bf16[256,128]{1,0:T(8,128)(2,1)} %get-tuple-element.93.refs_0_, bf16[256,128]{1,0:T(8,128)(2,1)} %copy-done.10, bf16[256,128]{1,0:T(8,128)(2,1)} %copy-done.11, ...), custom_call_target="tpu_custom_call", output_to_operand_aliasing={{0}: (9, {}), {1}: (10, {})} | custom-call | bytes 2097152 | tf_op jit(solution)/shard_map/unpack_last/pallas_call | solution.py:349
  (107 shorter events, 5.6 us)
Async XLA Ops:
  2.8 9.5 %collective-permute-start = (bf16[256,128]{1,0:T(8,128)(2,1)}, bf16[256,128]{1,0:T(8,128)(2,1)S(1)}, u32[]{:S(2)}, u32[]{:S(2)}) collective-permute-start(bf16[256,128]{1,0:T(8,128)(2,1)} %get-tuple-element.54), channel_id=1, source_target_pairs={{0,1},{1,0},{2,3},{3,2},{4,5},{5,4},{6,7},{7,6},{8,9},{9,8},{10,11... | collective-permute-start | bytes 196616 | tf_op jit(solution)/shard_map/ppermute | solution.py:364
  3.2 12.4 %collective-permute-start.1 = (bf16[256,128]{1,0:T(8,128)(2,1)}, bf16[256,128]{1,0:T(8,128)(2,1)S(1)}, u32[]{:S(2)}, u32[]{:S(2)}) collective-permute-start(bf16[256,128]{1,0:T(8,128)(2,1)} %get-tuple-element.55), channel_id=1, source_target_pairs={{0,2},{1,3},{2,0},{3,1},{4,6},{5,7},{6,4},{7,5},{8,10},{9,11},{10,... | collective-permute-start | bytes 196616 | tf_op jit(solution)/shard_map/ppermute | solution.py:364
  5.8 18.4 %collective-permute-start.8 = (bf16[256,128]{1,0:T(8,128)(2,1)}, bf16[256,128]{1,0:T(8,128)(2,1)S(1)}, u32[]{:S(2)}, u32[]{:S(2)}) collective-permute-start(bf16[256,128]{1,0:T(8,128)(2,1)} %get-tuple-element.67), channel_id=1, source_target_pairs={{0,6},{1,7},{2,4},{3,5},{4,2},{5,3},{6,0},{7,1},{8,14},{9,15},{10,... | collective-permute-start | bytes 196616 | tf_op jit(solution)/shard_map/ppermute | solution.py:364
  8.3 0.9 copy-start.24
  8.3 15.9 %collective-permute-start.9 = (bf16[256,128]{1,0:T(8,128)(2,1)}, bf16[256,128]{1,0:T(8,128)(2,1)S(1)}, u32[]{:S(2)}, u32[]{:S(2)}) collective-permute-start(bf16[256,128]{1,0:T(8,128)(2,1)} %get-tuple-element.68), channel_id=1, source_target_pairs={{0,7},{1,6},{2,5},{3,4},{4,3},{5,2},{6,1},{7,0},{8,15},{9,14},{10,... | collective-permute-start | bytes 196616 | tf_op jit(solution)/shard_map/ppermute | solution.py:364
  9.2 15.1 %collective-permute-start.5 = (bf16[256,128]{1,0:T(8,128)(2,1)}, bf16[256,128]{1,0:T(8,128)(2,1)S(1)}, u32[]{:S(2)}, u32[]{:S(2)}) collective-permute-start(bf16[256,128]{1,0:T(8,128)(2,1)} %get-tuple-element.64), channel_id=1, source_target_pairs={{0,3},{1,2},{2,1},{3,0},{4,7},{5,6},{6,5},{7,4},{8,11},{9,10},{10,... | collective-permute-start | bytes 196616 | tf_op jit(solution)/shard_map/ppermute | solution.py:364
  9.2 3.0 %copy-start.33 = (bf16[256,128]{1,0:T(8,128)(2,1)S(1)}, bf16[256,128]{1,0:T(8,128)(2,1)}, u32[]{:S(2)}) copy-start(bf16[256,128]{1,0:T(8,128)(2,1)} %get-tuple-element.65) | copy-start | bytes 196612
  9.2 6.3 %copy-start.32 = (bf16[256,128]{1,0:T(8,128)(2,1)S(1)}, bf16[256,128]{1,0:T(8,128)(2,1)}, u32[]{:S(2)}) copy-start(bf16[256,128]{1,0:T(8,128)(2,1)} %get-tuple-element.66) | copy-start | bytes 196612
  12.2 3.4 %copy-start.17 = (bf16[256,128]{1,0:T(8,128)(2,1)}, bf16[256,128]{1,0:T(8,128)(2,1)S(1)}, u32[]{:S(2)}) copy-start(bf16[256,128]{1,0:T(8,128)(2,1)S(1)} %collective-permute-done) | copy-start | bytes 196612
  12.3 12.0 %collective-permute-start.6 = (bf16[256,128]{1,0:T(8,128)(2,1)S(1)}, bf16[256,128]{1,0:T(8,128)(2,1)S(1)}, u32[]{:S(2)}, u32[]{:S(2)}) collective-permute-start(bf16[256,128]{1,0:T(8,128)(2,1)S(1)} %copy-done.33), channel_id=1, source_target_pairs={{0,4},{1,5},{2,6},{3,7},{4,0},{5,1},{6,2},{7,3},{8,12},{9,13},{10,... | collective-permute-start | bytes 196616 | tf_op jit(solution)/shard_map/ppermute | solution.py:364
  15.6 8.7 %collective-permute-start.7 = (bf16[256,128]{1,0:T(8,128)(2,1)S(1)}, bf16[256,128]{1,0:T(8,128)(2,1)S(1)}, u32[]{:S(2)}, u32[]{:S(2)}) collective-permute-start(bf16[256,128]{1,0:T(8,128)(2,1)S(1)} %copy-done.32), channel_id=1, source_target_pairs={{0,5},{1,4},{2,7},{3,6},{4,1},{5,0},{6,3},{7,2},{8,13},{9,12},{10,... | collective-permute-start | bytes 196616 | tf_op jit(solution)/shard_map/ppermute | solution.py:364
  16.2 18.8 %all-to-all-start = ((bf16[8,256,128]{2,1,0:T(8,128)(2,1)}), bf16[8,256,128]{2,1,0:T(8,128)(2,1)S(1)}, u32[]{:S(2)}, u32[]{:S(2)}) async-start(bf16[8,256,128]{2,1,0:T(8,128)(2,1)} %pack_one.1), calls=%async_computation | async-start | bytes 1048576 | tf_op jit(solution)/shard_map/all_to_all | solution.py:399
  22.7 0.8 copy-start.25
  26.9 12.4 %collective-permute-start.10 = (bf16[4,128,128]{2,1,0:T(8,128)(2,1)}, bf16[4,128,128]{2,1,0:T(8,128)(2,1)S(1)}, u32[]{:S(2)}, u32[]{:S(2)}) collective-permute-start(bf16[4,128,128]{2,1,0:T(8,128)(2,1)} %get-tuple-element.71), channel_id=1, source_target_pairs={{0,8},{8,0},{16,24},{24,16},{1,9},{9,1},{17,25},{25,17},{2,10},{10... | collective-permute-start | bytes 393224 | tf_op jit(solution)/shard_map/ppermute | solution.py:364
  28.5 10.9 %collective-permute-start.11 = (bf16[4,128,128]{2,1,0:T(8,128)(2,1)}, bf16[4,128,128]{2,1,0:T(8,128)(2,1)S(1)}, u32[]{:S(2)}, u32[]{:S(2)}) collective-permute-start(bf16[4,128,128]{2,1,0:T(8,128)(2,1)} %get-tuple-element.72), channel_id=1, source_target_pairs={{0,16},{8,24},{16,0},{24,8},{1,17},{9,25},{17,1},{25,9},{2,18},{10... | collective-permute-start | bytes 393224 | tf_op jit(solution)/shard_map/ppermute | solution.py:364
  30.0 9.4 %collective-permute-start.12 = (bf16[4,128,128]{2,1,0:T(8,128)(2,1)}, bf16[4,128,128]{2,1,0:T(8,128)(2,1)S(1)}, u32[]{:S(2)}, u32[]{:S(2)}) collective-permute-start(bf16[4,128,128]{2,1,0:T(8,128)(2,1)} %get-tuple-element.73), channel_id=1, source_target_pairs={{0,24},{8,16},{16,8},{24,0},{1,25},{9,17},{17,9},{25,1},{2,26},{10... | collective-permute-start | bytes 393224 | tf_op jit(solution)/shard_map/ppermute | solution.py:364
  35.0 0.8 copy-start.3
  35.8 30.1 %all-to-all-start.1 = ((bf16[8,512,128]{2,1,0:T(8,128)(2,1)}), bf16[8,512,128]{2,1,0:T(8,128)(2,1)S(1)}, u32[]{:S(2)}, u32[]{:S(2)}) async-start(bf16[8,512,128]{2,1,0:T(8,128)(2,1)} %pack.1), calls=%async_computation.1 | async-start | bytes 2097152 | tf_op jit(solution)/shard_map/all_to_all | solution.py:399
  39.3 0.7 copy-start.30
  39.4 0.7 copy-start.31
  55.8 16.1 %collective-permute-start.13 = (bf16[4,128,128]{2,1,0:T(8,128)(2,1)}, bf16[4,128,128]{2,1,0:T(8,128)(2,1)S(1)}, u32[]{:S(2)}, u32[]{:S(2)}) collective-permute-start(bf16[4,128,128]{2,1,0:T(8,128)(2,1)} %get-tuple-element.75), channel_id=1, source_target_pairs={{0,8},{8,0},{16,24},{24,16},{1,9},{9,1},{17,25},{25,17},{2,10},{10... | collective-permute-start | bytes 393224 | tf_op jit(solution)/shard_map/ppermute | solution.py:364
  57.3 15.1 %collective-permute-start.14 = (bf16[4,128,128]{2,1,0:T(8,128)(2,1)}, bf16[4,128,128]{2,1,0:T(8,128)(2,1)S(1)}, u32[]{:S(2)}, u32[]{:S(2)}) collective-permute-start(bf16[4,128,128]{2,1,0:T(8,128)(2,1)} %get-tuple-element.76), channel_id=1, source_target_pairs={{0,16},{8,24},{16,0},{24,8},{1,17},{9,25},{17,1},{25,9},{2,18},{10... | collective-permute-start | bytes 393224 | tf_op jit(solution)/shard_map/ppermute | solution.py:364
  58.9 13.5 %collective-permute-start.15 = (bf16[4,128,128]{2,1,0:T(8,128)(2,1)}, bf16[4,128,128]{2,1,0:T(8,128)(2,1)S(1)}, u32[]{:S(2)}, u32[]{:S(2)}) collective-permute-start(bf16[4,128,128]{2,1,0:T(8,128)(2,1)} %get-tuple-element.77), channel_id=1, source_target_pairs={{0,24},{8,16},{16,8},{24,0},{1,25},{9,17},{17,9},{25,1},{2,26},{10... | collective-permute-start | bytes 393224 | tf_op jit(solution)/shard_map/ppermute | solution.py:364
  65.8 1.0 copy-start
  68.9 10.3 %collective-permute-start.2 = (bf16[4,128,128]{2,1,0:T(8,128)(2,1)}, bf16[4,128,128]{2,1,0:T(8,128)(2,1)S(1)}, u32[]{:S(2)}, u32[]{:S(2)}) collective-permute-start(bf16[4,128,128]{2,1,0:T(8,128)(2,1)} %get-tuple-element.58), channel_id=1, source_target_pairs={{0,8},{8,0},{16,24},{24,16},{1,9},{9,1},{17,25},{25,17},{2,10},{10... | collective-permute-start | bytes 393224 | tf_op jit(solution)/shard_map/ppermute | solution.py:364
  70.4 8.8 %collective-permute-start.3 = (bf16[4,128,128]{2,1,0:T(8,128)(2,1)}, bf16[4,128,128]{2,1,0:T(8,128)(2,1)S(1)}, u32[]{:S(2)}, u32[]{:S(2)}) collective-permute-start(bf16[4,128,128]{2,1,0:T(8,128)(2,1)} %get-tuple-element.59), channel_id=1, source_target_pairs={{0,16},{8,24},{16,0},{24,8},{1,17},{9,25},{17,1},{25,9},{2,18},{10... | collective-permute-start | bytes 393224 | tf_op jit(solution)/shard_map/ppermute | solution.py:364
  71.9 7.3 %collective-permute-start.4 = (bf16[4,128,128]{2,1,0:T(8,128)(2,1)}, bf16[4,128,128]{2,1,0:T(8,128)(2,1)S(1)}, u32[]{:S(2)}, u32[]{:S(2)}) collective-permute-start(bf16[4,128,128]{2,1,0:T(8,128)(2,1)} %get-tuple-element.60), channel_id=1, source_target_pairs={{0,24},{8,16},{16,8},{24,0},{1,25},{9,17},{17,9},{25,1},{2,26},{10... | collective-permute-start | bytes 393224 | tf_op jit(solution)/shard_map/ppermute | solution.py:364
  75.6 24.4 %all-to-all-start.2 = ((bf16[8,384,128]{2,1,0:T(8,128)(2,1)}), bf16[8,384,128]{2,1,0:T(8,128)(2,1)S(1)}, u32[]{:S(2)}, u32[]{:S(2)}) async-start(bf16[8,384,128]{2,1,0:T(8,128)(2,1)} %collect.2), calls=%async_computation.2 | async-start | bytes 1572864 | tf_op jit(solution)/shard_map/all_to_all | solution.py:399
  96.2 6.3 %collective-permute-start.16 = (bf16[4,128,128]{2,1,0:T(8,128)(2,1)}, bf16[4,128,128]{2,1,0:T(8,128)(2,1)S(1)}, u32[]{:S(2)}, u32[]{:S(2)}) collective-permute-start(bf16[4,128,128]{2,1,0:T(8,128)(2,1)} %get-tuple-element.83), channel_id=1, source_target_pairs={{0,8},{8,0},{16,24},{24,16},{1,9},{9,1},{17,25},{25,17},{2,10},{10... | collective-permute-start | bytes 393224 | tf_op jit(solution)/shard_map/ppermute | solution.py:364
  97.7 8.6 %collective-permute-start.17 = (bf16[4,128,128]{2,1,0:T(8,128)(2,1)}, bf16[4,128,128]{2,1,0:T(8,128)(2,1)S(1)}, u32[]{:S(2)}, u32[]{:S(2)}) collective-permute-start(bf16[4,128,128]{2,1,0:T(8,128)(2,1)} %get-tuple-element.84), channel_id=1, source_target_pairs={{0,16},{8,24},{16,0},{24,8},{1,17},{9,25},{17,1},{25,9},{2,18},{10... | collective-permute-start | bytes 393224 | tf_op jit(solution)/shard_map/ppermute | solution.py:364
  99.2 7.1 %collective-permute-start.18 = (bf16[4,128,128]{2,1,0:T(8,128)(2,1)}, bf16[4,128,128]{2,1,0:T(8,128)(2,1)S(1)}, u32[]{:S(2)}, u32[]{:S(2)}) collective-permute-start(bf16[4,128,128]{2,1,0:T(8,128)(2,1)} %get-tuple-element.85), channel_id=1, source_target_pairs={{0,24},{8,16},{16,8},{24,0},{1,25},{9,17},{17,9},{25,1},{2,26},{10... | collective-permute-start | bytes 393224 | tf_op jit(solution)/shard_map/ppermute | solution.py:364
  100.1 13.3 %copy-start.1 = (bf16[8,384,128]{2,1,0:T(8,128)(2,1)}, bf16[8,384,128]{2,1,0:T(8,128)(2,1)S(1)}, u32[]{:S(2)}) copy-start(bf16[8,384,128]{2,1,0:T(8,128)(2,1)S(1)} %all-to-all-done.2.refs_0_) | copy-start | bytes 2359300
  102.6 8.5 %copy-start.6 = (bf16[4,128,128]{2,1,0:T(8,128)(2,1)}, bf16[4,128,128]{2,1,0:T(8,128)(2,1)S(1)}, u32[]{:S(2)}) copy-start(bf16[4,128,128]{2,1,0:T(8,128)(2,1)S(1)} %collective-permute-done.16.refs_0_) | copy-start | bytes 393220
  106.3 4.8 %copy-start.8 = (bf16[4,128,128]{2,1,0:T(8,128)(2,1)}, bf16[4,128,128]{2,1,0:T(8,128)(2,1)S(1)}, u32[]{:S(2)}) copy-start(bf16[4,128,128]{2,1,0:T(8,128)(2,1)S(1)} %collective-permute-done.17.refs_1_) | copy-start | bytes 393220
  106.3 4.8 %copy-start.9 = (bf16[4,128,128]{2,1,0:T(8,128)(2,1)}, bf16[4,128,128]{2,1,0:T(8,128)(2,1)S(1)}, u32[]{:S(2)}) copy-start(bf16[4,128,128]{2,1,0:T(8,128)(2,1)S(1)} %collective-permute-done.18.refs_2_) | copy-start | bytes 393220
  106.3 16.9 %all-to-all-start.3 = ((bf16[8,128,128]{2,1,0:T(8,128)(2,1)}), bf16[8,128,128]{2,1,0:T(8,128)(2,1)S(1)}, u32[]{:S(2)}, u32[]{:S(2)}) async-start(bf16[8,128,128]{2,1,0:T(8,128)(2,1)} %get-tuple-element.87), calls=%async_computation.3 | async-start | bytes 524288 | tf_op jit(solution)/shard_map/all_to_all | solution.py:399
  113.4 4.9 %collective-permute-start.19 = (bf16[256,128]{1,0:T(8,128)(2,1)}, bf16[256,128]{1,0:T(8,128)(2,1)S(1)}, u32[]{:S(2)}, u32[]{:S(2)}) collective-permute-start(bf16[256,128]{1,0:T(8,128)(2,1)} %get-tuple-element.94), channel_id=1, source_target_pairs={{0,1},{1,0},{2,3},{3,2},{4,5},{5,4},{6,7},{7,6},{8,9},{9,8},{10,11... | collective-permute-start | bytes 196616 | tf_op jit(solution)/shard_map/ppermute | solution.py:364
  113.9 9.2 %collective-permute-start.20 = (bf16[256,128]{1,0:T(8,128)(2,1)}, bf16[256,128]{1,0:T(8,128)(2,1)S(1)}, u32[]{:S(2)}, u32[]{:S(2)}) collective-permute-start(bf16[256,128]{1,0:T(8,128)(2,1)} %get-tuple-element.95), channel_id=1, source_target_pairs={{0,2},{1,3},{2,0},{3,1},{4,6},{5,7},{6,4},{7,5},{8,10},{9,11},{10,... | collective-permute-start | bytes 196616 | tf_op jit(solution)/shard_map/ppermute | solution.py:364
  115.6 10.9 %collective-permute-start.21 = (bf16[256,128]{1,0:T(8,128)(2,1)}, bf16[256,128]{1,0:T(8,128)(2,1)S(1)}, u32[]{:S(2)}, u32[]{:S(2)}) collective-permute-start(bf16[256,128]{1,0:T(8,128)(2,1)} %get-tuple-element.96), channel_id=1, source_target_pairs={{0,3},{1,2},{2,1},{3,0},{4,7},{5,6},{6,5},{7,4},{8,11},{9,10},{10,... | collective-permute-start | bytes 196616 | tf_op jit(solution)/shard_map/ppermute | solution.py:364
  115.6 10.9 %collective-permute-start.22 = (bf16[256,128]{1,0:T(8,128)(2,1)}, bf16[256,128]{1,0:T(8,128)(2,1)S(1)}, u32[]{:S(2)}, u32[]{:S(2)}) collective-permute-start(bf16[256,128]{1,0:T(8,128)(2,1)} %get-tuple-element.97), channel_id=1, source_target_pairs={{0,4},{1,5},{2,6},{3,7},{4,0},{5,1},{6,2},{7,3},{8,12},{9,13},{10,... | collective-permute-start | bytes 196616 | tf_op jit(solution)/shard_map/ppermute | solution.py:364
  118.2 10.8 %collective-permute-start.23 = (bf16[256,128]{1,0:T(8,128)(2,1)}, bf16[256,128]{1,0:T(8,128)(2,1)S(1)}, u32[]{:S(2)}, u32[]{:S(2)}) collective-permute-start(bf16[256,128]{1,0:T(8,128)(2,1)} %get-tuple-element.98), channel_id=1, source_target_pairs={{0,5},{1,4},{2,7},{3,6},{4,1},{5,0},{6,3},{7,2},{8,13},{9,12},{10,... | collective-permute-start | bytes 196616 | tf_op jit(solution)/shard_map/ppermute | solution.py:364
  118.3 8.1 %copy-start.10 = (bf16[256,128]{1,0:T(8,128)(2,1)}, bf16[256,128]{1,0:T(8,128)(2,1)S(1)}, u32[]{:S(2)}) copy-start(bf16[256,128]{1,0:T(8,128)(2,1)S(1)} %collective-permute-done.19.refs_1_) | copy-start | bytes 196612
  118.3 10.7 %collective-permute-start.24 = (bf16[256,128]{1,0:T(8,128)(2,1)}, bf16[256,128]{1,0:T(8,128)(2,1)S(1)}, u32[]{:S(2)}, u32[]{:S(2)}) collective-permute-start(bf16[256,128]{1,0:T(8,128)(2,1)} %get-tuple-element.99), channel_id=1, source_target_pairs={{0,6},{1,7},{2,4},{3,5},{4,2},{5,3},{6,0},{7,1},{8,14},{9,15},{10,... | collective-permute-start | bytes 196616 | tf_op jit(solution)/shard_map/ppermute | solution.py:364
  123.1 3.3 %copy-start.11 = (bf16[256,128]{1,0:T(8,128)(2,1)}, bf16[256,128]{1,0:T(8,128)(2,1)S(1)}, u32[]{:S(2)}) copy-start(bf16[256,128]{1,0:T(8,128)(2,1)S(1)} %collective-permute-done.20.refs_2_) | copy-start | bytes 196612
  123.1 5.9 %collective-permute-start.25 = (bf16[256,128]{1,0:T(8,128)(2,1)}, bf16[256,128]{1,0:T(8,128)(2,1)S(1)}, u32[]{:S(2)}, u32[]{:S(2)}) collective-permute-start(bf16[256,128]{1,0:T(8,128)(2,1)} %get-tuple-element.100), channel_id=1, source_target_pairs={{0,7},{1,6},{2,5},{3,4},{4,3},{5,2},{6,1},{7,0},{8,15},{9,14},{10,... | collective-permute-start | bytes 196616 | tf_op jit(solution)/shard_map/ppermute | solution.py:364
  123.1 0.7 copy-start.2
  126.5 2.5 %copy-start.12 = (bf16[256,128]{1,0:T(8,128)(2,1)}, bf16[256,128]{1,0:T(8,128)(2,1)S(1)}, u32[]{:S(2)}) copy-start(bf16[256,128]{1,0:T(8,128)(2,1)S(1)} %collective-permute-done.21.refs_3_) | copy-start | bytes 196612
  126.5 2.5 %copy-start.13 = (bf16[256,128]{1,0:T(8,128)(2,1)}, bf16[256,128]{1,0:T(8,128)(2,1)S(1)}, u32[]{:S(2)}) copy-start(bf16[256,128]{1,0:T(8,128)(2,1)S(1)} %collective-permute-done.22.refs_4_) | copy-start | bytes 196612
  (16 other events, 10.3 us)
